TPU v7x, 32 devices: a whole 2x2x4 slice. The times are simulated.
32 devices in a mesh: grp: 2 (over x), seq: 16 (over z, y, core).
Axes of the slice: x: 2, y: 2, z: 4, core: 2. Of those that a mesh axis runs over, the one named last changes fastest.
Arguments:
- fresh_query: bfloat16 [4096, 4096], P(('grp', 'seq')), parts along dimension 0, may hold values from -80 to 80
- fresh_key: bfloat16 [4096, 4096], P(('grp', 'seq')), parts along dimension 0, may hold values from -4 to 4
- fresh_value: bfloat16 [4096, 4096], P(('grp', 'seq')), parts along dimension 0, may hold values from -4 to 4
- stale_key: bfloat16 [8192, 4096], P('grp', 'seq'), parts along dimension 0, may hold values from -4 to 4
- stale_value: bfloat16 [8192, 4096], P('grp', 'seq'), parts along dimension 0, may hold values from -4 to 4
- patch_start: int32 [2], P('grp'), parts along dimension 0, may hold values from 0 to 2048
- timestep: int32 [2], P('grp'), parts along dimension 0, may hold values from 0 to 34
- gate_table: float32 [35, 4096], replicated, may hold values from -4 to 4
Outputs:
- gated: bfloat16 [4096, 4096], P(('grp', 'seq')), parts along dimension 0
There are 2 independent parts, one for each index of `grp`. A program takes and returns all parts, laid end to end along the dimension named above; an argument that names none is the same for every part. Nothing has to cross between parts.
All inputs are finite; a program needn't handle non-finite values.
Results may differ from a plain program's by a relative error of at most 0.0056.
Values may be sent and summed in bfloat16 or wider, within the bound.
No kernel may reach another device: no remote copies, remote signals or barrier semaphores. Data moves between devices by JAX's collectives and lax.ppermute only.
A program may use at most 64 MiB of HBM per device.

v0:
```python
import jax
import jax.numpy as jnp
from jax import lax
from jax.sharding import PartitionSpec as P

HD = 128


def attend_group(queries, keys, values):
    scores = jnp.dot(queries, keys.T, preferred_element_type=jnp.float32) * HD ** (-0.5)
    row_max = jnp.max(scores, axis=1)
    expo = jnp.exp(scores - row_max[:, None])
    total = jnp.sum(expo, axis=1)
    output = jnp.dot(expo.astype(jnp.bfloat16), values, preferred_element_type=jnp.float32)
    return (row_max, total, output)


def attend_blocks(queries, keys, values):
    all_rows = queries.shape[0]
    block_rows = min(512, all_rows)
    blocks = queries.reshape(all_rows // block_rows, block_rows, queries.shape[1])
    row_max, total, output = lax.map(lambda q_block: attend_group(q_block, keys, values), blocks)
    return (
        row_max.reshape(all_rows),
        total.reshape(all_rows),
        output.reshape(all_rows, values.shape[1]),
    )


def old_partials(queries_all, old_key, old_value, heads_dev):
    results = []
    for head_idx in range(heads_dev):
        cols = slice(head_idx * HD, (head_idx + 1) * HD)
        results.append(
            attend_blocks(queries_all[:, head_idx, :], old_key[:, cols], old_value[:, cols])
        )
    return results


def shards(
    fresh_query, fresh_key, fresh_value, stale_key, stale_value, patch_start, timestep, gate_table
):
    tok_rows = fresh_query.shape[0]
    model_width = fresh_query.shape[1]
    heads_dev = stale_key.shape[1] // HD
    patch_rows = tok_rows * lax.axis_size("seq")
    seq_rows = stale_key.shape[0]
    query_heads = fresh_query.reshape(tok_rows, model_width // HD, HD)
    key_heads = fresh_key.reshape(tok_rows, model_width // HD, HD)
    value_heads = fresh_value.reshape(tok_rows, model_width // HD, HD)
    shift_by = -(patch_start[0] + patch_rows)
    old_key = jnp.roll(stale_key, shift_by, axis=0)[: seq_rows - patch_rows]
    old_value = jnp.roll(stale_value, shift_by, axis=0)[: seq_rows - patch_rows]
    queries_all, keys_all, values_all = (
        lax.all_to_all(query_heads, "seq", split_axis=1, concat_axis=0, tiled=True),
        lax.all_to_all(key_heads, "seq", split_axis=1, concat_axis=0, tiled=True),
        lax.all_to_all(value_heads, "seq", split_axis=1, concat_axis=0, tiled=True),
    )
    old_parts = old_partials(queries_all, old_key, old_value, heads_dev)
    outputs = []
    for head_idx in range(heads_dev):
        max_old, sum_old, out_old = old_parts[head_idx]
        max_new, sum_new, out_new = attend_blocks(
            queries_all[:, head_idx, :], keys_all[:, head_idx, :], values_all[:, head_idx, :]
        )
        top = jnp.maximum(max_old, max_new)
        scale_old = jnp.exp(max_old - top)
        scale_new = jnp.exp(max_new - top)
        numer = scale_old[:, None] * out_old + scale_new[:, None] * out_new
        denom = scale_old * sum_old + scale_new * sum_new
        outputs.append((numer / denom[:, None]).astype(jnp.bfloat16))
    heads_out = jnp.stack(outputs, axis=1)
    back_home = lax.all_to_all(heads_out, "seq", split_axis=0, concat_axis=1, tiled=True)
    attn = back_home.reshape(tok_rows, model_width)
    gate_row = lax.dynamic_slice_in_dim(gate_table, timestep[0], 1, 0)
    return (attn.astype(jnp.float32) * gate_row).astype(jnp.bfloat16)


def solution(mesh):
    return jax.shard_map(
        shards,
        mesh=mesh,
        in_specs=(
            P(("grp", "seq"), None),
            P(("grp", "seq"), None),
            P(("grp", "seq"), None),
            P("grp", "seq"),
            P("grp", "seq"),
            P("grp"),
            P("grp"),
            P(),
        ),
        out_specs=P(("grp", "seq"), None),
        check_vma=False,
    )
```

profile of v0, /device:TPU:11, one launch (start us, length us, event | category | flops | bytes accessed | tf_op | source)
XLA Modules:
  0.0 210.6 jit_solution(3825884178690398125)
XLA Ops:
  0.0 1.7 copy.40
  3.1 6.6 %all-to-all-start = ((bf16[128,32,128]{2,0,1:T(8,128)(2,1)}), bf16[128,32,128]{2,0,1:T(8,128)(2,1)S(1)}, u32[]{:S(2)}, u32[]{:S(2)}) async-start(bf16[128,32,128]{2,0,1:T(8,128)(2,1)} %copy.41), calls=%async_computation | async-start | bytes 2097152 | tf_op jit(solution)/shard_map/all_to_all | solution.py:55
  11.6 2.3 %copy.46 = bf16[128,4096]{0,1:T(8,128)(2,1)} copy(bf16[128,4096]{1,0:T(8,128)(2,1)} %param.20) | data formatting | bytes 2097152 | tf_op args[2]
  13.9 20.7 %all-to-all-done = bf16[128,32,128]{2,0,1:T(8,128)(2,1)S(1)} async-done(((bf16[128,32,128]{2,0,1:T(8,128)(2,1)}), bf16[128,32,128]{2,0,1:T(8,128)(2,1)S(1)}, u32[]{:S(2)}, u32[]{:S(2)}) %all-to-all-start) | async-done | bytes 1048608 | tf_op jit(solution)/shard_map/all_to_all | solution.py:55
  34.6 4.8 %all-to-all-start.1 = ((bf16[128,32,128]{0,2,1:T(8,128)(2,1)}), bf16[128,32,128]{0,2,1:T(8,128)(2,1)}, u32[]{:S(2)}, u32[]{:S(2)}) async-start(bf16[128,32,128]{0,2,1:T(8,128)(2,1)} %bitcast.22), calls=%async_computation.1 | async-start | bytes 2097152 | tf_op jit(solution)/shard_map/all_to_all | solution.py:56
  39.3 4.8 %fusion.68 = (bf16[4096,256]{1,0:T(8,128)(2,1)S(1)}, bf16[4096,256]{1,0:T(8,128)(2,1)S(1)}) fusion(s32[]{:T(128)S(6)} %select_n.17, bf16[4096,256]{1,0:T(8,128)(2,1)} %param.22, bf16[4096,256]{1,0:T(8,128)(2,1)} %param.21), kind=kLoop, calls=%fused_computation.60 | loop fusion | flops 8388608 | bytes 8388612 | tf_op jit(solution)/shard_map/jit(_roll_dynamic)/concatenate | solution.py:53
  46.4 18.0 %all-to-all-done.1 = bf16[128,32,128]{0,2,1:T(8,128)(2,1)} async-done(((bf16[128,32,128]{0,2,1:T(8,128)(2,1)}), bf16[128,32,128]{0,2,1:T(8,128)(2,1)}, u32[]{:S(2)}, u32[]{:S(2)}) %all-to-all-start.1) | async-done | bytes 1048608 | tf_op jit(solution)/shard_map/all_to_all | solution.py:56
  64.4 4.8 %all-to-all-start.2 = ((bf16[128,32,128]{0,2,1:T(8,128)(2,1)}), bf16[128,32,128]{0,2,1:T(8,128)(2,1)}, u32[]{:S(2)}, u32[]{:S(2)}) async-start(bf16[128,32,128]{0,2,1:T(8,128)(2,1)} %bitcast.163), calls=%async_computation.2 | async-start | bytes 2097152 | tf_op jit(solution)/shard_map/all_to_all | solution.py:57
  70.2 13.2 %while.56 = (s32[]{:T(128)}, f32[4,512]{1,0:T(4,128)S(1)}, f32[4,512]{1,0:T(4,128)S(1)}, f32[4,512,128]{2,1,0:T(8,128)}, bf16[4,512,128]{2,1,0:T(8,128)(2,1)S(1)...) while((s32[]{:T(128)}, f32[4,512]{1,0:T(4,128)S(1)}, ...), condition=%wide.region_3.5_spmd, body=%wide.region_0.4_spmd.sunk | while | flops 545258496 | bytes 14041705 | solution.py:22
  83.4 2.4 %copy.45 = bf16[16,128,2,128]{3,1,0,2:T(8,128)(2,1)} copy(bf16[16,128,2,128]{1,3,2,0:T(8,128)(2,1)} %bitcast.25) | data formatting | bytes 2097152 | tf_op jit(solution)/shard_map/all_to_all | solution.py:56
  85.8 8.3 %all-to-all-done.2 = bf16[128,32,128]{0,2,1:T(8,128)(2,1)} async-done(((bf16[128,32,128]{0,2,1:T(8,128)(2,1)}), bf16[128,32,128]{0,2,1:T(8,128)(2,1)}, u32[]{:S(2)}, u32[]{:S(2)}) %all-to-all-start.2) | async-done | bytes 1048608 | tf_op jit(solution)/shard_map/all_to_all | solution.py:57
  94.1 2.3 %copy.48 = bf16[16,128,2,128]{3,1,0,2:T(8,128)(2,1)} copy(bf16[16,128,2,128]{1,3,2,0:T(8,128)(2,1)} %bitcast.31) | data formatting | bytes 2097152 | tf_op jit(solution)/shard_map/all_to_all | solution.py:57
  96.4 2.5 %slice_bitcast_fusion.2 = (bf16[2048,128]{1,0:T(8,128)(2,1)S(1)}, bf16[2048,128]{1,0:T(8,128)(2,1)S(1)}, bf16[2048,128]{1,0:T(8,128)(2,1)S(1)}, bf16[2048,128]{1,0:T(8,128)(2,1)}) fusion(bf16[2048,2,128]{2,0,1:T(8,128)(2,1)} %bitcast.168, bf16[2048,2,128]{2,0,1:T(8,128)(2,1)} %bitcast.167), kind=kLoop, calls=%fused_computation.70 | loop fusion | bytes 4194304 | tf_op jit(solution)/shard_map/squeeze | solution.py:64
  99.9 17.5 %while.57 = (s32[]{:T(128)}, f32[4,512]{1,0:T(4,128)S(1)}, f32[4,512]{1,0:T(4,128)S(1)}, f32[4,512,128]{2,1,0:T(8,128)}, bf16[4,512,128]{2,1,0:T(8,128)(2,1)}, /...) while((s32[]{:T(128)}, f32[4,512]{1,0:T(4,128)S(1)}, ...), condition=%wide.region_7.9_spmd, body=%wide.region_4.8_spmd.sunk | while | flops 545258496 | bytes 14042213 | solution.py:22
  99.9 1.9 multiply_reduce_fusion.9
  104.3 1.9 multiply_reduce_fusion.9
  108.7 1.9 multiply_reduce_fusion.9
  113.1 1.9 multiply_reduce_fusion.9
  118.6 16.7 %while.58 = (s32[]{:T(128)}, f32[4,512]{1,0:T(4,128)S(1)}, f32[4,512]{1,0:T(4,128)S(1)}, f32[4,512,128]{2,1,0:T(8,128)}, bf16[4,512,128]{2,1,0:T(8,128)(2,1)}, /...) while((s32[]{:T(128)}, f32[4,512]{1,0:T(4,128)S(1)}, ...), condition=%wide.region_11.13_spmd, body=%wide.region_8.12_spmd.sunk | while | flops 545258496 | bytes 14042213 | solution.py:22
  122.7 1.7 multiply_reduce_fusion.10
  126.9 1.7 multiply_reduce_fusion.10
  131.1 1.7 multiply_reduce_fusion.10
  135.4 13.9 %while.59 = (s32[]{:T(128)}, f32[4,512]{1,0:T(4,128)S(1)}, f32[4,512]{1,0:T(4,128)S(1)}, f32[4,512,128]{2,1,0:T(8,128)S(1)}, bf16[4,512,128]{2,1,0:T(8,128)(2,1)...) while((s32[]{:T(128)}, f32[4,512]{1,0:T(4,128)S(1)}, ...), condition=%wide.region_15.17_spmd, body=%wide.region_12.16_spmd.sunk | while | flops 545258496 | bytes 14041705 | solution.py:22
  135.4 1.7 multiply_reduce_fusion.11
  145.9 1.7 multiply_reduce_fusion.11
  149.4 10.3 %divide_convert_fusion.1 = bf16[2048,1,128]{2,1,0:T(2,128)(2,1)S(1)} fusion(f32[2048,1,128]{2,1,0:T(1,128)} %bitcast.35, f32[2048,1,128]{2,1,0:T(1,128)} %bitcast.34, f32[2048]{0:T(1024)S(1)} %get-tuple-element.230, f32[2048]{0:T(1024)S(1)} %get-tuple-element.232, f32[2048]{0:T(1024)S(1)} %get-tuple-element.231), kind=kLoop, calls=%fused_computation.67 | loop fusion | flops 1310720 | bytes 2646016 | tf_op jit(solution)/shard_map/convert_element_type | solution.py:71
  159.7 10.2 %divide_convert_fusion = bf16[2048,1,128]{2,1,0:T(2,128)(2,1)S(1)} fusion(f32[2048,1,128]{2,1,0:T(1,128)S(1)} %bitcast.161, f32[2048,1,128]{2,1,0:T(1,128)} %bitcast.39, f32[2048]{0:T(1024)S(1)} %get-tuple-element.233, f32[2048]{0:T(1024)S(1)} %get-tuple-element.235, f32[2048]{0:T(1024)S(1)} %get-tuple-element.234), kind=kLoop, calls=%fused_computation.66 | loop fusion | flops 1310720 | bytes 2646016 | tf_op jit(solution)/shard_map/convert_element_type | solution.py:71
  170.0 3.4 %pad_maximum_fusion = bf16[2048,2,128]{2,1,0:T(2,128)(2,1)} fusion(bf16[2048,1,128]{2,1,0:T(2,128)(2,1)S(1)} %divide_convert_fusion, bf16[2048,1,128]{2,1,0:T(2,128)(2,1)S(1)} %divide_convert_fusion.1), kind=kLoop, calls=%fused_computation.65 | loop fusion | flops 2097152 | bytes 2097152 | tf_op jit(solution)/shard_map/stack | solution.py:72
  173.4 4.8 %all-to-all-start.3 = ((bf16[2048,2,128]{2,1,0:T(2,128)(2,1)}), bf16[2048,2,128]{2,1,0:T(2,128)(2,1)S(1)}, u32[]{:S(2)}, u32[]{:S(2)}) async-start(bf16[2048,2,128]{2,1,0:T(2,128)(2,1)} %pad_maximum_fusion), calls=%async_computation.3 | async-start | bytes 2097152 | tf_op jit(solution)/shard_map/all_to_all | solution.py:73
  178.9 24.2 %all-to-all-done.3 = bf16[2048,2,128]{2,1,0:T(2,128)(2,1)S(1)} async-done(((bf16[2048,2,128]{2,1,0:T(2,128)(2,1)}), bf16[2048,2,128]{2,1,0:T(2,128)(2,1)S(1)}, u32[]{:S(2)}, u32[]{:S(2)}) %all-to-all-start.3) | async-done | bytes 1048608 | tf_op jit(solution)/shard_map/all_to_all | solution.py:73
  204.8 1.9 copy.50
  208.4 2.3 %copy.51 = bf16[128,4096]{1,0:T(8,128)(2,1)} copy(bf16[128,4096]{0,1:T(8,128)(2,1)} %fusion.70) | data formatting | bytes 2097152 | tf_op jit(solution)/shard_map/convert_element_type | solution.py:76
  (113 shorter events, 56.4 us)
Async XLA Ops:
  0.0 178.8 %copy-start = (f32[35,4096]{1,0:T(8,128)S(1)}, f32[35,4096]{1,0:T(8,128)}, u32[]{:S(2)}) copy-start(f32[35,4096]{1,0:T(8,128)} %param.25) | copy-start | bytes 1720324
  0.0 10.3 %copy-start.4 = (bf16[128,4096]{1,0:T(8,128)(2,1)S(1)}, bf16[128,4096]{1,0:T(8,128)(2,1)}, u32[]{:S(2)}) copy-start(bf16[128,4096]{1,0:T(8,128)(2,1)} %param.19) | copy-start | bytes 3145732
  3.1 31.5 %all-to-all-start = ((bf16[128,32,128]{2,0,1:T(8,128)(2,1)}), bf16[128,32,128]{2,0,1:T(8,128)(2,1)S(1)}, u32[]{:S(2)}, u32[]{:S(2)}) async-start(bf16[128,32,128]{2,0,1:T(8,128)(2,1)} %copy.41), calls=%async_computation | async-start | bytes 2097152 | tf_op jit(solution)/shard_map/all_to_all | solution.py:55
  34.6 9.6 %copy-start.2 = (bf16[128,32,128]{2,0,1:T(8,128)(2,1)}, bf16[128,32,128]{2,0,1:T(8,128)(2,1)S(1)}, u32[]{:S(2)}) copy-start(bf16[128,32,128]{2,0,1:T(8,128)(2,1)S(1)} %all-to-all-done) | copy-start | bytes 3145732
  34.6 29.8 %all-to-all-start.1 = ((bf16[128,32,128]{0,2,1:T(8,128)(2,1)}), bf16[128,32,128]{0,2,1:T(8,128)(2,1)}, u32[]{:S(2)}, u32[]{:S(2)}) async-start(bf16[128,32,128]{0,2,1:T(8,128)(2,1)} %bitcast.22), calls=%async_computation.1 | async-start | bytes 2097152 | tf_op jit(solution)/shard_map/all_to_all | solution.py:56
  44.2 1.2 copy-start.3
  64.4 29.8 %all-to-all-start.2 = ((bf16[128,32,128]{0,2,1:T(8,128)(2,1)}), bf16[128,32,128]{0,2,1:T(8,128)(2,1)}, u32[]{:S(2)}, u32[]{:S(2)}) async-start(bf16[128,32,128]{0,2,1:T(8,128)(2,1)} %bitcast.163), calls=%async_computation.2 | async-start | bytes 2097152 | tf_op jit(solution)/shard_map/all_to_all | solution.py:57
  83.3 13.1 %copy-start.1 = (bf16[4,512,128]{2,1,0:T(8,128)(2,1)}, bf16[4,512,128]{2,1,0:T(8,128)(2,1)S(1)}, u32[]{:S(2)}) copy-start(bf16[4,512,128]{2,1,0:T(8,128)(2,1)S(1)} %get-tuple-element.555) | copy-start | bytes 1572868
  173.4 29.7 %all-to-all-start.3 = ((bf16[2048,2,128]{2,1,0:T(2,128)(2,1)}), bf16[2048,2,128]{2,1,0:T(2,128)(2,1)S(1)}, u32[]{:S(2)}, u32[]{:S(2)}) async-start(bf16[2048,2,128]{2,1,0:T(2,128)(2,1)} %pad_maximum_fusion), calls=%async_computation.3 | async-start | bytes 2097152 | tf_op jit(solution)/shard_map/all_to_all | solution.py:73
where the time goes:
time: 212 us; the launch traced here: 211 us
  waiting for transfers between devices  71.2 us (34%)
  matrix products  46.4 us (22%)
  other arithmetic  45.1 us (21%)
  local copies, waits for them, and re-layouts  25.2 us (12%)
  starting transfers between devices  20.9 us (10%)
    dot_general x16, matrix products, attend_group(): jnp.dot(queries, keys.T, preferred_element_type=jnp.float32) * HD ** (-0.5)  24.3 us
    all_to_all x1, waiting for transfers between devices, shards(): lax.all_to_all(heads_out, 'seq', split_axis=0, concat_axis=1, tiled=True)  24.2 us
    dot_general x16, matrix products, attend_group(): jnp.dot(expo.astype(jnp.bfloat16), values, preferred_element_type=jnp.flo...  22.1 us
    all_to_all x1, waiting for transfers between devices, shards(): lax.all_to_all(query_heads, 'seq', split_axis=1, concat_axis=0, tiled=True)  20.7 us
    convert_element_type x2, other arithmetic, shards(): outputs.append((numer / denom[:, None]).astype(jnp.bfloat16))  20.5 us
    all_to_all x1, waiting for transfers between devices, shards(): lax.all_to_all(key_heads, 'seq', split_axis=1, concat_axis=0, tiled=True)  18 us
    reduce_sum x16, other arithmetic, attend_group(): total = jnp.sum(expo, axis=1)  13 us
    all_to_all x1, waiting for transfers between devices, shards(): lax.all_to_all(value_heads, 'seq', split_axis=1, concat_axis=0, tiled=True)  8.33 us
  transfers between devices with their start and end apart: 4, of which 4 were waited for; matrix products, arithmetic and copies ran while one was open for 12% of the time, Pallas kernels for 0%

commit v1 on v0

v1 whole, which is shorter than its diff:
```python
import functools
import math

import jax
import jax.numpy as jnp
from jax import lax
from jax.experimental import pallas as pl
from jax.experimental.pallas import tpu as pltpu
from jax.sharding import PartitionSpec as P


HD = 128
TO_LOG2 = HD ** (-0.5) * math.log2(math.e)
NT = (((1,), (1,)), ((), ()))


def pack_first_body(heads_dev, q_ref, k_ref, v_ref, out_ref):
    rows = q_ref.shape[0]
    for dest in range(out_ref.shape[0]):
        base = dest * heads_dev * HD
        head0 = slice(base, base + HD)
        out_ref[dest, :rows] = q_ref[:, head0]
        out_ref[dest, rows : 2 * rows] = k_ref[:, head0]
        out_ref[dest, 2 * rows : 3 * rows] = v_ref[:, head0]
        for head in range(1, heads_dev):
            cols = slice(base + head * HD, base + (head + 1) * HD)
            out_ref[dest, (2 + head) * rows : (3 + head) * rows] = q_ref[:, cols]


def pack_first(q, k, v, n, heads_dev):
    rows, width = q.shape
    per = min(4, n)
    cols = per * heads_dev * HD
    src = pl.BlockSpec((rows, cols), lambda i: (0, i))
    return pl.pallas_call(
        functools.partial(pack_first_body, heads_dev),
        out_shape=jax.ShapeDtypeStruct((n, (2 + heads_dev) * rows, HD), q.dtype),
        grid=(n // per,),
        in_specs=[src, src, src],
        out_specs=pl.BlockSpec((per, (2 + heads_dev) * rows, HD), lambda i: (i, 0, 0)),
        cost_estimate=pl.CostEstimate(
            flops=0, bytes_accessed=2 * rows * width * 5, transcendentals=0
        ),
    )(q, k, v)


def pack_rest_body(heads_dev, me_ref, k_ref, v_ref, *out_refs):
    rows = k_ref.shape[0]
    for step, out_ref in enumerate(out_refs):
        dest = me_ref[0] ^ step
        for head in range(1, heads_dev):
            at = pl.multiple_of((dest * heads_dev + head) * HD, HD)
            out_ref[head - 1, :rows] = k_ref[:, pl.ds(at, HD)]
            out_ref[head - 1, rows:] = v_ref[:, pl.ds(at, HD)]


def pack_rest(me, k, v, n, heads_dev):
    rows, width = k.shape
    whole = pl.BlockSpec(memory_space=pltpu.VMEM)
    block = jax.ShapeDtypeStruct((heads_dev - 1, 2 * rows, HD), k.dtype)
    return pl.pallas_call(
        functools.partial(pack_rest_body, heads_dev),
        out_shape=[block] * n,
        in_specs=[pl.BlockSpec(memory_space=pltpu.SMEM), whole, whole],
        out_specs=[whole] * n,
        cost_estimate=pl.CostEstimate(
            flops=0, bytes_accessed=2 * rows * width * 3, transcendentals=0
        ),
    )(me, k, v)


def keep_old_body(scal_ref, k_low, k_high, v_low, v_high, k_ref, v_ref):
    rows = k_low.shape[0]
    at = lax.broadcasted_iota(jnp.int32, (rows, HD), 0) + pl.program_id(1) * rows
    before = at < scal_ref[1]
    for low, high, out_ref in ((k_low, k_high, k_ref), (v_low, v_high, v_ref)):
        kept = jnp.where(before, low[...].astype(jnp.float32), high[...].astype(jnp.float32))
        out_ref[0] = kept.astype(out_ref.dtype)


def keep_old(scal, stale_k, stale_v, patch, heads_dev):
    n_old = stale_k.shape[0] - patch
    rows = math.gcd(math.gcd(n_old, patch), 1024)
    low = pl.BlockSpec((rows, HD), lambda h, i, s: (i, h))
    high = pl.BlockSpec((rows, HD), lambda h, i, s: (i + patch // rows, h))
    out = pl.BlockSpec((1, rows, HD), lambda h, i, s: (h, i, 0))
    kept = jax.ShapeDtypeStruct((heads_dev, n_old, HD), stale_k.dtype)
    return pl.pallas_call(
        keep_old_body,
        out_shape=[kept, kept],
        grid_spec=pltpu.PrefetchScalarGridSpec(
            num_scalar_prefetch=1,
            grid=(heads_dev, n_old // rows),
            in_specs=[low, high, low, high],
            out_specs=[out, out],
        ),
        cost_estimate=pl.CostEstimate(
            flops=0, bytes_accessed=12 * heads_dev * n_old * HD, transcendentals=0
        ),
    )(scal, stale_k, stale_k, stale_v, stale_v)


def attend_body(rows, n_new_refs, scal_ref, q_ref, *refs):
    new_refs = refs[:n_new_refs]
    old_k_ref, old_v_ref, gate_ref, out_ref, keys, values = refs[n_new_refs:]
    total = keys.shape[0]
    n_old = old_k_ref.shape[1]
    patch = total - n_old

    @pl.when(pl.program_id(0) == 0)
    def _():
        keys[:n_old] = old_k_ref[0]
        values[:n_old, :HD] = old_v_ref[0]
        values[:, HD:] = jnp.ones((total, HD), jnp.bfloat16)
        if n_new_refs == 2:
            keys[n_old:] = new_refs[0][...].reshape(patch, HD)
            values[n_old:, :HD] = new_refs[1][...].reshape(patch, HD)
        else:
            for source, ref in enumerate(new_refs):
                at = slice(n_old + source * rows, n_old + (source + 1) * rows)
                keys[at] = ref[0, :rows]
                values[at, :HD] = ref[0, rows:]

    queries = q_ref[...].reshape(-1, HD)
    gate = gate_ref[pl.ds(scal_ref[2], 1), :]
    block = min(256, queries.shape[0])
    chunk = 512
    for start in range(0, queries.shape[0], block):
        q = queries[start : start + block]
        top, acc = None, None
        for at in range(0, total, chunk):
            s = lax.dot_general(
                q, keys[at : at + chunk], NT, preferred_element_type=jnp.float32
            )
            chunk_top = jnp.max(s, axis=1, keepdims=True)
            new_top = chunk_top if top is None else jnp.maximum(top, chunk_top)
            p = jnp.exp2((s - new_top) * TO_LOG2).astype(jnp.bfloat16)
            part = jnp.dot(p, values[at : at + chunk], preferred_element_type=jnp.float32)
            if top is None:
                acc = part
            else:
                acc = acc * jnp.exp2((top - new_top) * TO_LOG2) + part
            top = new_top
        attn = (acc[:, :HD] / acc[:, HD:]).astype(jnp.bfloat16)
        gated = (attn.astype(jnp.float32) * gate).astype(jnp.bfloat16)
        for part in range(block // rows):
            piece = gated[part * rows : (part + 1) * rows]
            out_ref[start // rows + part] = piece


def attend(scal, first, head, new_parts, old_k, old_v, gate_table, n, rows, heads_dev):
    per = min(4, n)
    n_old = old_k.shape[1]
    patch = n * rows
    total = n_old + patch
    q_at = 0 if head == 0 else 2 + head
    query = pl.BlockSpec((per, rows, HD), lambda i, s: (i, q_at, 0))
    if head == 0:
        new_ops = [first, first]
        new_specs = [
            pl.BlockSpec((n, rows, HD), lambda i, s: (0, 1, 0)),
            pl.BlockSpec((n, rows, HD), lambda i, s: (0, 2, 0)),
        ]
    else:
        new_ops = new_parts
        new_specs = [pl.BlockSpec((1, 2 * rows, HD), lambda i, s: (head - 1, 0, 0))] * n
    old = pl.BlockSpec((1, n_old, HD), lambda i, s: (head, 0, 0))
    gate = pl.BlockSpec(
        (gate_table.shape[0], HD), lambda i, s: (0, s[0] * heads_dev + head)
    )
    return pl.pallas_call(
        functools.partial(attend_body, rows, len(new_ops)),
        out_shape=jax.ShapeDtypeStruct((n, rows, HD), jnp.bfloat16),
        grid_spec=pltpu.PrefetchScalarGridSpec(
            num_scalar_prefetch=1,
            grid=(n // per,),
            in_specs=[query, *new_specs, old, old, gate],
            out_specs=pl.BlockSpec((per, rows, HD), lambda i, s: (i, 0, 0)),
            scratch_shapes=[
                pltpu.VMEM((total, HD), jnp.bfloat16),
                pltpu.VMEM((total, 2 * HD), jnp.bfloat16),
            ],
        ),
        compiler_params=pltpu.CompilerParams(vmem_limit_bytes=32 << 20),
        cost_estimate=pl.CostEstimate(
            flops=4 * patch * total * 2 * HD,
            bytes_accessed=2 * HD * (2 * patch + 2 * total),
            transcendentals=patch * total,
        ),
    )(scal, first, *new_ops, old_k, old_v, gate_table)


def unpack_body(heads_dev, *refs):
    out_ref = refs[-1]
    for source in range(refs[0].shape[0]):
        for head in range(heads_dev):
            at = (source * heads_dev + head) * HD
            out_ref[:, at : at + HD] = refs[head][source]


def unpack(parts, n, rows, heads_dev):
    per = min(4, n)
    src = pl.BlockSpec((per, rows, HD), lambda i: (i, 0, 0))
    return pl.pallas_call(
        functools.partial(unpack_body, heads_dev),
        out_shape=jax.ShapeDtypeStruct((rows, n * heads_dev * HD), parts[0].dtype),
        grid=(n // per,),
        in_specs=[src] * heads_dev,
        out_specs=pl.BlockSpec((rows, per * heads_dev * HD), lambda i: (0, i)),
    )(*parts)


def shards(
    fresh_query, fresh_key, fresh_value, stale_key, stale_value, patch_start, timestep, gate_table
):
    n = lax.axis_size("seq")
    rows = fresh_query.shape[0]
    heads_dev = stale_key.shape[1] // HD
    me = lax.axis_index("seq").astype(jnp.int32)
    scal = jnp.stack([me, patch_start[0], timestep[0]])
    exchange = functools.partial(
        lax.all_to_all, axis_name="seq", split_axis=0, concat_axis=0, tiled=True
    )
    packed = pack_first(fresh_query, fresh_key, fresh_value, n, heads_dev)
    first = exchange(packed)
    old_k, old_v = keep_old(scal, stale_key, stale_value, n * rows, heads_dev)
    rest = None
    if heads_dev > 1:
        blocks = pack_rest(me[None], fresh_key, fresh_value, n, heads_dev)
        rest = [blocks[0]]
        for step in range(1, n):
            pairs = [(i, i ^ step) for i in range(n)]
            rest.append(lax.ppermute(blocks[step], "seq", pairs))
    parts = []
    for head in range(heads_dev):
        gated = attend(
            scal, first, head, rest, old_k, old_v, gate_table,
            n, rows, heads_dev,
        )
        parts.append(exchange(gated))
    return unpack(parts, n, rows, heads_dev)


def solution(mesh):
    return jax.shard_map(
        shards,
        mesh=mesh,
        in_specs=(
            P(("grp", "seq"), None),
            P(("grp", "seq"), None),
            P(("grp", "seq"), None),
            P("grp", "seq"),
            P("grp", "seq"),
            P("grp"),
            P("grp"),
            P(),
        ),
        out_specs=P(("grp", "seq"), None),
        check_vma=False,
    )
```

time: 212 us -> 154 us (0.73)
  matrix products: 46.4 us -> 0 us
  other arithmetic: 45.1 us -> 0.61 us
  Pallas kernels: 0 us -> 40.3 us
  waiting for transfers between devices: 71.2 us -> 45.5 us
  starting transfers between devices: 20.9 us -> 39.2 us
  local copies, waits for them, and re-layouts: 25.2 us -> 7.85 us
  blocking collectives: 0 us -> 17.2 us
    dot_general x32 -> x0, matrix products: 46.4 us -> none  [the longest x16 24.3 us: attend_group(): jnp.dot(queries, keys.T, preferred_element_type=jnp.float32) * HD ** (-0.5)]
    pallas_call x0 -> x6, Pallas kernels: none -> 40.3 us  [the longest x2 24.9 us: attend(): pl.pallas_call(functools.partial(attend_body, rows, len(new_ops)), out_sh...]
    all_to_all x4 -> x2, waiting for transfers between devices: 71.2 us -> 32.4 us  [the longest x1 32.4 us: shards(): first = exchange(packed)]
    ppermute x0 -> x15, starting transfers between devices: none -> 26.5 us  [shards(): rest.append(lax.ppermute(blocks[step], 'seq', pairs))]
    convert_element_type x4 -> x0, other arithmetic: 23.8 us -> none  [the longest x2 20.5 us: shards(): outputs.append((numer / denom[:, None]).astype(jnp.bfloat16))]
    all_to_all x0 -> x1, blocking collectives: none -> 17.2 us  [shards(): parts.append(exchange(gated))]
    ppermute x0 -> x15, waiting for transfers between devices: none -> 13.1 us  [shards(): rest.append(lax.ppermute(blocks[step], 'seq', pairs))]
    reduce_sum x16 -> x0, other arithmetic: 13 us -> none  [attend_group(): total = jnp.sum(expo, axis=1)]
  transfers between devices with their start and end apart: 4 -> 17, of which waited for: 4 -> 6; matrix products, arithmetic and copies ran while one was open for 12% -> 0% of each run, Pallas kernels for 0% -> 22%
where the time goes in v1:
time: 154 us; the launch traced here: 152 us
  waiting for transfers between devices  45.5 us (30%)
  Pallas kernels  40.3 us (26%)
  starting transfers between devices  39.2 us (25%)
  blocking collectives  17.2 us (11%)
  local copies, waits for them, and re-layouts  7.85 us (5%)
    all_to_all x1, waiting for transfers between devices, shards(): first = exchange(packed)  32.4 us
    ppermute x15, starting transfers between devices, shards(): rest.append(lax.ppermute(blocks[step], 'seq', pairs))  26.5 us
    pallas_call x2, Pallas kernels, attend(): pl.pallas_call(functools.partial(attend_body, rows, len(new_ops)), out_sh...  24.9 us
    all_to_all x1, blocking collectives, shards(): parts.append(exchange(gated))  17.2 us
    ppermute x15, waiting for transfers between devices, shards(): rest.append(lax.ppermute(blocks[step], 'seq', pairs))  13.1 us
    unnamed x34, local copies, waits for them, and re-layouts  7.85 us
    all_to_all x1, starting transfers between devices, shards(): first = exchange(packed)  6.58 us
    all_to_all x1, starting transfers between devices, shards(): parts.append(exchange(gated))  6.16 us
  transfers between devices with their start and end apart: 17, of which 6 were waited for; matrix products, arithmetic and copies ran while one was open for 0% of the time, Pallas kernels for 22%

profile of v1, /device:TPU:11, one launch (start us, length us, event | category | flops | bytes accessed | tf_op | source)
XLA Modules:
  0.0 152.0 jit_solution(5316007796433803228)
XLA Ops:
  0.0 4.0 %shard_map.82 = bf16[16,512,128]{2,1,0:T(8,128)(2,1)} custom-call(bf16[128,4096]{1,0:T(8,128)(2,1)} %q_ref.1, bf16[128,4096]{1,0:T(8,128)(2,1)} %k_ref.3, bf16[128,4096]{1,0:T(8,128)(2,1)} %v_ref.3), custom_call_target="tpu_custom_call" | custom-call | bytes 5242880 | tf_op jit(solution)/shard_map/pallas_call | solution.py:35
  4.0 6.6 %all-to-all-start = ((bf16[16,512,128]{2,1,0:T(8,128)(2,1)}), bf16[16,512,128]{2,1,0:T(8,128)(2,1)S(1)}, u32[]{:S(2)}, u32[]{:S(2)}) async-start(bf16[16,512,128]{2,1,0:T(8,128)(2,1)} %shard_map.82), calls=%async_computation | async-start | bytes 4194304 | tf_op jit(solution)/shard_map/all_to_all | solution.py:225
  10.6 2.8 %shard_map.85 = (bf16[1,256,128]{2,1,0:T(8,128)(2,1)}, bf16[1,256,128]{2,1,0:T(8,128)(2,1)}, bf16[1,256,128]{2,1,0:T(8,128)(2,1)}, bf16[1,256,128]{2,1,0:T(8,128...) custom-call(s32[1]{0:T(128)} %bitcast.me_ref, ...), custom_call_target="tpu_custom_call" | custom-call | bytes 3145728 | tf_op jit(solution)/shard_map/pallas_call | solution.py:61
  13.9 1.2 collective-permute-start.1
  15.7 1.6 %collective-permute-start.4 = (bf16[1,256,128]{2,1,0:T(8,128)(2,1)}, bf16[1,256,128]{2,1,0:T(8,128)(2,1)S(1)}, u32[]{:S(2)}, u32[]{:S(2)}) collective-permute-start(bf16[1,256,128]{2,1,0:T(8,128)(2,1)} %get-tuple-element.30), channel_id=1, source_target_pairs={{0,5},{1,4},{2,7},{3,6},{4,1},{5,0},{6,3},{7,2},{8,13},{9,12},{10,... | collective-permute-start | bytes 196616 | tf_op jit(solution)/shard_map/ppermute | solution.py:233
  19.3 5.1 %shard_map.83 = (bf16[2,2048,128]{2,1,0:T(8,128)(2,1)}, bf16[2,2048,128]{2,1,0:T(8,128)(2,1)}) custom-call(s32[3]{0:T(128)} %pad_add_fusion.scal_ref, bf16[4096,256]{1,0:T(8,128)(2,1)} %k_high.1, bf16[4096,256]{1,0:T(8,128)(2,1)} %k_high.1, bf16[4096,256]{1,0:T(8,128)(2,1)} %v_high.1, bf16[4096,256]{1,0:T(8,128)(2,1)} %v_high.1), custom_call_target="tpu_custom_call" | custom-call | bytes 6291456 | tf_op jit(solution)/shard_map/pallas_call | solution.py:88
  24.3 32.4 %all-to-all-done.q_ref.refs_0_.refs_1_ = bf16[16,512,128]{2,1,0:T(8,128)(2,1)S(1)} async-done(((bf16[16,512,128]{2,1,0:T(8,128)(2,1)}), bf16[16,512,128]{2,1,0:T(8,128)(2,1)S(1)}, u32[]{:S(2)}, u32[]{:S(2)}) %all-to-all-start) | async-done | bytes 2097184 | tf_op jit(solution)/shard_map/all_to_all | solution.py:225
  56.7 1.2 copy-done.1
  57.9 1.2 copy-done.3
  59.2 12.8 %shard_map.84 = bf16[16,128,128]{2,1,0:T(8,128)(2,1)} custom-call(s32[3]{0:T(128)S(1)} %copy-done, bf16[16,512,128]{2,1,0:T(8,128)(2,1)S(1)} %all-to-all-done.q_ref.refs_0_.refs_1_, bf16[16,512,128]{2,1,0:T(8,128)(2,1)S(1)} %all-to-all-done.q_ref.refs_0_.refs_1_, bf16[16,512,128]{2,1,0:T(8,128)(2,1)S(1)} %all-to-all-done.q_ref.refs_0_.refs_1_, ...), custom_call_target="tpu_custom_call" | custom-call | flops 8589934592 | bytes 3145728 | tf_op jit(solution)/shard_map/pallas_call | solution.py:171
  72.0 6.2 %all-to-all-start.1 = ((bf16[16,128,128]{2,1,0:T(8,128)(2,1)}), bf16[16,128,128]{2,1,0:T(8,128)(2,1)}, u32[]{:S(2)}, u32[]{:S(2)}) async-start(bf16[16,128,128]{2,1,0:T(8,128)(2,1)} %shard_map.84), calls=%async_computation.1 | async-start | bytes 1048576 | tf_op jit(solution)/shard_map/all_to_all | solution.py:240
  78.2 1.2 collective-permute-start.5
  79.4 1.7 %collective-permute-start.6 = (bf16[1,256,128]{2,1,0:T(8,128)(2,1)}, bf16[1,256,128]{2,1,0:T(8,128)(2,1)S(1)}, u32[]{:S(2)}, u32[]{:S(2)}) collective-permute-start(bf16[1,256,128]{2,1,0:T(8,128)(2,1)} %get-tuple-element.32), channel_id=1, source_target_pairs={{0,7},{1,6},{2,5},{3,4},{4,3},{5,2},{6,1},{7,0},{8,15},{9,14},{10,... | collective-permute-start | bytes 196616 | tf_op jit(solution)/shard_map/ppermute | solution.py:233
  81.2 2.1 %collective-permute-start.7 = (bf16[1,256,128]{2,1,0:T(8,128)(2,1)}, bf16[1,256,128]{2,1,0:T(8,128)(2,1)S(1)}, u32[]{:S(2)}, u32[]{:S(2)}) collective-permute-start(bf16[1,256,128]{2,1,0:T(8,128)(2,1)} %get-tuple-element.33), channel_id=1, source_target_pairs={{0,8},{1,9},{2,10},{3,11},{4,12},{5,13},{6,14},{7,15},{8,0},{9,1},... | collective-permute-start | bytes 196616 | tf_op jit(solution)/shard_map/ppermute | solution.py:233
  84.8 3.0 %collective-permute-start.9 = (bf16[1,256,128]{2,1,0:T(8,128)(2,1)S(1)}, bf16[1,256,128]{2,1,0:T(8,128)(2,1)S(1)}, u32[]{:S(2)}, u32[]{:S(2)}) collective-permute-start(bf16[1,256,128]{2,1,0:T(8,128)(2,1)S(1)} %copy-done.16), channel_id=1, source_target_pairs={{0,10},{1,11},{2,8},{3,9},{4,14},{5,15},{6,12},{7,13},{8,2},{9,3},... | collective-permute-start | bytes 196616 | tf_op jit(solution)/shard_map/ppermute | solution.py:233
  87.8 2.3 %collective-permute-done.5.refs_6_ = bf16[1,256,128]{2,1,0:T(8,128)(2,1)S(1)} collective-permute-done((bf16[1,256,128]{2,1,0:T(8,128)(2,1)}, bf16[1,256,128]{2,1,0:T(8,128)(2,1)S(1)}, u32[]{:S(2)}, u32[]{:S(2)}) %collective-permute-start.5) | collective-permute-done | bytes 65568 | tf_op jit(solution)/shard_map/ppermute | solution.py:233
  90.0 2.7 %collective-permute-start.10 = (bf16[1,256,128]{2,1,0:T(8,128)(2,1)S(1)}, bf16[1,256,128]{2,1,0:T(8,128)(2,1)S(1)}, u32[]{:S(2)}, u32[]{:S(2)}) collective-permute-start(bf16[1,256,128]{2,1,0:T(8,128)(2,1)S(1)} %copy-done.15), channel_id=1, source_target_pairs={{0,11},{1,10},{2,9},{3,8},{4,15},{5,14},{6,13},{7,12},{8,3},{9,2},... | collective-permute-start | bytes 196616 | tf_op jit(solution)/shard_map/ppermute | solution.py:233
  92.8 2.3 %collective-permute-start.11 = (bf16[1,256,128]{2,1,0:T(8,128)(2,1)S(1)}, bf16[1,256,128]{2,1,0:T(8,128)(2,1)S(1)}, u32[]{:S(2)}, u32[]{:S(2)}) collective-permute-start(bf16[1,256,128]{2,1,0:T(8,128)(2,1)S(1)} %copy-done.14), channel_id=1, source_target_pairs={{0,12},{1,13},{2,14},{3,15},{4,8},{5,9},{6,10},{7,11},{8,4},{9,5},... | collective-permute-start | bytes 196616 | tf_op jit(solution)/shard_map/ppermute | solution.py:233
  95.1 5.5 %collective-permute-start.12 = (bf16[1,256,128]{2,1,0:T(8,128)(2,1)S(1)}, bf16[1,256,128]{2,1,0:T(8,128)(2,1)S(1)}, u32[]{:S(2)}, u32[]{:S(2)}) collective-permute-start(bf16[1,256,128]{2,1,0:T(8,128)(2,1)S(1)} %copy-done.13), channel_id=1, source_target_pairs={{0,13},{1,12},{2,15},{3,14},{4,9},{5,8},{6,11},{7,10},{8,5},{9,4},... | collective-permute-start | bytes 196616 | tf_op jit(solution)/shard_map/ppermute | solution.py:233
  100.5 1.2 collective-permute-start.13
  101.7 2.5 %collective-permute-start.14 = (bf16[1,256,128]{2,1,0:T(8,128)(2,1)S(1)}, bf16[1,256,128]{2,1,0:T(8,128)(2,1)S(1)}, u32[]{:S(2)}, u32[]{:S(2)}) collective-permute-start(bf16[1,256,128]{2,1,0:T(8,128)(2,1)S(1)} %copy-done.11), channel_id=1, source_target_pairs={{0,15},{1,14},{2,13},{3,12},{4,11},{5,10},{6,9},{7,8},{8,7},{9,6},... | collective-permute-start | bytes 196616 | tf_op jit(solution)/shard_map/ppermute | solution.py:233
  104.3 2.6 %collective-permute-done.11.refs_12_ = bf16[1,256,128]{2,1,0:T(8,128)(2,1)S(1)} collective-permute-done((bf16[1,256,128]{2,1,0:T(8,128)(2,1)S(1)}, bf16[1,256,128]{2,1,0:T(8,128)(2,1)S(1)}, u32[]{:S(2)}, u32[]{:S(2)}) %collective-permute-start.11) | collective-permute-done | bytes 65568 | tf_op jit(solution)/shard_map/ppermute | solution.py:233
  106.9 5.1 %collective-permute-done.12.refs_13_ = bf16[1,256,128]{2,1,0:T(8,128)(2,1)S(1)} collective-permute-done((bf16[1,256,128]{2,1,0:T(8,128)(2,1)S(1)}, bf16[1,256,128]{2,1,0:T(8,128)(2,1)S(1)}, u32[]{:S(2)}, u32[]{:S(2)}) %collective-permute-start.12) | collective-permute-done | bytes 65568 | tf_op jit(solution)/shard_map/ppermute | solution.py:233
  112.0 1.5 collective-permute-done.13.refs_14_
  113.4 1.7 %collective-permute-done.14.refs_15_ = bf16[1,256,128]{2,1,0:T(8,128)(2,1)S(1)} collective-permute-done((bf16[1,256,128]{2,1,0:T(8,128)(2,1)S(1)}, bf16[1,256,128]{2,1,0:T(8,128)(2,1)S(1)}, u32[]{:S(2)}, u32[]{:S(2)}) %collective-permute-start.14) | collective-permute-done | bytes 65568 | tf_op jit(solution)/shard_map/ppermute | solution.py:233
  115.1 1.2 copy-done.2
  116.3 1.2 copy-done.4
  117.5 0.8 copy-done.8
  118.4 0.8 copy-done.10
  119.2 12.1 %shard_map.86 = bf16[16,128,128]{2,1,0:T(8,128)(2,1)S(1)} custom-call(s32[3]{0:T(128)S(1)} %copy-done, bf16[16,512,128]{2,1,0:T(8,128)(2,1)S(1)} %all-to-all-done.q_ref.refs_0_.refs_1_, bf16[1,256,128]{2,1,0:T(8,128)(2,1)S(1)} %copy-done.6, bf16[1,256,128]{2,1,0:T(8,128)(2,1)S(1)} %collective-permute-done.refs_1_, ...), custom_call_target="tpu_custom_call" | custom-call | flops 8589934592 | bytes 3145728 | tf_op jit(solution)/shard_map/pallas_call | solution.py:171
  131.3 17.2 %all_to_all.15.refs_1_ = bf16[16,128,128]{2,1,0:T(8,128)(2,1)} all-to-all(bf16[16,128,128]{2,1,0:T(8,128)(2,1)S(1)} %shard_map.86), channel_id=1, replica_groups=mesh['grp'=2,'seq'=16] {'seq'}, dimensions={0} | all-to-all | bytes 1048576 | tf_op jit(solution)/shard_map/all_to_all | solution.py:240
  148.5 3.5 %shard_map.87 = bf16[128,4096]{1,0:T(8,128)(2,1)} custom-call(bf16[16,128,128]{2,1,0:T(8,128)(2,1)} %all-to-all-done.1.refs_0_, bf16[16,128,128]{2,1,0:T(8,128)(2,1)} %all_to_all.15.refs_1_), custom_call_target="tpu_custom_call" | custom-call | tf_op jit(solution)/shard_map/pallas_call | solution.py:204
  (44 shorter events, 3.3 us)
Async XLA Ops:
  4.0 52.7 %all-to-all-start = ((bf16[16,512,128]{2,1,0:T(8,128)(2,1)}), bf16[16,512,128]{2,1,0:T(8,128)(2,1)S(1)}, u32[]{:S(2)}, u32[]{:S(2)}) async-start(bf16[16,512,128]{2,1,0:T(8,128)(2,1)} %shard_map.82), calls=%async_computation | async-start | bytes 4194304 | tf_op jit(solution)/shard_map/all_to_all | solution.py:225
  13.4 64.7 %collective-permute-start = (bf16[1,256,128]{2,1,0:T(8,128)(2,1)}, bf16[1,256,128]{2,1,0:T(8,128)(2,1)S(1)}, u32[]{:S(2)}, u32[]{:S(2)}) collective-permute-start(bf16[1,256,128]{2,1,0:T(8,128)(2,1)} %get-tuple-element.26), channel_id=1, source_target_pairs={{0,1},{1,0},{2,3},{3,2},{4,5},{5,4},{6,7},{7,6},{8,9},{9,8},{10,11... | collective-permute-start | bytes 196616 | tf_op jit(solution)/shard_map/ppermute | solution.py:233
  13.9 65.5 %collective-permute-start.1 = (bf16[1,256,128]{2,1,0:T(8,128)(2,1)}, bf16[1,256,128]{2,1,0:T(8,128)(2,1)S(1)}, u32[]{:S(2)}, u32[]{:S(2)}) collective-permute-start(bf16[1,256,128]{2,1,0:T(8,128)(2,1)} %get-tuple-element.27), channel_id=1, source_target_pairs={{0,2},{1,3},{2,0},{3,1},{4,6},{5,7},{6,4},{7,5},{8,10},{9,11},{10,... | collective-permute-start | bytes 196616 | tf_op jit(solution)/shard_map/ppermute | solution.py:233
  15.1 66.1 %collective-permute-start.2 = (bf16[1,256,128]{2,1,0:T(8,128)(2,1)}, bf16[1,256,128]{2,1,0:T(8,128)(2,1)S(1)}, u32[]{:S(2)}, u32[]{:S(2)}) collective-permute-start(bf16[1,256,128]{2,1,0:T(8,128)(2,1)} %get-tuple-element.28), channel_id=1, source_target_pairs={{0,3},{1,2},{2,1},{3,0},{4,7},{5,6},{6,5},{7,4},{8,11},{9,10},{10,... | collective-permute-start | bytes 196616 | tf_op jit(solution)/shard_map/ppermute | solution.py:233
  15.6 67.6 %collective-permute-start.3 = (bf16[1,256,128]{2,1,0:T(8,128)(2,1)}, bf16[1,256,128]{2,1,0:T(8,128)(2,1)S(1)}, u32[]{:S(2)}, u32[]{:S(2)}) collective-permute-start(bf16[1,256,128]{2,1,0:T(8,128)(2,1)} %get-tuple-element.29), channel_id=1, source_target_pairs={{0,4},{1,5},{2,6},{3,7},{4,0},{5,1},{6,2},{7,3},{8,12},{9,13},{10,... | collective-permute-start | bytes 196616 | tf_op jit(solution)/shard_map/ppermute | solution.py:233
  15.7 68.4 %collective-permute-start.4 = (bf16[1,256,128]{2,1,0:T(8,128)(2,1)}, bf16[1,256,128]{2,1,0:T(8,128)(2,1)S(1)}, u32[]{:S(2)}, u32[]{:S(2)}) collective-permute-start(bf16[1,256,128]{2,1,0:T(8,128)(2,1)} %get-tuple-element.30), channel_id=1, source_target_pairs={{0,5},{1,4},{2,7},{3,6},{4,1},{5,0},{6,3},{7,2},{8,13},{9,12},{10,... | collective-permute-start | bytes 196616 | tf_op jit(solution)/shard_map/ppermute | solution.py:233
  19.3 37.4 %copy-start = (s32[3]{0:T(128)S(1)}, s32[3]{0:T(128)}, u32[]{:S(2)}) copy-start(s32[3]{0:T(128)} %pad_add_fusion.scal_ref) | copy-start | bytes 40
  19.3 37.4 %copy-start.5 = (f32[35,4096]{1,0:T(8,128)S(1)}, f32[35,4096]{1,0:T(8,128)}, u32[]{:S(2)}) copy-start(f32[35,4096]{1,0:T(8,128)} %refs_18_.1) | copy-start | bytes 1720324
  56.7 1.2 copy-start.1
  57.9 1.2 copy-start.3
  59.2 25.6 %copy-start.16 = (bf16[1,256,128]{2,1,0:T(8,128)(2,1)S(1)}, bf16[1,256,128]{2,1,0:T(8,128)(2,1)}, u32[]{:S(2)}) copy-start(bf16[1,256,128]{2,1,0:T(8,128)(2,1)} %get-tuple-element.35) | copy-start | bytes 196612
  59.2 30.9 %copy-start.15 = (bf16[1,256,128]{2,1,0:T(8,128)(2,1)S(1)}, bf16[1,256,128]{2,1,0:T(8,128)(2,1)}, u32[]{:S(2)}) copy-start(bf16[1,256,128]{2,1,0:T(8,128)(2,1)} %get-tuple-element.36) | copy-start | bytes 196612
  59.2 33.6 %copy-start.14 = (bf16[1,256,128]{2,1,0:T(8,128)(2,1)S(1)}, bf16[1,256,128]{2,1,0:T(8,128)(2,1)}, u32[]{:S(2)}) copy-start(bf16[1,256,128]{2,1,0:T(8,128)(2,1)} %get-tuple-element.37) | copy-start | bytes 196612
  59.2 35.9 %copy-start.13 = (bf16[1,256,128]{2,1,0:T(8,128)(2,1)S(1)}, bf16[1,256,128]{2,1,0:T(8,128)(2,1)}, u32[]{:S(2)}) copy-start(bf16[1,256,128]{2,1,0:T(8,128)(2,1)} %get-tuple-element.38) | copy-start | bytes 196612
  59.2 41.4 %copy-start.12 = (bf16[1,256,128]{2,1,0:T(8,128)(2,1)S(1)}, bf16[1,256,128]{2,1,0:T(8,128)(2,1)}, u32[]{:S(2)}) copy-start(bf16[1,256,128]{2,1,0:T(8,128)(2,1)} %get-tuple-element.39) | copy-start | bytes 196612
  59.2 42.6 %copy-start.11 = (bf16[1,256,128]{2,1,0:T(8,128)(2,1)S(1)}, bf16[1,256,128]{2,1,0:T(8,128)(2,1)}, u32[]{:S(2)}) copy-start(bf16[1,256,128]{2,1,0:T(8,128)(2,1)} %get-tuple-element.40) | copy-start | bytes 196612
  59.2 55.9 %copy-start.6 = (bf16[1,256,128]{2,1,0:T(8,128)(2,1)S(1)}, bf16[1,256,128]{2,1,0:T(8,128)(2,1)}, u32[]{:S(2)}) copy-start(bf16[1,256,128]{2,1,0:T(8,128)(2,1)} %get-tuple-element.25.refs_0_) | copy-start | bytes 196612
  72.0 59.3 %all-to-all-start.1 = ((bf16[16,128,128]{2,1,0:T(8,128)(2,1)}), bf16[16,128,128]{2,1,0:T(8,128)(2,1)}, u32[]{:S(2)}, u32[]{:S(2)}) async-start(bf16[16,128,128]{2,1,0:T(8,128)(2,1)} %shard_map.84), calls=%async_computation.1 | async-start | bytes 1048576 | tf_op jit(solution)/shard_map/all_to_all | solution.py:240
  78.2 11.9 %collective-permute-start.5 = (bf16[1,256,128]{2,1,0:T(8,128)(2,1)}, bf16[1,256,128]{2,1,0:T(8,128)(2,1)S(1)}, u32[]{:S(2)}, u32[]{:S(2)}) collective-permute-start(bf16[1,256,128]{2,1,0:T(8,128)(2,1)} %get-tuple-element.31), channel_id=1, source_target_pairs={{0,6},{1,7},{2,4},{3,5},{4,2},{5,3},{6,0},{7,1},{8,14},{9,15},{10,... | collective-permute-start | bytes 196616 | tf_op jit(solution)/shard_map/ppermute | solution.py:233
  79.4 13.4 %collective-permute-start.6 = (bf16[1,256,128]{2,1,0:T(8,128)(2,1)}, bf16[1,256,128]{2,1,0:T(8,128)(2,1)S(1)}, u32[]{:S(2)}, u32[]{:S(2)}) collective-permute-start(bf16[1,256,128]{2,1,0:T(8,128)(2,1)} %get-tuple-element.32), channel_id=1, source_target_pairs={{0,7},{1,6},{2,5},{3,4},{4,3},{5,2},{6,1},{7,0},{8,15},{9,14},{10,... | collective-permute-start | bytes 196616 | tf_op jit(solution)/shard_map/ppermute | solution.py:233
  81.2 13.9 %collective-permute-start.7 = (bf16[1,256,128]{2,1,0:T(8,128)(2,1)}, bf16[1,256,128]{2,1,0:T(8,128)(2,1)S(1)}, u32[]{:S(2)}, u32[]{:S(2)}) collective-permute-start(bf16[1,256,128]{2,1,0:T(8,128)(2,1)} %get-tuple-element.33), channel_id=1, source_target_pairs={{0,8},{1,9},{2,10},{3,11},{4,12},{5,13},{6,14},{7,15},{8,0},{9,1},... | collective-permute-start | bytes 196616 | tf_op jit(solution)/shard_map/ppermute | solution.py:233
  83.9 16.7 %collective-permute-start.8 = (bf16[1,256,128]{2,1,0:T(8,128)(2,1)}, bf16[1,256,128]{2,1,0:T(8,128)(2,1)S(1)}, u32[]{:S(2)}, u32[]{:S(2)}) collective-permute-start(bf16[1,256,128]{2,1,0:T(8,128)(2,1)} %get-tuple-element.34), channel_id=1, source_target_pairs={{0,9},{1,8},{2,11},{3,10},{4,13},{5,12},{6,15},{7,14},{8,1},{9,0},... | collective-permute-start | bytes 196616 | tf_op jit(solution)/shard_map/ppermute | solution.py:233
  84.8 17.0 %collective-permute-start.9 = (bf16[1,256,128]{2,1,0:T(8,128)(2,1)S(1)}, bf16[1,256,128]{2,1,0:T(8,128)(2,1)S(1)}, u32[]{:S(2)}, u32[]{:S(2)}) collective-permute-start(bf16[1,256,128]{2,1,0:T(8,128)(2,1)S(1)} %copy-done.16), channel_id=1, source_target_pairs={{0,10},{1,11},{2,8},{3,9},{4,14},{5,15},{6,12},{7,13},{8,2},{9,3},... | collective-permute-start | bytes 196616 | tf_op jit(solution)/shard_map/ppermute | solution.py:233
  90.0 14.2 %collective-permute-start.10 = (bf16[1,256,128]{2,1,0:T(8,128)(2,1)S(1)}, bf16[1,256,128]{2,1,0:T(8,128)(2,1)S(1)}, u32[]{:S(2)}, u32[]{:S(2)}) collective-permute-start(bf16[1,256,128]{2,1,0:T(8,128)(2,1)S(1)} %copy-done.15), channel_id=1, source_target_pairs={{0,11},{1,10},{2,9},{3,8},{4,15},{5,14},{6,13},{7,12},{8,3},{9,2},... | collective-permute-start | bytes 196616 | tf_op jit(solution)/shard_map/ppermute | solution.py:233
  92.8 14.1 %collective-permute-start.11 = (bf16[1,256,128]{2,1,0:T(8,128)(2,1)S(1)}, bf16[1,256,128]{2,1,0:T(8,128)(2,1)S(1)}, u32[]{:S(2)}, u32[]{:S(2)}) collective-permute-start(bf16[1,256,128]{2,1,0:T(8,128)(2,1)S(1)} %copy-done.14), channel_id=1, source_target_pairs={{0,12},{1,13},{2,14},{3,15},{4,8},{5,9},{6,10},{7,11},{8,4},{9,5},... | collective-permute-start | bytes 196616 | tf_op jit(solution)/shard_map/ppermute | solution.py:233
  95.1 16.9 %collective-permute-start.12 = (bf16[1,256,128]{2,1,0:T(8,128)(2,1)S(1)}, bf16[1,256,128]{2,1,0:T(8,128)(2,1)S(1)}, u32[]{:S(2)}, u32[]{:S(2)}) collective-permute-start(bf16[1,256,128]{2,1,0:T(8,128)(2,1)S(1)} %copy-done.13), channel_id=1, source_target_pairs={{0,13},{1,12},{2,15},{3,14},{4,9},{5,8},{6,11},{7,10},{8,5},{9,4},... | collective-permute-start | bytes 196616 | tf_op jit(solution)/shard_map/ppermute | solution.py:233
  100.5 12.9 %collective-permute-start.13 = (bf16[1,256,128]{2,1,0:T(8,128)(2,1)S(1)}, bf16[1,256,128]{2,1,0:T(8,128)(2,1)S(1)}, u32[]{:S(2)}, u32[]{:S(2)}) collective-permute-start(bf16[1,256,128]{2,1,0:T(8,128)(2,1)S(1)} %copy-done.12), channel_id=1, source_target_pairs={{0,14},{1,15},{2,12},{3,13},{4,10},{5,11},{6,8},{7,9},{8,6},{9,7},... | collective-permute-start | bytes 196616 | tf_op jit(solution)/shard_map/ppermute | solution.py:233
  101.7 13.4 %collective-permute-start.14 = (bf16[1,256,128]{2,1,0:T(8,128)(2,1)S(1)}, bf16[1,256,128]{2,1,0:T(8,128)(2,1)S(1)}, u32[]{:S(2)}, u32[]{:S(2)}) collective-permute-start(bf16[1,256,128]{2,1,0:T(8,128)(2,1)S(1)} %copy-done.11), channel_id=1, source_target_pairs={{0,15},{1,14},{2,13},{3,12},{4,11},{5,10},{6,9},{7,8},{8,7},{9,6},... | collective-permute-start | bytes 196616 | tf_op jit(solution)/shard_map/ppermute | solution.py:233
  115.1 1.2 copy-start.2
  116.3 1.2 copy-start.4
  117.5 0.8 copy-start.8
  118.4 0.8 copy-start.10
  (2 other events, 1.2 us)

commit v2 on v0

v2 whole, which is shorter than its diff:
```python
import functools
import math

import jax
import jax.numpy as jnp
from jax import lax
from jax.experimental import pallas as pl
from jax.experimental.pallas import tpu as pltpu
from jax.sharding import PartitionSpec as P


HD = 128
TO_LOG2 = HD ** (-0.5) * math.log2(math.e)
NT = (((1,), (1,)), ((), ()))

ANY = pl.BlockSpec(memory_space=pl.ANY)
WHOLE = pl.BlockSpec(memory_space=pltpu.VMEM)
SCALARS = pl.BlockSpec(memory_space=pltpu.SMEM)


def pack_body(slots, n_in, scal_ref, *refs):
    ins, outs = refs[:n_in], refs[n_in:]
    rows = ins[0].shape[0]
    width = outs[0].shape[1]
    for slot, out_ref in zip(slots, outs):
        at = pl.multiple_of((scal_ref[0] ^ slot) * width, HD)
        for place, ref in enumerate(ins):
            out_ref[place * rows : (place + 1) * rows] = ref[:, pl.ds(at, width)]


def pack(scal, arrays, slots, width):
    rows = arrays[0].shape[0]
    block = jax.ShapeDtypeStruct((len(arrays) * rows, width), arrays[0].dtype)
    return pl.pallas_call(
        functools.partial(pack_body, tuple(slots), len(arrays)),
        out_shape=[block] * len(slots),
        in_specs=[SCALARS] + [WHOLE] * len(arrays),
        out_specs=[WHOLE] * len(slots),
        cost_estimate=pl.CostEstimate(
            flops=0, bytes_accessed=4 * len(arrays) * arrays[0].size, transcendentals=0
        ),
    )(scal, *arrays)


def softmax_part(q, keys, values, head):
    cols = slice(head * HD, (head + 1) * HD)
    total = keys.shape[0]
    chunk = min(512, total)
    ones = jnp.ones((chunk, HD), jnp.bfloat16)
    top, acc = None, None
    for at in range(0, total, chunk):
        k = keys[at : at + chunk, cols]
        v = jnp.concatenate([values[at : at + chunk, cols], ones], axis=1)
        s = lax.dot_general(q, k, NT, preferred_element_type=jnp.float32)
        chunk_top = jnp.max(s, axis=1, keepdims=True)
        new_top = chunk_top if top is None else jnp.maximum(top, chunk_top)
        p = jnp.exp2((s - new_top) * TO_LOG2).astype(jnp.bfloat16)
        part = jnp.dot(p, v, preferred_element_type=jnp.float32)
        if top is None:
            acc = part
        else:
            acc = acc * jnp.exp2((top - new_top) * TO_LOG2) + part
        top = new_top
    return top, acc


def main_body(n_q, n_three, n_kv, scal_ref, *refs):
    three, only_q, only_kv = (
        refs[:n_three],
        refs[n_three : n_three + n_q],
        refs[n_three + n_q : n_three + n_q + n_kv],
    )
    rest = refs[n_three + n_q + n_kv :]
    stale_k, stale_v, acc_ref, stat_ref, q_ref, queries, keys, values, low_k, low_v, sems = rest
    rows = three[0].shape[0] // 3
    heads_dev = queries.shape[1] // HD
    patch = (n_three + n_q) * rows
    n_old = keys.shape[0] - (n_three + n_kv) * rows
    start = scal_ref[1]
    edge = pl.multiple_of(jnp.minimum(start // rows, n_old // rows - 1) * rows, rows)

    @pl.when(pl.program_id(0) == 0)
    def _():
        copies = []

        def take(src, dst):
            copies.append(pltpu.make_async_copy(src, dst, sems.at[len(copies)]))
            copies[-1].start()

        for at in range(0, n_old, rows):
            src = pl.multiple_of(jnp.where(at + rows <= start, at, at + patch), rows)
            take(stale_k.at[pl.ds(src, rows)], keys.at[pl.ds(at, rows)])
            take(stale_v.at[pl.ds(src, rows)], values.at[pl.ds(at, rows)])
        take(stale_k.at[pl.ds(edge, rows)], low_k)
        take(stale_v.at[pl.ds(edge, rows)], low_v)
        at = n_old
        for place, ref in enumerate(three):
            take(ref.at[pl.ds(0, rows)], queries.at[pl.ds(place * rows, rows)])
            take(ref.at[pl.ds(rows, rows)], keys.at[pl.ds(at, rows)])
            take(ref.at[pl.ds(2 * rows, rows)], values.at[pl.ds(at, rows)])
            at += rows
        for place, ref in enumerate(only_q):
            take(ref, queries.at[pl.ds((n_three + place) * rows, rows)])
        for ref in only_kv:
            take(ref.at[pl.ds(0, rows)], keys.at[pl.ds(at, rows)])
            take(ref.at[pl.ds(rows, rows)], values.at[pl.ds(at, rows)])
            at += rows
        for copy in copies:
            copy.wait()
        row = lax.broadcasted_iota(jnp.int32, low_k.shape, 0) + edge
        for low, full in ((low_k, keys), (low_v, values)):
            here = full.at[pl.ds(edge, rows)]
            kept = jnp.where(
                row < start, low[...].astype(jnp.float32), here[...].astype(jnp.float32)
            )
            here[...] = kept.astype(jnp.bfloat16)

    step_rows = q_ref.shape[0]
    base = pl.multiple_of(pl.program_id(0) * step_rows, step_rows)
    q_all = queries[pl.ds(base, step_rows), :]
    q_ref[...] = q_all
    block = min(256, step_rows)
    lane = lax.broadcasted_iota(jnp.int32, (block, HD), 1)
    for at in range(0, step_rows, block):
        for head in range(heads_dev):
            cols = slice(head * HD, (head + 1) * HD)
            q = q_all[at : at + block, cols]
            top, acc = softmax_part(q, keys, values, head)
            acc_ref[at : at + block, cols] = acc[:, :HD]
            stat_ref[at : at + block, cols] = jnp.where(lane < HD // 2, top, acc[:, HD:])


def attend_main(scal, three, only_q, only_kv, stale_k, stale_v):
    rows, width = three[0].shape[0] // 3, three[0].shape[1]
    patch = (len(three) + len(only_q)) * rows
    n_old = stale_k.shape[0] - patch
    total = n_old + (len(three) + len(only_kv)) * rows
    step = min(512, patch)
    n_copies = 2 * (n_old // rows) + 2 + 3 * len(three) + len(only_q) + 2 * len(only_kv)
    operands = (*three, *only_q, *only_kv, stale_k, stale_v)
    out = pl.BlockSpec((step, width), lambda i, s: (i, 0))
    return pl.pallas_call(
        functools.partial(main_body, len(only_q), len(three), len(only_kv)),
        out_shape=[
            jax.ShapeDtypeStruct((patch, width), jnp.float32),
            jax.ShapeDtypeStruct((patch, width), jnp.float32),
            jax.ShapeDtypeStruct((patch, width), jnp.bfloat16),
        ],
        grid_spec=pltpu.PrefetchScalarGridSpec(
            num_scalar_prefetch=1,
            grid=(patch // step,),
            in_specs=[ANY] * len(operands),
            out_specs=[out] * 3,
            scratch_shapes=[
                pltpu.VMEM((patch, width), jnp.bfloat16),
                pltpu.VMEM((total, width), jnp.bfloat16),
                pltpu.VMEM((total, width), jnp.bfloat16),
                pltpu.VMEM((rows, width), jnp.bfloat16),
                pltpu.VMEM((rows, width), jnp.bfloat16),
                pltpu.SemaphoreType.DMA((n_copies,)),
            ],
        ),
        cost_estimate=pl.CostEstimate(
            flops=6 * patch * total * width,
            bytes_accessed=2 * width * (6 * patch + 2 * total),
            transcendentals=patch * total * (width // HD),
        ),
    )(scal, *operands)


def last_body(n_kv, n_slots, scal_ref, *refs):
    kv_refs = refs[:n_kv]
    acc_ref, stat_ref, q_ref, gate_ref = refs[n_kv : n_kv + 4]
    out_refs = refs[n_kv + 4 : n_kv + 4 + n_slots]
    keys, values, sems = refs[n_kv + 4 + n_slots :]
    rows = out_refs[0].shape[0]
    heads_dev = q_ref.shape[1] // HD
    step_id = pl.program_id(0)

    @pl.when(step_id == 0)
    def _():
        copies = []
        for place, ref in enumerate(kv_refs):
            for half, full in enumerate((keys, values)):
                src = ref.at[pl.ds(half * rows, rows)]
                dst = full.at[pl.ds(place * rows, rows)]
                copies.append(pltpu.make_async_copy(src, dst, sems.at[len(copies)]))
                copies[-1].start()
        for copy in copies:
            copy.wait()

    gate = gate_ref[pl.ds(scal_ref[2], 1), :]
    step_rows = q_ref.shape[0]
    per = step_rows // rows
    block = min(256, step_rows)
    pieces = []
    for at in range(0, step_rows, block):
        heads = []
        for head in range(heads_dev):
            cols = slice(head * HD, (head + 1) * HD)
            here = slice(at, at + block)
            top, acc = softmax_part(q_ref[here, cols], keys, values, head)
            old_top = stat_ref[here, head * HD : head * HD + 1]
            old_sum = stat_ref[here, (head + 1) * HD - 1 : (head + 1) * HD]
            new_top = jnp.maximum(top, old_top)
            scale = jnp.exp2((top - new_top) * TO_LOG2)
            old_scale = jnp.exp2((old_top - new_top) * TO_LOG2)
            numer = acc[:, :HD] * scale + acc_ref[here, cols] * old_scale
            denom = acc[:, HD:] * scale + old_sum * old_scale
            attn = (numer / denom).astype(jnp.bfloat16)
            heads.append((attn.astype(jnp.float32) * gate[:, cols]).astype(jnp.bfloat16))
        gated = jnp.concatenate(heads, axis=1)
        pieces += [gated[i : i + rows] for i in range(0, block, rows)]
    for turn in range(n_slots // per):

        @pl.when(step_id == turn)
        def _():
            for place in range(per):
                out_refs[turn * per + place][...] = pieces[place]


def attend_last(scal, only_kv, acc, stat, queries, gate_table):
    rows, width = only_kv[0].shape[0] // 2, only_kv[0].shape[1]
    patch = queries.shape[0]
    total = len(only_kv) * rows
    step = min(512, patch)
    n_slots = patch // rows
    state = pl.BlockSpec((step, width), lambda i, s: (i, 0))
    gate = pl.BlockSpec((gate_table.shape[0], width), lambda i, s: (0, s[0]))
    piece = jax.ShapeDtypeStruct((rows, width), jnp.bfloat16)
    return pl.pallas_call(
        functools.partial(last_body, len(only_kv), n_slots),
        out_shape=[piece] * n_slots,
        grid_spec=pltpu.PrefetchScalarGridSpec(
            num_scalar_prefetch=1,
            grid=(patch // step,),
            in_specs=[ANY] * len(only_kv) + [state, state, state, gate],
            out_specs=[pl.BlockSpec((rows, width), lambda i, s: (0, 0))] * n_slots,
            scratch_shapes=[
                pltpu.VMEM((total, width), jnp.bfloat16),
                pltpu.VMEM((total, width), jnp.bfloat16),
                pltpu.SemaphoreType.DMA((2 * len(only_kv),)),
            ],
        ),
        cost_estimate=pl.CostEstimate(
            flops=6 * patch * total * width,
            bytes_accessed=2 * width * (6 * patch + 2 * total),
            transcendentals=patch * total * (width // HD),
        ),
    )(scal, *only_kv, acc, stat, queries, gate_table)


def unpack_body(scal_ref, *refs):
    out_ref = refs[-1]
    width = refs[0].shape[1]
    for slot, ref in enumerate(refs[:-1]):
        at = pl.multiple_of((scal_ref[0] ^ slot) * width, HD)
        out_ref[:, pl.ds(at, width)] = ref[...]


def unpack(scal, parts):
    rows, width = parts[0].shape
    return pl.pallas_call(
        unpack_body,
        out_shape=jax.ShapeDtypeStruct((rows, len(parts) * width), parts[0].dtype),
        in_specs=[SCALARS] + [WHOLE] * len(parts),
        out_specs=WHOLE,
    )(scal, *parts)


def shards(
    fresh_query, fresh_key, fresh_value, stale_key, stale_value, patch_start, timestep, gate_table
):
    n = lax.axis_size("seq")
    width = stale_key.shape[1]
    me = lax.axis_index("seq").astype(jnp.int32)
    near, far = range(n // 2), range(n // 2, n)

    def send(slot, block):
        return lax.ppermute(block, "seq", [(i, i ^ slot) for i in range(n)])

    def send_all(slots, blocks):
        return [b if s == 0 else send(s, b) for s, b in zip(slots, blocks)]

    scal = jnp.stack([me, patch_start[0], timestep[0]])
    q_blocks = pack(me[None], (fresh_query,), far, width)
    far_q = send_all(far, q_blocks)
    kv_blocks = pack(me[None], (fresh_key, fresh_value), far, width)
    far_kv = send_all(far, kv_blocks)
    near_blocks = pack(me[None], (fresh_query, fresh_key, fresh_value), near, width)
    three = send_all(near, near_blocks)
    early = len(far) // 2
    acc, stat, queries = attend_main(scal, three, far_q, far_kv[:early], stale_key, stale_value)
    outs = attend_last(scal, far_kv[early:], acc, stat, queries, gate_table)
    home_far = send_all(far, outs[n // 2 :])
    home_near = send_all(near, outs[: n // 2])
    return unpack(me[None], [*home_near, *home_far])


def solution(mesh):
    return jax.shard_map(
        shards,
        mesh=mesh,
        in_specs=(
            P(("grp", "seq"), None),
            P(("grp", "seq"), None),
            P(("grp", "seq"), None),
            P("grp", "seq"),
            P("grp", "seq"),
            P("grp"),
            P("grp"),
            P(),
        ),
        out_specs=P(("grp", "seq"), None),
        check_vma=False,
    )
```

time: 212 us -> 154 us (0.73)
  matrix products: 46.4 us -> 0 us
  Pallas kernels: 0 us -> 45.3 us
  starting transfers between devices: 20.9 us -> 65.4 us
  other arithmetic: 45.1 us -> 0.61 us
  waiting for transfers between devices: 71.2 us -> 38.7 us
  local copies, waits for them, and re-layouts: 25.2 us -> 1.91 us
    all_to_all x4 -> x0, waiting for transfers between devices: 71.2 us -> none  [the longest x1 24.2 us: shards(): lax.all_to_all(heads_out, 'seq', split_axis=0, concat_axis=1, tiled=True)]
    ppermute x0 -> x38, starting transfers between devices: none -> 65.4 us  [send(): return lax.ppermute(block, 'seq', [(i, i ^ slot) for i in range(n)])]
    dot_general x32 -> x0, matrix products: 46.4 us -> none  [the longest x16 24.3 us: attend_group(): jnp.dot(queries, keys.T, preferred_element_type=jnp.float32) * HD ** (-0.5)]
    pallas_call x0 -> x6, Pallas kernels: none -> 45.3 us  [the longest x1 22.7 us: attend_main(): pl.pallas_call(functools.partial(main_body, len(only_q), len(three), len(...]
    ppermute x0 -> x38, waiting for transfers between devices: none -> 38.7 us  [send(): return lax.ppermute(block, 'seq', [(i, i ^ slot) for i in range(n)])]
    convert_element_type x4 -> x0, other arithmetic: 23.8 us -> none  [the longest x2 20.5 us: shards(): outputs.append((numer / denom[:, None]).astype(jnp.bfloat16))]
    all_to_all x4 -> x0, starting transfers between devices: 20.9 us -> none  [the longest x1 6.58 us: shards(): lax.all_to_all(query_heads, 'seq', split_axis=1, concat_axis=0, tiled=True)]
    reduce_sum x16 -> x0, other arithmetic: 13 us -> none  [attend_group(): total = jnp.sum(expo, axis=1)]
  transfers between devices with their start and end apart: 4 -> 38, of which waited for: 4 -> 18; matrix products, arithmetic and copies ran while one was open for 12% -> 0% of each run, Pallas kernels for 0% -> 19%
where the time goes in v2:
time: 154 us
  starting transfers between devices  65.4 us (42%)
  Pallas kernels  45.3 us (29%)
  waiting for transfers between devices  38.7 us (25%)
  local copies, waits for them, and re-layouts  1.91 us (1%)
  between operations  1.76 us (1%)
    ppermute x38, starting transfers between devices, send(): return lax.ppermute(block, 'seq', [(i, i ^ slot) for i in range(n)])  65.4 us
    ppermute x38, waiting for transfers between devices, send(): return lax.ppermute(block, 'seq', [(i, i ^ slot) for i in range(n)])  38.7 us
    pallas_call x1, Pallas kernels, attend_main(): pl.pallas_call(functools.partial(main_body, len(only_q), len(three), len(...  22.7 us
    pallas_call x1, Pallas kernels, attend_last(): pl.pallas_call(functools.partial(last_body, len(only_kv), n_slots), out_s...  12.3 us
    pallas_call x3, Pallas kernels, pack(): pl.pallas_call(functools.partial(pack_body, tuple(slots), len(arrays)), o...  7.92 us
  transfers between devices with their start and end apart: 38, of which 18 were waited for; matrix products, arithmetic and copies ran while one was open for 0% of the time, Pallas kernels for 19%

profile of v2, /device:TPU:11, one launch (start us, length us, event | category | flops | bytes accessed | tf_op | source)
XLA Modules:
  0.0 153.6 jit_solution(5115501526011978914)
XLA Ops:
  0.0 2.1 %shard_map.84 = (bf16[128,256]{1,0:T(8,128)(2,1)}, bf16[128,256]{1,0:T(8,128)(2,1)}, bf16[128,256]{1,0:T(8,128)(2,1)}, bf16[128,256]{1,0:T(8,128)(2,1)}, bf16[12...) custom-call(s32[1]{0:T(128)} %bitcast.scal_ref, ...), custom_call_target="tpu_custom_call" | custom-call | bytes 2097152 | tf_op jit(solution)/shard_map/pallas_call | solution.py:34
  2.1 2.4 %collective-permute-start.11 = (bf16[128,256]{1,0:T(8,128)(2,1)}, bf16[128,256]{1,0:T(8,128)(2,1)S(1)}, u32[]{:S(2)}, u32[]{:S(2)}) collective-permute-start(bf16[128,256]{1,0:T(8,128)(2,1)} %get-tuple-element.60), channel_id=1, source_target_pairs={{0,8},{1,9},{2,10},{3,11},{4,12},{5,13},{6,14},{7,15},{8,0},{9,1},... | collective-permute-start | bytes 196616 | tf_op jit(solution)/shard_map/ppermute | solution.py:280
  5.4 3.3 %collective-permute-start.13 = (bf16[128,256]{1,0:T(8,128)(2,1)}, bf16[128,256]{1,0:T(8,128)(2,1)S(1)}, u32[]{:S(2)}, u32[]{:S(2)}) collective-permute-start(bf16[128,256]{1,0:T(8,128)(2,1)} %get-tuple-element.62), channel_id=1, source_target_pairs={{0,10},{1,11},{2,8},{3,9},{4,14},{5,15},{6,12},{7,13},{8,2},{9,3},... | collective-permute-start | bytes 196616 | tf_op jit(solution)/shard_map/ppermute | solution.py:280
  8.8 2.7 %shard_map.82 = (bf16[256,256]{1,0:T(8,128)(2,1)}, bf16[256,256]{1,0:T(8,128)(2,1)}, bf16[256,256]{1,0:T(8,128)(2,1)}, bf16[256,256]{1,0:T(8,128)(2,1)}, bf16[25...) custom-call(s32[1]{0:T(128)} %bitcast.scal_ref, ...), custom_call_target="tpu_custom_call" | custom-call | bytes 4194304 | tf_op jit(solution)/shard_map/pallas_call | solution.py:34
  11.6 1.9 %collective-permute-start.19 = (bf16[256,256]{1,0:T(8,128)(2,1)}, bf16[256,256]{1,0:T(8,128)(2,1)S(1)}, u32[]{:S(2)}, u32[]{:S(2)}) collective-permute-start(bf16[256,256]{1,0:T(8,128)(2,1)} %get-tuple-element.68), channel_id=1, source_target_pairs={{0,8},{1,9},{2,10},{3,11},{4,12},{5,13},{6,14},{7,15},{8,0},{9,1},... | collective-permute-start | bytes 393224 | tf_op jit(solution)/shard_map/ppermute | solution.py:280
  13.6 2.6 %collective-permute-start.16 = (bf16[128,256]{1,0:T(8,128)(2,1)S(1)}, bf16[128,256]{1,0:T(8,128)(2,1)S(1)}, u32[]{:S(2)}, u32[]{:S(2)}) collective-permute-start(bf16[128,256]{1,0:T(8,128)(2,1)S(1)} %copy-done.47), channel_id=1, source_target_pairs={{0,13},{1,12},{2,15},{3,14},{4,9},{5,8},{6,11},{7,10},{8,5},{9,4},... | collective-permute-start | bytes 196616 | tf_op jit(solution)/shard_map/ppermute | solution.py:280
  16.2 4.1 %collective-permute-done.13.refs_10_ = bf16[128,256]{1,0:T(8,128)(2,1)S(1)} collective-permute-done((bf16[128,256]{1,0:T(8,128)(2,1)}, bf16[128,256]{1,0:T(8,128)(2,1)S(1)}, u32[]{:S(2)}, u32[]{:S(2)}) %collective-permute-start.13) | collective-permute-done | bytes 65568 | tf_op jit(solution)/shard_map/ppermute | solution.py:280
  21.8 2.0 %collective-permute-start.18 = (bf16[128,256]{1,0:T(8,128)(2,1)S(1)}, bf16[128,256]{1,0:T(8,128)(2,1)S(1)}, u32[]{:S(2)}, u32[]{:S(2)}) collective-permute-start(bf16[128,256]{1,0:T(8,128)(2,1)S(1)} %copy-done.45), channel_id=1, source_target_pairs={{0,15},{1,14},{2,13},{3,12},{4,11},{5,10},{6,9},{7,8},{8,7},{9,6},... | collective-permute-start | bytes 196616 | tf_op jit(solution)/shard_map/ppermute | solution.py:280
  23.8 3.2 %shard_map.83 = (bf16[384,256]{1,0:T(8,128)(2,1)}, bf16[384,256]{1,0:T(8,128)(2,1)}, bf16[384,256]{1,0:T(8,128)(2,1)}, bf16[384,256]{1,0:T(8,128)(2,1)}, bf16[38...) custom-call(s32[1]{0:T(128)} %bitcast.scal_ref, ...), custom_call_target="tpu_custom_call" | custom-call | bytes 6291456 | tf_op jit(solution)/shard_map/pallas_call | solution.py:34
  28.1 2.0 %collective-permute-done.16.refs_13_ = bf16[128,256]{1,0:T(8,128)(2,1)S(1)} collective-permute-done((bf16[128,256]{1,0:T(8,128)(2,1)S(1)}, bf16[128,256]{1,0:T(8,128)(2,1)S(1)}, u32[]{:S(2)}, u32[]{:S(2)}) %collective-permute-start.16) | collective-permute-done | bytes 65568 | tf_op jit(solution)/shard_map/ppermute | solution.py:280
  35.6 2.7 %collective-permute-start.22 = (bf16[256,256]{1,0:T(8,128)(2,1)S(1)}, bf16[256,256]{1,0:T(8,128)(2,1)S(1)}, u32[]{:S(2)}, u32[]{:S(2)}) collective-permute-start(bf16[256,256]{1,0:T(8,128)(2,1)S(1)} %copy-done.33), channel_id=1, source_target_pairs={{0,11},{1,10},{2,9},{3,8},{4,15},{5,14},{6,13},{7,12},{8,3},{9,2},... | collective-permute-start | bytes 393224 | tf_op jit(solution)/shard_map/ppermute | solution.py:280
  38.3 7.2 %collective-permute-done.20.refs_17_ = bf16[256,256]{1,0:T(8,128)(2,1)S(1)} collective-permute-done((bf16[256,256]{1,0:T(8,128)(2,1)S(1)}, bf16[256,256]{1,0:T(8,128)(2,1)S(1)}, u32[]{:S(2)}, u32[]{:S(2)}) %collective-permute-start.20) | collective-permute-done | bytes 131104 | tf_op jit(solution)/shard_map/ppermute | solution.py:280
  48.3 1.8 %collective-permute-start.7 = (bf16[384,256]{1,0:T(8,128)(2,1)}, bf16[384,256]{1,0:T(8,128)(2,1)S(1)}, u32[]{:S(2)}, u32[]{:S(2)}) collective-permute-start(bf16[384,256]{1,0:T(8,128)(2,1)} %get-tuple-element.56), channel_id=1, source_target_pairs={{0,4},{1,5},{2,6},{3,7},{4,0},{5,1},{6,2},{7,3},{8,12},{9,13},{10,... | collective-permute-start | bytes 589832 | tf_op jit(solution)/shard_map/ppermute | solution.py:280
  51.1 2.2 %collective-permute-start.8 = (bf16[384,256]{1,0:T(8,128)(2,1)}, bf16[384,256]{1,0:T(8,128)(2,1)S(1)}, u32[]{:S(2)}, u32[]{:S(2)}) collective-permute-start(bf16[384,256]{1,0:T(8,128)(2,1)} %get-tuple-element.57), channel_id=1, source_target_pairs={{0,5},{1,4},{2,7},{3,6},{4,1},{5,0},{6,3},{7,2},{8,13},{9,12},{10,... | collective-permute-start | bytes 589832 | tf_op jit(solution)/shard_map/ppermute | solution.py:280
  58.6 1.8 %collective-permute-start = (bf16[256,256]{1,0:T(8,128)(2,1)S(1)}, bf16[256,256]{1,0:T(8,128)(2,1)S(1)}, u32[]{:S(2)}, u32[]{:S(2)}) collective-permute-start(bf16[256,256]{1,0:T(8,128)(2,1)S(1)} %copy-done.29), channel_id=1, source_target_pairs={{0,12},{1,13},{2,14},{3,15},{4,8},{5,9},{6,10},{7,11},{8,4},{9,5},... | collective-permute-start | bytes 393224 | tf_op jit(solution)/shard_map/ppermute | solution.py:280
  60.9 1.9 %collective-permute-start.2 = (bf16[256,256]{1,0:T(8,128)(2,1)S(1)}, bf16[256,256]{1,0:T(8,128)(2,1)S(1)}, u32[]{:S(2)}, u32[]{:S(2)}) collective-permute-start(bf16[256,256]{1,0:T(8,128)(2,1)S(1)} %copy-done.27), channel_id=1, source_target_pairs={{0,14},{1,15},{2,12},{3,13},{4,10},{5,11},{6,8},{7,9},{8,6},{9,7},... | collective-permute-start | bytes 393224 | tf_op jit(solution)/shard_map/ppermute | solution.py:280
  62.8 2.2 %collective-permute-done.9.refs_6_ = bf16[384,256]{1,0:T(8,128)(2,1)S(1)} collective-permute-done((bf16[384,256]{1,0:T(8,128)(2,1)}, bf16[384,256]{1,0:T(8,128)(2,1)S(1)}, u32[]{:S(2)}, u32[]{:S(2)}) %collective-permute-start.9) | collective-permute-done | bytes 196640 | tf_op jit(solution)/shard_map/ppermute | solution.py:280
  65.0 3.6 %collective-permute-start.3 = (bf16[256,256]{1,0:T(8,128)(2,1)S(1)}, bf16[256,256]{1,0:T(8,128)(2,1)S(1)}, u32[]{:S(2)}, u32[]{:S(2)}) collective-permute-start(bf16[256,256]{1,0:T(8,128)(2,1)S(1)} %copy-done.26), channel_id=1, source_target_pairs={{0,15},{1,14},{2,13},{3,12},{4,11},{5,10},{6,9},{7,8},{8,7},{9,6},... | collective-permute-start | bytes 393224 | tf_op jit(solution)/shard_map/ppermute | solution.py:280
  68.6 3.0 %collective-permute-done.10.refs_7_ = bf16[384,256]{1,0:T(8,128)(2,1)S(1)} collective-permute-done((bf16[384,256]{1,0:T(8,128)(2,1)}, bf16[384,256]{1,0:T(8,128)(2,1)S(1)}, u32[]{:S(2)}, u32[]{:S(2)}) %collective-permute-start.10) | collective-permute-done | bytes 196640 | tf_op jit(solution)/shard_map/ppermute | solution.py:280
  72.2 22.7 %shard_map.85 = (f32[2048,256]{1,0:T(8,128)}, f32[2048,256]{1,0:T(8,128)}, bf16[2048,256]{1,0:T(8,128)(2,1)}) custom-call(s32[3]{0:T(128)} %pad_add_fusion.scal_ref, bf16[384,256]{1,0:T(8,128)(2,1)} %get-tuple-element.52.refs_0_, bf16[384,256]{1,0:T(8,128)(2,1)} %copy-done.19, bf16[384,256]{1,0:T(8,128)(2,1)} %copy-done.20, bf16[384,256]{1,0:T(8,128)(2,1)} %copy-done.21, ...), custom_call_target="tpu_custom_call" | custom-call | flops 11274289152 | bytes 9961472 | tf_op jit(solution)/shard_map/pallas_call | solution.py:142
  95.7 12.3 %shard_map.86 = (bf16[128,256]{1,0:T(8,128)(2,1)}, bf16[128,256]{1,0:T(8,128)(2,1)}, bf16[128,256]{1,0:T(8,128)(2,1)}, bf16[128,256]{1,0:T(8,128)(2,1)}, bf16[12...) custom-call(s32[3]{0:T(128)} %pad_add_fusion.scal_ref, ...), custom_call_target="tpu_custom_call" | custom-call | flops 1610612736 | bytes 6815744 | tf_op jit(solution)/shard_map/pallas_call | solution.py:231
  108.3 2.0 %collective-permute-start.25 = (bf16[128,256]{1,0:T(8,128)(2,1)}, bf16[128,256]{1,0:T(8,128)(2,1)S(1)}, u32[]{:S(2)}, u32[]{:S(2)}) collective-permute-start(bf16[128,256]{1,0:T(8,128)(2,1)} %get-tuple-element.78), channel_id=1, source_target_pairs={{0,3},{1,2},{2,1},{3,0},{4,7},{5,6},{6,5},{7,4},{8,11},{9,10},{10,... | collective-permute-start | bytes 196616 | tf_op jit(solution)/shard_map/ppermute | solution.py:280
  111.7 2.9 %collective-permute-start.29 = (bf16[128,256]{1,0:T(8,128)(2,1)}, bf16[128,256]{1,0:T(8,128)(2,1)S(1)}, u32[]{:S(2)}, u32[]{:S(2)}) collective-permute-start(bf16[128,256]{1,0:T(8,128)(2,1)} %get-tuple-element.82), channel_id=1, source_target_pairs={{0,7},{1,6},{2,5},{3,4},{4,3},{5,2},{6,1},{7,0},{8,15},{9,14},{10,... | collective-permute-start | bytes 196616 | tf_op jit(solution)/shard_map/ppermute | solution.py:280
  114.7 11.1 %collective-permute-start.30 = (bf16[128,256]{1,0:T(8,128)(2,1)}, bf16[128,256]{1,0:T(8,128)(2,1)S(1)}, u32[]{:S(2)}, u32[]{:S(2)}) collective-permute-start(bf16[128,256]{1,0:T(8,128)(2,1)} %get-tuple-element.83), channel_id=1, source_target_pairs={{0,8},{1,9},{2,10},{3,11},{4,12},{5,13},{6,14},{7,15},{8,0},{9,1},... | collective-permute-start | bytes 196616 | tf_op jit(solution)/shard_map/ppermute | solution.py:280
  126.6 2.9 %collective-permute-start.32 = (bf16[128,256]{1,0:T(8,128)(2,1)}, bf16[128,256]{1,0:T(8,128)(2,1)S(1)}, u32[]{:S(2)}, u32[]{:S(2)}) collective-permute-start(bf16[128,256]{1,0:T(8,128)(2,1)} %get-tuple-element.85), channel_id=1, source_target_pairs={{0,10},{1,11},{2,8},{3,9},{4,14},{5,15},{6,12},{7,13},{8,2},{9,3},... | collective-permute-start | bytes 196616 | tf_op jit(solution)/shard_map/ppermute | solution.py:280
  130.1 2.4 %collective-permute-start.34 = (bf16[128,256]{1,0:T(8,128)(2,1)}, bf16[128,256]{1,0:T(8,128)(2,1)S(1)}, u32[]{:S(2)}, u32[]{:S(2)}) collective-permute-start(bf16[128,256]{1,0:T(8,128)(2,1)} %get-tuple-element.87), channel_id=1, source_target_pairs={{0,12},{1,13},{2,14},{3,15},{4,8},{5,9},{6,10},{7,11},{8,4},{9,5},... | collective-permute-start | bytes 196616 | tf_op jit(solution)/shard_map/ppermute | solution.py:280
  132.5 3.1 %collective-permute-done.31.refs_9_ = bf16[128,256]{1,0:T(8,128)(2,1)S(1)} collective-permute-done((bf16[128,256]{1,0:T(8,128)(2,1)}, bf16[128,256]{1,0:T(8,128)(2,1)S(1)}, u32[]{:S(2)}, u32[]{:S(2)}) %collective-permute-start.31) | collective-permute-done | bytes 65568 | tf_op jit(solution)/shard_map/ppermute | solution.py:280
  137.8 3.2 %collective-permute-start.37 = (bf16[128,256]{1,0:T(8,128)(2,1)}, bf16[128,256]{1,0:T(8,128)(2,1)S(1)}, u32[]{:S(2)}, u32[]{:S(2)}) collective-permute-start(bf16[128,256]{1,0:T(8,128)(2,1)} %get-tuple-element.90), channel_id=1, source_target_pairs={{0,15},{1,14},{2,13},{3,12},{4,11},{5,10},{6,9},{7,8},{8,7},{9,6},... | collective-permute-start | bytes 196616 | tf_op jit(solution)/shard_map/ppermute | solution.py:280
  141.0 1.8 %collective-permute-done.34.refs_12_ = bf16[128,256]{1,0:T(8,128)(2,1)S(1)} collective-permute-done((bf16[128,256]{1,0:T(8,128)(2,1)}, bf16[128,256]{1,0:T(8,128)(2,1)S(1)}, u32[]{:S(2)}, u32[]{:S(2)}) %collective-permute-start.34) | collective-permute-done | bytes 65568 | tf_op jit(solution)/shard_map/ppermute | solution.py:280
  142.8 2.8 %collective-permute-done.35.refs_13_ = bf16[128,256]{1,0:T(8,128)(2,1)S(1)} collective-permute-done((bf16[128,256]{1,0:T(8,128)(2,1)}, bf16[128,256]{1,0:T(8,128)(2,1)S(1)}, u32[]{:S(2)}, u32[]{:S(2)}) %collective-permute-start.35) | collective-permute-done | bytes 65568 | tf_op jit(solution)/shard_map/ppermute | solution.py:280
  145.7 3.7 %collective-permute-done.36.refs_14_ = bf16[128,256]{1,0:T(8,128)(2,1)S(1)} collective-permute-done((bf16[128,256]{1,0:T(8,128)(2,1)}, bf16[128,256]{1,0:T(8,128)(2,1)S(1)}, u32[]{:S(2)}, u32[]{:S(2)}) %collective-permute-start.36) | collective-permute-done | bytes 65568 | tf_op jit(solution)/shard_map/ppermute | solution.py:280
  151.3 2.3 %shard_map.87 = bf16[128,4096]{1,0:T(8,128)(2,1)} custom-call(s32[1]{0:T(128)} %bitcast.scal_ref, bf16[128,256]{1,0:T(8,128)(2,1)} %get-tuple-element.75.refs_0_, bf16[128,256]{1,0:T(8,128)(2,1)} %copy-done.4, bf16[128,256]{1,0:T(8,128)(2,1)} %copy-done.5, bf16[128,256]{1,0:T(8,128)(2,1)} %copy-done.6, bf16[128,256]{1,0:T(8,128)(2,1)} %copy-done.7, ...), custom_call_target="tpu_custom_call" | custom-call | tf_op jit(solution)/shard_map/pallas_call | solution.py:263
  (149 shorter events, 26.1 us)
Async XLA Ops:
  2.1 11.4 %collective-permute-start.11 = (bf16[128,256]{1,0:T(8,128)(2,1)}, bf16[128,256]{1,0:T(8,128)(2,1)S(1)}, u32[]{:S(2)}, u32[]{:S(2)}) collective-permute-start(bf16[128,256]{1,0:T(8,128)(2,1)} %get-tuple-element.60), channel_id=1, source_target_pairs={{0,8},{1,9},{2,10},{3,11},{4,12},{5,13},{6,14},{7,15},{8,0},{9,1},... | collective-permute-start | bytes 196616 | tf_op jit(solution)/shard_map/ppermute | solution.py:280
  5.4 14.9 %collective-permute-start.13 = (bf16[128,256]{1,0:T(8,128)(2,1)}, bf16[128,256]{1,0:T(8,128)(2,1)S(1)}, u32[]{:S(2)}, u32[]{:S(2)}) collective-permute-start(bf16[128,256]{1,0:T(8,128)(2,1)} %get-tuple-element.62), channel_id=1, source_target_pairs={{0,10},{1,11},{2,8},{3,9},{4,14},{5,15},{6,12},{7,13},{8,2},{9,3},... | collective-permute-start | bytes 196616 | tf_op jit(solution)/shard_map/ppermute | solution.py:280
  8.6 13.2 %collective-permute-start.14 = (bf16[128,256]{1,0:T(8,128)(2,1)}, bf16[128,256]{1,0:T(8,128)(2,1)S(1)}, u32[]{:S(2)}, u32[]{:S(2)}) collective-permute-start(bf16[128,256]{1,0:T(8,128)(2,1)} %get-tuple-element.63), channel_id=1, source_target_pairs={{0,11},{1,10},{2,9},{3,8},{4,15},{5,14},{6,13},{7,12},{8,3},{9,2},... | collective-permute-start | bytes 196616 | tf_op jit(solution)/shard_map/ppermute | solution.py:280
  11.6 24.0 %collective-permute-start.19 = (bf16[256,256]{1,0:T(8,128)(2,1)}, bf16[256,256]{1,0:T(8,128)(2,1)S(1)}, u32[]{:S(2)}, u32[]{:S(2)}) collective-permute-start(bf16[256,256]{1,0:T(8,128)(2,1)} %get-tuple-element.68), channel_id=1, source_target_pairs={{0,8},{1,9},{2,10},{3,11},{4,12},{5,13},{6,14},{7,15},{8,0},{9,1},... | collective-permute-start | bytes 393224 | tf_op jit(solution)/shard_map/ppermute | solution.py:280
  13.4 14.3 %collective-permute-start.15 = (bf16[128,256]{1,0:T(8,128)(2,1)S(1)}, bf16[128,256]{1,0:T(8,128)(2,1)S(1)}, u32[]{:S(2)}, u32[]{:S(2)}) collective-permute-start(bf16[128,256]{1,0:T(8,128)(2,1)S(1)} %copy-done.48), channel_id=1, source_target_pairs={{0,12},{1,13},{2,14},{3,15},{4,8},{5,9},{6,10},{7,11},{8,4},{9,5},... | collective-permute-start | bytes 196616 | tf_op jit(solution)/shard_map/ppermute | solution.py:280
  13.6 16.6 %collective-permute-start.16 = (bf16[128,256]{1,0:T(8,128)(2,1)S(1)}, bf16[128,256]{1,0:T(8,128)(2,1)S(1)}, u32[]{:S(2)}, u32[]{:S(2)}) collective-permute-start(bf16[128,256]{1,0:T(8,128)(2,1)S(1)} %copy-done.47), channel_id=1, source_target_pairs={{0,13},{1,12},{2,15},{3,14},{4,9},{5,8},{6,11},{7,10},{8,5},{9,4},... | collective-permute-start | bytes 196616 | tf_op jit(solution)/shard_map/ppermute | solution.py:280
  20.3 12.6 %collective-permute-start.17 = (bf16[128,256]{1,0:T(8,128)(2,1)S(1)}, bf16[128,256]{1,0:T(8,128)(2,1)S(1)}, u32[]{:S(2)}, u32[]{:S(2)}) collective-permute-start(bf16[128,256]{1,0:T(8,128)(2,1)S(1)} %copy-done.46), channel_id=1, source_target_pairs={{0,14},{1,15},{2,12},{3,13},{4,10},{5,11},{6,8},{7,9},{8,6},{9,7},... | collective-permute-start | bytes 196616 | tf_op jit(solution)/shard_map/ppermute | solution.py:280
  21.8 12.4 %collective-permute-start.18 = (bf16[128,256]{1,0:T(8,128)(2,1)S(1)}, bf16[128,256]{1,0:T(8,128)(2,1)S(1)}, u32[]{:S(2)}, u32[]{:S(2)}) collective-permute-start(bf16[128,256]{1,0:T(8,128)(2,1)S(1)} %copy-done.45), channel_id=1, source_target_pairs={{0,15},{1,14},{2,13},{3,12},{4,11},{5,10},{6,9},{7,8},{8,7},{9,6},... | collective-permute-start | bytes 196616 | tf_op jit(solution)/shard_map/ppermute | solution.py:280
  27.7 25.7 %collective-permute-start.4 = (bf16[384,256]{1,0:T(8,128)(2,1)}, bf16[384,256]{1,0:T(8,128)(2,1)S(1)}, u32[]{:S(2)}, u32[]{:S(2)}) collective-permute-start(bf16[384,256]{1,0:T(8,128)(2,1)} %get-tuple-element.53), channel_id=1, source_target_pairs={{0,1},{1,0},{2,3},{3,2},{4,5},{5,4},{6,7},{7,6},{8,9},{9,8},{10,11... | collective-permute-start | bytes 589832 | tf_op jit(solution)/shard_map/ppermute | solution.py:280
  30.1 25.0 %collective-permute-start.5 = (bf16[384,256]{1,0:T(8,128)(2,1)}, bf16[384,256]{1,0:T(8,128)(2,1)S(1)}, u32[]{:S(2)}, u32[]{:S(2)}) collective-permute-start(bf16[384,256]{1,0:T(8,128)(2,1)} %get-tuple-element.54), channel_id=1, source_target_pairs={{0,2},{1,3},{2,0},{3,1},{4,6},{5,7},{6,4},{7,5},{8,10},{9,11},{10,... | collective-permute-start | bytes 589832 | tf_op jit(solution)/shard_map/ppermute | solution.py:280
  32.9 12.7 %collective-permute-start.20 = (bf16[256,256]{1,0:T(8,128)(2,1)S(1)}, bf16[256,256]{1,0:T(8,128)(2,1)S(1)}, u32[]{:S(2)}, u32[]{:S(2)}) collective-permute-start(bf16[256,256]{1,0:T(8,128)(2,1)S(1)} %copy-done.36), channel_id=1, source_target_pairs={{0,9},{1,8},{2,11},{3,10},{4,13},{5,12},{6,15},{7,14},{8,1},{9,0},... | collective-permute-start | bytes 393224 | tf_op jit(solution)/shard_map/ppermute | solution.py:280
  34.3 14.1 %collective-permute-start.21 = (bf16[256,256]{1,0:T(8,128)(2,1)S(1)}, bf16[256,256]{1,0:T(8,128)(2,1)S(1)}, u32[]{:S(2)}, u32[]{:S(2)}) collective-permute-start(bf16[256,256]{1,0:T(8,128)(2,1)S(1)} %copy-done.35), channel_id=1, source_target_pairs={{0,10},{1,11},{2,8},{3,9},{4,14},{5,15},{6,12},{7,13},{8,2},{9,3},... | collective-permute-start | bytes 393224 | tf_op jit(solution)/shard_map/ppermute | solution.py:280
  35.6 15.5 %collective-permute-start.22 = (bf16[256,256]{1,0:T(8,128)(2,1)S(1)}, bf16[256,256]{1,0:T(8,128)(2,1)S(1)}, u32[]{:S(2)}, u32[]{:S(2)}) collective-permute-start(bf16[256,256]{1,0:T(8,128)(2,1)S(1)} %copy-done.33), channel_id=1, source_target_pairs={{0,11},{1,10},{2,9},{3,8},{4,15},{5,14},{6,13},{7,12},{8,3},{9,2},... | collective-permute-start | bytes 393224 | tf_op jit(solution)/shard_map/ppermute | solution.py:280
  45.5 13.1 %collective-permute-start.6 = (bf16[384,256]{1,0:T(8,128)(2,1)}, bf16[384,256]{1,0:T(8,128)(2,1)S(1)}, u32[]{:S(2)}, u32[]{:S(2)}) collective-permute-start(bf16[384,256]{1,0:T(8,128)(2,1)} %get-tuple-element.55), channel_id=1, source_target_pairs={{0,3},{1,2},{2,1},{3,0},{4,7},{5,6},{6,5},{7,4},{8,11},{9,10},{10,... | collective-permute-start | bytes 589832 | tf_op jit(solution)/shard_map/ppermute | solution.py:280
  48.3 12.1 %collective-permute-start.7 = (bf16[384,256]{1,0:T(8,128)(2,1)}, bf16[384,256]{1,0:T(8,128)(2,1)S(1)}, u32[]{:S(2)}, u32[]{:S(2)}) collective-permute-start(bf16[384,256]{1,0:T(8,128)(2,1)} %get-tuple-element.56), channel_id=1, source_target_pairs={{0,4},{1,5},{2,6},{3,7},{4,0},{5,1},{6,2},{7,3},{8,12},{9,13},{10,... | collective-permute-start | bytes 589832 | tf_op jit(solution)/shard_map/ppermute | solution.py:280
  53.4 11.6 %collective-permute-start.9 = (bf16[384,256]{1,0:T(8,128)(2,1)}, bf16[384,256]{1,0:T(8,128)(2,1)S(1)}, u32[]{:S(2)}, u32[]{:S(2)}) collective-permute-start(bf16[384,256]{1,0:T(8,128)(2,1)} %get-tuple-element.58), channel_id=1, source_target_pairs={{0,6},{1,7},{2,4},{3,5},{4,2},{5,3},{6,0},{7,1},{8,14},{9,15},{10,... | collective-permute-start | bytes 589832 | tf_op jit(solution)/shard_map/ppermute | solution.py:280
  55.1 16.4 %collective-permute-start.10 = (bf16[384,256]{1,0:T(8,128)(2,1)}, bf16[384,256]{1,0:T(8,128)(2,1)S(1)}, u32[]{:S(2)}, u32[]{:S(2)}) collective-permute-start(bf16[384,256]{1,0:T(8,128)(2,1)} %get-tuple-element.59), channel_id=1, source_target_pairs={{0,7},{1,6},{2,5},{3,4},{4,3},{5,2},{6,1},{7,0},{8,15},{9,14},{10,... | collective-permute-start | bytes 589832 | tf_op jit(solution)/shard_map/ppermute | solution.py:280
  58.6 36.3 %collective-permute-start = (bf16[256,256]{1,0:T(8,128)(2,1)S(1)}, bf16[256,256]{1,0:T(8,128)(2,1)S(1)}, u32[]{:S(2)}, u32[]{:S(2)}) collective-permute-start(bf16[256,256]{1,0:T(8,128)(2,1)S(1)} %copy-done.29), channel_id=1, source_target_pairs={{0,12},{1,13},{2,14},{3,15},{4,8},{5,9},{6,10},{7,11},{8,4},{9,5},... | collective-permute-start | bytes 393224 | tf_op jit(solution)/shard_map/ppermute | solution.py:280
  60.4 34.6 %collective-permute-start.1 = (bf16[256,256]{1,0:T(8,128)(2,1)S(1)}, bf16[256,256]{1,0:T(8,128)(2,1)S(1)}, u32[]{:S(2)}, u32[]{:S(2)}) collective-permute-start(bf16[256,256]{1,0:T(8,128)(2,1)S(1)} %copy-done.28), channel_id=1, source_target_pairs={{0,13},{1,12},{2,15},{3,14},{4,9},{5,8},{6,11},{7,10},{8,5},{9,4},... | collective-permute-start | bytes 393224 | tf_op jit(solution)/shard_map/ppermute | solution.py:280
  60.9 34.1 %collective-permute-start.2 = (bf16[256,256]{1,0:T(8,128)(2,1)S(1)}, bf16[256,256]{1,0:T(8,128)(2,1)S(1)}, u32[]{:S(2)}, u32[]{:S(2)}) collective-permute-start(bf16[256,256]{1,0:T(8,128)(2,1)S(1)} %copy-done.27), channel_id=1, source_target_pairs={{0,14},{1,15},{2,12},{3,13},{4,10},{5,11},{6,8},{7,9},{8,6},{9,7},... | collective-permute-start | bytes 393224 | tf_op jit(solution)/shard_map/ppermute | solution.py:280
  65.0 30.0 %collective-permute-start.3 = (bf16[256,256]{1,0:T(8,128)(2,1)S(1)}, bf16[256,256]{1,0:T(8,128)(2,1)S(1)}, u32[]{:S(2)}, u32[]{:S(2)}) collective-permute-start(bf16[256,256]{1,0:T(8,128)(2,1)S(1)} %copy-done.26), channel_id=1, source_target_pairs={{0,15},{1,14},{2,13},{3,12},{4,11},{5,10},{6,9},{7,8},{8,7},{9,6},... | collective-permute-start | bytes 393224 | tf_op jit(solution)/shard_map/ppermute | solution.py:280
  110.3 15.6 %collective-permute-start.26 = (bf16[128,256]{1,0:T(8,128)(2,1)}, bf16[128,256]{1,0:T(8,128)(2,1)S(1)}, u32[]{:S(2)}, u32[]{:S(2)}) collective-permute-start(bf16[128,256]{1,0:T(8,128)(2,1)} %get-tuple-element.79), channel_id=1, source_target_pairs={{0,4},{1,5},{2,6},{3,7},{4,0},{5,1},{6,2},{7,3},{8,12},{9,13},{10,... | collective-permute-start | bytes 196616 | tf_op jit(solution)/shard_map/ppermute | solution.py:280
  110.3 16.3 %collective-permute-start.27 = (bf16[128,256]{1,0:T(8,128)(2,1)}, bf16[128,256]{1,0:T(8,128)(2,1)S(1)}, u32[]{:S(2)}, u32[]{:S(2)}) collective-permute-start(bf16[128,256]{1,0:T(8,128)(2,1)} %get-tuple-element.80), channel_id=1, source_target_pairs={{0,5},{1,4},{2,7},{3,6},{4,1},{5,0},{6,3},{7,2},{8,13},{9,12},{10,... | collective-permute-start | bytes 196616 | tf_op jit(solution)/shard_map/ppermute | solution.py:280
  111.7 17.8 %collective-permute-start.28 = (bf16[128,256]{1,0:T(8,128)(2,1)}, bf16[128,256]{1,0:T(8,128)(2,1)S(1)}, u32[]{:S(2)}, u32[]{:S(2)}) collective-permute-start(bf16[128,256]{1,0:T(8,128)(2,1)} %get-tuple-element.81), channel_id=1, source_target_pairs={{0,6},{1,7},{2,4},{3,5},{4,2},{5,3},{6,0},{7,1},{8,14},{9,15},{10,... | collective-permute-start | bytes 196616 | tf_op jit(solution)/shard_map/ppermute | solution.py:280
  111.7 18.3 %collective-permute-start.29 = (bf16[128,256]{1,0:T(8,128)(2,1)}, bf16[128,256]{1,0:T(8,128)(2,1)S(1)}, u32[]{:S(2)}, u32[]{:S(2)}) collective-permute-start(bf16[128,256]{1,0:T(8,128)(2,1)} %get-tuple-element.82), channel_id=1, source_target_pairs={{0,7},{1,6},{2,5},{3,4},{4,3},{5,2},{6,1},{7,0},{8,15},{9,14},{10,... | collective-permute-start | bytes 196616 | tf_op jit(solution)/shard_map/ppermute | solution.py:280
  114.7 17.8 %collective-permute-start.30 = (bf16[128,256]{1,0:T(8,128)(2,1)}, bf16[128,256]{1,0:T(8,128)(2,1)S(1)}, u32[]{:S(2)}, u32[]{:S(2)}) collective-permute-start(bf16[128,256]{1,0:T(8,128)(2,1)} %get-tuple-element.83), channel_id=1, source_target_pairs={{0,8},{1,9},{2,10},{3,11},{4,12},{5,13},{6,14},{7,15},{8,0},{9,1},... | collective-permute-start | bytes 196616 | tf_op jit(solution)/shard_map/ppermute | solution.py:280
  126.6 11.2 %collective-permute-start.32 = (bf16[128,256]{1,0:T(8,128)(2,1)}, bf16[128,256]{1,0:T(8,128)(2,1)S(1)}, u32[]{:S(2)}, u32[]{:S(2)}) collective-permute-start(bf16[128,256]{1,0:T(8,128)(2,1)} %get-tuple-element.85), channel_id=1, source_target_pairs={{0,10},{1,11},{2,8},{3,9},{4,14},{5,15},{6,12},{7,13},{8,2},{9,3},... | collective-permute-start | bytes 196616 | tf_op jit(solution)/shard_map/ppermute | solution.py:280
  129.5 11.5 %collective-permute-start.33 = (bf16[128,256]{1,0:T(8,128)(2,1)}, bf16[128,256]{1,0:T(8,128)(2,1)S(1)}, u32[]{:S(2)}, u32[]{:S(2)}) collective-permute-start(bf16[128,256]{1,0:T(8,128)(2,1)} %get-tuple-element.86), channel_id=1, source_target_pairs={{0,11},{1,10},{2,9},{3,8},{4,15},{5,14},{6,13},{7,12},{8,3},{9,2},... | collective-permute-start | bytes 196616 | tf_op jit(solution)/shard_map/ppermute | solution.py:280
  130.1 12.8 %collective-permute-start.34 = (bf16[128,256]{1,0:T(8,128)(2,1)}, bf16[128,256]{1,0:T(8,128)(2,1)S(1)}, u32[]{:S(2)}, u32[]{:S(2)}) collective-permute-start(bf16[128,256]{1,0:T(8,128)(2,1)} %get-tuple-element.87), channel_id=1, source_target_pairs={{0,12},{1,13},{2,14},{3,15},{4,8},{5,9},{6,10},{7,11},{8,4},{9,5},... | collective-permute-start | bytes 196616 | tf_op jit(solution)/shard_map/ppermute | solution.py:280
  132.5 13.2 %collective-permute-start.35 = (bf16[128,256]{1,0:T(8,128)(2,1)}, bf16[128,256]{1,0:T(8,128)(2,1)S(1)}, u32[]{:S(2)}, u32[]{:S(2)}) collective-permute-start(bf16[128,256]{1,0:T(8,128)(2,1)} %get-tuple-element.88), channel_id=1, source_target_pairs={{0,13},{1,12},{2,15},{3,14},{4,9},{5,8},{6,11},{7,10},{8,5},{9,4},... | collective-permute-start | bytes 196616 | tf_op jit(solution)/shard_map/ppermute | solution.py:280
  135.6 13.7 %collective-permute-start.36 = (bf16[128,256]{1,0:T(8,128)(2,1)}, bf16[128,256]{1,0:T(8,128)(2,1)S(1)}, u32[]{:S(2)}, u32[]{:S(2)}) collective-permute-start(bf16[128,256]{1,0:T(8,128)(2,1)} %get-tuple-element.89), channel_id=1, source_target_pairs={{0,14},{1,15},{2,12},{3,13},{4,10},{5,11},{6,8},{7,9},{8,6},{9,7},... | collective-permute-start | bytes 196616 | tf_op jit(solution)/shard_map/ppermute | solution.py:280
  137.8 12.9 %collective-permute-start.37 = (bf16[128,256]{1,0:T(8,128)(2,1)}, bf16[128,256]{1,0:T(8,128)(2,1)S(1)}, u32[]{:S(2)}, u32[]{:S(2)}) collective-permute-start(bf16[128,256]{1,0:T(8,128)(2,1)} %get-tuple-element.90), channel_id=1, source_target_pairs={{0,15},{1,14},{2,13},{3,12},{4,11},{5,10},{6,9},{7,8},{8,7},{9,6},... | collective-permute-start | bytes 196616 | tf_op jit(solution)/shard_map/ppermute | solution.py:280
  (55 other events, 1210.8 us)

commit v3 on v0

v3 whole, which is shorter than its diff:
```python
import functools
import math

import jax
import jax.numpy as jnp
from jax import lax
from jax.experimental import pallas as pl
from jax.experimental.pallas import tpu as pltpu
from jax.sharding import PartitionSpec as P


HD = 128
TO_LOG2 = HD ** (-0.5) * math.log2(math.e)
NT = (((1,), (1,)), ((), ()))

IN_HBM = pl.BlockSpec(memory_space=pltpu.HBM)
WHOLE = pl.BlockSpec(memory_space=pltpu.VMEM)
SCALARS = pl.BlockSpec(memory_space=pltpu.SMEM)


def run_copies(pairs, sems):
    copies = [
        pltpu.make_async_copy(src, dst, sems.at[i]) for i, (src, dst) in enumerate(pairs)
    ]
    for copy in copies:
        copy.start()
    for copy in copies:
        copy.wait()


def spread_body(x_ref, out_ref, sems):
    n, _, width = out_ref.shape
    run_copies(
        [(x_ref.at[:, pl.ds(dest * width, width)], out_ref.at[dest]) for dest in range(n)], sems
    )


def spread(x, n, width):
    return pl.pallas_call(
        spread_body,
        out_shape=jax.ShapeDtypeStruct((n, x.shape[0], width), x.dtype),
        in_specs=[IN_HBM],
        out_specs=WHOLE,
        scratch_shapes=[pltpu.SemaphoreType.DMA((n,))],
    )(x)


def pack_body(slots, scal_ref, k_ref, v_ref, *refs):
    outs, sems = refs[:-1], refs[-1]
    rows = k_ref.shape[0]
    width = outs[0].shape[1]
    pairs = []
    for slot, out_ref in zip(slots, outs):
        cols = pl.ds(pl.multiple_of((scal_ref[0] ^ slot) * width, HD), width)
        pairs.append((k_ref.at[:, cols], out_ref.at[pl.ds(0, rows)]))
        pairs.append((v_ref.at[:, cols], out_ref.at[pl.ds(rows, rows)]))
    run_copies(pairs, sems)


def pack(scal, k, v, slots, width):
    rows = k.shape[0]
    block = jax.ShapeDtypeStruct((2 * rows, width), k.dtype)
    return pl.pallas_call(
        functools.partial(pack_body, tuple(slots)),
        out_shape=[block] * len(slots),
        in_specs=[SCALARS, IN_HBM, IN_HBM],
        out_specs=[WHOLE] * len(slots),
        scratch_shapes=[pltpu.SemaphoreType.DMA((2 * len(slots),))],
    )(scal, k, v)


def softmax_add(queries, tops, accs, take_keys, take_values, total, limit):
    chunk = math.gcd(limit, total)
    ones = jnp.ones((chunk, HD), jnp.bfloat16)
    every = range(len(queries))
    for at in range(0, total, chunk):
        scores = [
            lax.dot_general(
                queries[i], take_keys(i, at, chunk), NT, preferred_element_type=jnp.float32
            )
            for i in every
        ]
        new_tops = [jnp.max(s, axis=1, keepdims=True) for s in scores]
        if tops is not None:
            new_tops = [jnp.maximum(new, old) for new, old in zip(new_tops, tops)]
        probs = [
            jnp.exp2((s - top) * TO_LOG2).astype(jnp.bfloat16)
            for s, top in zip(scores, new_tops)
        ]
        parts = [
            jnp.dot(
                probs[i],
                jnp.concatenate([take_values(i, at, chunk), ones], axis=1),
                preferred_element_type=jnp.float32,
            )
            for i in every
        ]
        if accs is not None:
            parts = [
                acc * jnp.exp2((old - new) * TO_LOG2) + part
                for acc, old, new, part in zip(accs, tops, new_tops, parts)
            ]
        tops, accs = new_tops, parts
    return tops, accs


def split_stat(stat):
    first = lax.broadcasted_iota(jnp.int32, stat.shape, 1) < HD // 2
    top = jnp.max(jnp.where(first, stat, -jnp.inf), axis=1, keepdims=True)
    row_sum = jnp.max(jnp.where(first, 0.0, stat), axis=1, keepdims=True)
    return top, jnp.broadcast_to(row_sum, stat.shape)


def stage_body(n_kv, has_stale, has_state, scal_ref, q_ref, *refs):
    refs = list(refs)
    take_refs = lambda count: [refs.pop(0) for _ in range(count)]
    state_in = take_refs(2 * has_state)
    kv_refs = take_refs(n_kv)
    stale = take_refs(2 * has_stale)
    acc_ref, stat_ref, keys, values, low_k, low_v, sems = refs
    per, rows, width = q_ref.shape
    total = keys.shape[0]
    n_old = total - n_kv * rows

    @pl.when(pl.program_id(0) == 0)
    def _():
        pairs = []
        for place, ref in enumerate(kv_refs):
            to = pl.ds(n_old + place * rows, rows)
            pairs.append((ref.at[pl.ds(0, rows)], keys.at[to]))
            pairs.append((ref.at[pl.ds(rows, rows)], values.at[to]))
        if has_stale:
            patch = stale[0].shape[0] - n_old
            start = scal_ref[1]
            edge = pl.multiple_of(jnp.minimum(start // rows, n_old // rows - 1) * rows, rows)
            for at in range(0, n_old, rows):
                src = pl.multiple_of(jnp.where(at + rows <= start, at, at + patch), rows)
                for ref, full in zip(stale, (keys, values)):
                    pairs.append((ref.at[pl.ds(src, rows)], full.at[pl.ds(at, rows)]))
            for ref, low in zip(stale, (low_k, low_v)):
                pairs.append((ref.at[pl.ds(edge, rows)], low))
        run_copies(pairs, sems)
        if has_stale:
            row = lax.broadcasted_iota(jnp.int32, low_k.shape, 0) + edge
            for low, full in ((low_k, keys), (low_v, values)):
                here = full.at[pl.ds(edge, rows)]
                kept = jnp.where(
                    row < start, low[...].astype(jnp.float32), here[...].astype(jnp.float32)
                )
                here[...] = kept.astype(jnp.bfloat16)

    q_all = q_ref[...].reshape(per * rows, width)
    block = min(256, per * rows)
    lane = lax.broadcasted_iota(jnp.int32, (block, HD), 1)
    for at in range(0, per * rows, block):
        here = slice(at, at + block)
        for cols in [slice(col, col + HD) for col in range(0, width, HD)]:
            tops, accs = None, None
            if has_state:
                top, row_sum = split_stat(state_in[1][here, cols])
                tops = [top]
                accs = [jnp.concatenate([state_in[0][here, cols], row_sum], axis=1)]
            (top,), (acc,) = softmax_add(
                [q_all[here, cols]],
                tops,
                accs,
                lambda i, at, chunk, cols=cols: keys[at : at + chunk, cols],
                lambda i, at, chunk, cols=cols: values[at : at + chunk, cols],
                total,
                1024 if has_state else 512,
            )
            acc_ref[here, cols] = acc[:, :HD]
            stat_ref[here, cols] = jnp.where(lane < HD // 2, top, acc[:, HD:])


def cost(patch, total, width):
    return pl.CostEstimate(
        flops=6 * patch * total * width,
        bytes_accessed=2 * width * (6 * patch + 2 * total),
        transcendentals=patch * total * (width // HD),
    )


def attend_stage(scal, queries, state, kv, stale):
    n, rows, width = queries.shape
    patch = n * rows
    n_old = stale[0].shape[0] - patch if stale else 0
    total = n_old + len(kv) * rows
    per = min(4, n)
    kept = jax.ShapeDtypeStruct((patch, width), jnp.float32)
    block = pl.BlockSpec((per * rows, width), lambda i, s: (i, 0))
    full = pltpu.VMEM((total, width), jnp.bfloat16)
    low = pltpu.VMEM((rows, width), jnp.bfloat16)
    n_copies = 2 * (total // rows + 1)
    return pl.pallas_call(
        functools.partial(stage_body, len(kv), bool(stale), bool(state)),
        out_shape=[kept, kept],
        grid_spec=pltpu.PrefetchScalarGridSpec(
            num_scalar_prefetch=1,
            grid=(n // per,),
            in_specs=[pl.BlockSpec((per, rows, width), lambda i, s: (i, 0, 0))]
            + [block] * len(state)
            + [IN_HBM] * (len(kv) + len(stale)),
            out_specs=[block, block],
            scratch_shapes=[full, full, low, low, pltpu.SemaphoreType.DMA((n_copies,))],
        ),
        cost_estimate=cost(patch, total, width),
    )(scal, queries, *state, *kv, *stale)


def last_body(n_kv, n, scal_ref, *refs):
    kv_refs = refs[:n_kv]
    q_hbm, acc_hbm, stat_hbm, gate_hbm = refs[n_kv : n_kv + 4]
    out_refs = refs[n_kv + 4 : n_kv + 4 + n]
    q_ref, acc_ref, stat_ref, gate_ref, keys, values, sems = refs[n_kv + 4 + n :]
    rows, width = out_refs[0].shape
    me = scal_ref[0]
    at = pl.multiple_of(me * width, HD)
    gate_copy = pltpu.make_async_copy(gate_hbm.at[:, pl.ds(at, width)], gate_ref, sems.at[3 * n])
    kv_copies = []
    for place, ref in enumerate(kv_refs):
        to = pl.ds(place * rows, rows)
        for half, full in enumerate((keys, values)):
            sem = sems.at[3 * n + 1 + len(kv_copies)]
            kv_copies.append(
                pltpu.make_async_copy(ref.at[pl.ds(half * rows, rows)], full.at[to], sem)
            )
            kv_copies[-1].start()
    copies = []
    for slot in range(n):
        source = me ^ slot
        place = pl.ds(pl.multiple_of(source * rows, rows), rows)
        to = pl.ds(slot * rows, rows)
        copies += [
            pltpu.make_async_copy(q_hbm.at[source], q_ref.at[to], sems.at[3 * slot]),
            pltpu.make_async_copy(acc_hbm.at[place], acc_ref.at[to], sems.at[3 * slot + 1]),
            pltpu.make_async_copy(stat_hbm.at[place], stat_ref.at[to], sems.at[3 * slot + 2]),
        ]
        for copy in copies[-3:]:
            copy.start()
        if slot == 1:
            gate_copy.start()
    head_cols = [slice(at, at + HD) for at in range(0, width, HD)]

    for copy in kv_copies:
        copy.wait()
    gate = None
    for first in range(0, n, 2):
        for copy in copies[3 * first : 3 * first + 6]:
            copy.wait()
        if gate is None:
            gate_copy.wait()
            gate = gate_ref[pl.ds(scal_ref[2], 1), :]
        here = slice(first * rows, (first + 2) * rows)
        for cols in head_cols:
            top, row_sum = split_stat(stat_ref[here, cols])
            _, (acc,) = softmax_add(
                [q_ref[here, cols]],
                [top],
                [jnp.concatenate([acc_ref[here, cols], row_sum], axis=1)],
                lambda i, at, chunk, cols=cols: keys[at : at + chunk, cols],
                lambda i, at, chunk, cols=cols: values[at : at + chunk, cols],
                n_kv * rows,
                1024,
            )
            attn = (acc[:, :HD] / acc[:, HD:]).astype(jnp.bfloat16)
            gated = (attn.astype(jnp.float32) * gate[:, cols]).astype(jnp.bfloat16)
            out_refs[first][:, cols] = gated[:rows]
            out_refs[first + 1][:, cols] = gated[rows:]


def attend_last(scal, queries, state, kv, gate_table):
    n, rows, width = queries.shape
    piece = jax.ShapeDtypeStruct((rows, width), jnp.bfloat16)
    kept = pltpu.VMEM((n * rows, width), jnp.float32)
    full = pltpu.VMEM((len(kv) * rows, width), jnp.bfloat16)
    return pl.pallas_call(
        functools.partial(last_body, len(kv), n),
        out_shape=[piece] * n,
        in_specs=[SCALARS] + [IN_HBM] * (len(kv) + 4),
        out_specs=[WHOLE] * n,
        scratch_shapes=[
            pltpu.VMEM((n * rows, width), jnp.bfloat16),
            kept,
            kept,
            pltpu.VMEM((gate_table.shape[0], width), jnp.float32),
            full,
            full,
            pltpu.SemaphoreType.DMA((3 * n + 1 + 2 * len(kv),)),
        ],
        cost_estimate=cost(n * rows, len(kv) * rows, width),
    )(scal, *kv, queries, *state, gate_table)


def unpack_body(scal_ref, *refs):
    parts, out_ref, sems = refs[:-2], refs[-2], refs[-1]
    width = parts[0].shape[1]
    pairs = []
    for slot, ref in enumerate(parts):
        at = pl.multiple_of((scal_ref[0] ^ slot) * width, HD)
        pairs.append((ref, out_ref.at[:, pl.ds(at, width)]))
    run_copies(pairs, sems)


def unpack(scal, parts):
    rows, width = parts[0].shape
    return pl.pallas_call(
        unpack_body,
        out_shape=jax.ShapeDtypeStruct((rows, len(parts) * width), parts[0].dtype),
        in_specs=[SCALARS] + [IN_HBM] * len(parts),
        out_specs=WHOLE,
        scratch_shapes=[pltpu.SemaphoreType.DMA((len(parts),))],
    )(scal, *parts)


def shards(
    fresh_query, fresh_key, fresh_value, stale_key, stale_value, patch_start, timestep, gate_table
):
    n = lax.axis_size("seq")
    width = stale_key.shape[1]
    me = lax.axis_index("seq").astype(jnp.int32)
    near, far = range(n // 2), range(n // 2, n)

    def send(slot, block):
        return lax.ppermute(block, "seq", [(i, i ^ slot) for i in range(n)])

    def send_all(slots, blocks):
        return [b if s == 0 else send(s, b) for s, b in zip(slots, blocks)]

    scal = jnp.stack([me, patch_start[0], timestep[0]])
    head, tail = far[: n // 8], far[n // 8 :]
    head_blocks = pack(me[None], fresh_key, fresh_value, head, width)
    head_kv = send_all(head, head_blocks)
    spread_q = spread(fresh_query, n, width)
    queries = lax.all_to_all(spread_q, "seq", 0, 0, tiled=True)
    blocks = pack(me[None], fresh_key, fresh_value, (*near, *tail), width)
    near_kv = send_all(near, blocks[: n // 2])
    tail_kv = send_all(tail, blocks[n // 2 :])
    state = attend_stage(scal, queries, [], head_kv, [stale_key, stale_value])
    state = attend_stage(scal, queries, state, near_kv, [])
    outs = attend_last(scal, queries, state, tail_kv, gate_table)
    home_far = send_all(far, outs[n // 2 :])
    home_near = send_all(near, outs[: n // 2])
    return unpack(me[None], [*home_near, *home_far])


def solution(mesh):
    return jax.shard_map(
        shards,
        mesh=mesh,
        in_specs=(
            P(("grp", "seq"), None),
            P(("grp", "seq"), None),
            P(("grp", "seq"), None),
            P("grp", "seq"),
            P("grp", "seq"),
            P("grp"),
            P("grp"),
            P(),
        ),
        out_specs=P(("grp", "seq"), None),
        check_vma=False,
    )
```

time: 212 us -> 151 us (0.71)
  Pallas kernels: 0 us -> 47.5 us
  matrix products: 46.4 us -> 0 us
  other arithmetic: 45.1 us -> 0.61 us
  starting transfers between devices: 20.9 us -> 49.3 us
  local copies, waits for them, and re-layouts: 25.2 us -> 2.5 us
  waiting for transfers between devices: 71.2 us -> 48.9 us
    all_to_all x4 -> x1, waiting for transfers between devices: 71.2 us -> 0.01 us  [shards(): queries = lax.all_to_all(spread_q, 'seq', 0, 0, tiled=True)]
    ppermute x0 -> x30, waiting for transfers between devices: none -> 48.9 us  [send(): return lax.ppermute(block, 'seq', [(i, i ^ slot) for i in range(n)])]
    pallas_call x0 -> x7, Pallas kernels: none -> 47.5 us  [the longest x2 28.3 us: attend_stage(): pl.pallas_call(functools.partial(stage_body, len(kv), bool(stale), bool(s...]
    dot_general x32 -> x0, matrix products: 46.4 us -> none  [the longest x16 24.3 us: attend_group(): jnp.dot(queries, keys.T, preferred_element_type=jnp.float32) * HD ** (-0.5)]
    ppermute x0 -> x30, starting transfers between devices: none -> 42.7 us  [send(): return lax.ppermute(block, 'seq', [(i, i ^ slot) for i in range(n)])]
    convert_element_type x4 -> x0, other arithmetic: 23.8 us -> none  [the longest x2 20.5 us: shards(): outputs.append((numer / denom[:, None]).astype(jnp.bfloat16))]
    all_to_all x4 -> x1, starting transfers between devices: 20.9 us -> 6.59 us  [shards(): queries = lax.all_to_all(spread_q, 'seq', 0, 0, tiled=True)]
    reduce_sum x16 -> x0, other arithmetic: 13 us -> none  [attend_group(): total = jnp.sum(expo, axis=1)]
  transfers between devices with their start and end apart: 4 -> 31, of which waited for: 4 -> 13; matrix products, arithmetic and copies ran while one was open for 12% -> 0% of each run, Pallas kernels for 0% -> 22%
where the time goes in v3:
time: 151 us
  starting transfers between devices  49.3 us (33%)
  waiting for transfers between devices  48.9 us (32%)
  Pallas kernels  47.5 us (31%)
  local copies, waits for them, and re-layouts  2.5 us (2%)
  between operations  1.79 us (1%)
    ppermute x30, waiting for transfers between devices, send(): return lax.ppermute(block, 'seq', [(i, i ^ slot) for i in range(n)])  48.9 us
    ppermute x30, starting transfers between devices, send(): return lax.ppermute(block, 'seq', [(i, i ^ slot) for i in range(n)])  42.7 us
    pallas_call x2, Pallas kernels, attend_stage(): pl.pallas_call(functools.partial(stage_body, len(kv), bool(stale), bool(s...  28.3 us
    pallas_call x1, Pallas kernels, attend_last(): pl.pallas_call(functools.partial(last_body, len(kv), n), out_shape=[piece...  9.8 us
    all_to_all x1, starting transfers between devices, shards(): queries = lax.all_to_all(spread_q, 'seq', 0, 0, tiled=True)  6.59 us
    pallas_call x2, Pallas kernels, pack(): pl.pallas_call(functools.partial(pack_body, tuple(slots)), out_shape=[blo...  4.69 us
  transfers between devices with their start and end apart: 31, of which 13 were waited for; matrix products, arithmetic and copies ran while one was open for 0% of the time, Pallas kernels for 22%

profile of v3, /device:TPU:11, one launch (start us, length us, event | category | flops | bytes accessed | tf_op | source)
XLA Modules:
  0.0 150.6 jit_solution(6529323093836424570)
XLA Ops:
  0.0 2.4 %shard_map.83 = bf16[16,128,256]{2,1,0:T(8,128)(2,1)} custom-call(bf16[128,4096]{1,0:T(8,128)(2,1)} %x_ref.1), custom_call_target="tpu_custom_call" | custom-call | tf_op jit(solution)/shard_map/pallas_call | solution.py:39
  2.4 6.6 %all-to-all-start = ((bf16[16,128,256]{2,1,0:T(8,128)(2,1)}), bf16[16,128,256]{2,1,0:T(8,128)(2,1)S(1)}, u32[]{:S(2)}, u32[]{:S(2)}) async-start(bf16[16,128,256]{2,1,0:T(8,128)(2,1)} %shard_map.83), calls=%async_computation | async-start | bytes 2097152 | tf_op jit(solution)/shard_map/all_to_all | solution.py:335
  9.0 1.7 %shard_map.84 = (bf16[256,256]{1,0:T(8,128)(2,1)}, bf16[256,256]{1,0:T(8,128)(2,1)}) custom-call(s32[1]{0:T(128)} %bitcast.scal_ref, bf16[128,4096]{1,0:T(8,128)(2,1)} %k_ref.3, bf16[128,4096]{1,0:T(8,128)(2,1)} %v_ref.3), custom_call_target="tpu_custom_call" | custom-call | tf_op jit(solution)/shard_map/pallas_call | solution.py:63
  10.7 2.2 %collective-permute-start.6 = (bf16[256,256]{1,0:T(8,128)(2,1)}, bf16[256,256]{1,0:T(8,128)(2,1)S(1)}, u32[]{:S(2)}, u32[]{:S(2)}) collective-permute-start(bf16[256,256]{1,0:T(8,128)(2,1)} %get-tuple-element.47), channel_id=1, source_target_pairs={{0,8},{1,9},{2,10},{3,11},{4,12},{5,13},{6,14},{7,15},{8,0},{9,1},... | collective-permute-start | bytes 393224 | tf_op jit(solution)/shard_map/ppermute | solution.py:325
  13.6 3.0 %shard_map.82 = (bf16[256,256]{1,0:T(8,128)(2,1)}, bf16[256,256]{1,0:T(8,128)(2,1)}, bf16[256,256]{1,0:T(8,128)(2,1)}, bf16[256,256]{1,0:T(8,128)(2,1)}, bf16[25...) custom-call(s32[1]{0:T(128)} %bitcast.scal_ref, ...), custom_call_target="tpu_custom_call" | custom-call | tf_op jit(solution)/shard_map/pallas_call | solution.py:63
  16.6 3.1 %collective-permute-start = (bf16[256,256]{1,0:T(8,128)(2,1)}, bf16[256,256]{1,0:T(8,128)(2,1)S(1)}, u32[]{:S(2)}, u32[]{:S(2)}) collective-permute-start(bf16[256,256]{1,0:T(8,128)(2,1)} %get-tuple-element.41), channel_id=1, source_target_pairs={{0,10},{1,11},{2,8},{3,9},{4,14},{5,15},{6,12},{7,13},{8,2},{9,3},... | collective-permute-start | bytes 393224 | tf_op jit(solution)/shard_map/ppermute | solution.py:325
  22.0 20.9 %collective-permute-done.6.refs_0_ = bf16[256,256]{1,0:T(8,128)(2,1)S(1)} collective-permute-done((bf16[256,256]{1,0:T(8,128)(2,1)}, bf16[256,256]{1,0:T(8,128)(2,1)S(1)}, u32[]{:S(2)}, u32[]{:S(2)}) %collective-permute-start.6) | collective-permute-done | bytes 131104 | tf_op jit(solution)/shard_map/ppermute | solution.py:325
  42.9 2.6 %collective-permute-start.10 = (bf16[256,256]{1,0:T(8,128)(2,1)}, bf16[256,256]{1,0:T(8,128)(2,1)S(1)}, u32[]{:S(2)}, u32[]{:S(2)}) collective-permute-start(bf16[256,256]{1,0:T(8,128)(2,1)} %get-tuple-element.54), channel_id=1, source_target_pairs={{0,3},{1,2},{2,1},{3,0},{4,7},{5,6},{6,5},{7,4},{8,11},{9,10},{10,... | collective-permute-start | bytes 393224 | tf_op jit(solution)/shard_map/ppermute | solution.py:325
  45.8 3.9 %collective-permute-start.11 = (bf16[256,256]{1,0:T(8,128)(2,1)}, bf16[256,256]{1,0:T(8,128)(2,1)S(1)}, u32[]{:S(2)}, u32[]{:S(2)}) collective-permute-start(bf16[256,256]{1,0:T(8,128)(2,1)} %get-tuple-element.55), channel_id=1, source_target_pairs={{0,4},{1,5},{2,6},{3,7},{4,0},{5,1},{6,2},{7,3},{8,12},{9,13},{10,... | collective-permute-start | bytes 393224 | tf_op jit(solution)/shard_map/ppermute | solution.py:325
  49.6 3.8 %collective-permute-start.12 = (bf16[256,256]{1,0:T(8,128)(2,1)}, bf16[256,256]{1,0:T(8,128)(2,1)S(1)}, u32[]{:S(2)}, u32[]{:S(2)}) collective-permute-start(bf16[256,256]{1,0:T(8,128)(2,1)} %get-tuple-element.56), channel_id=1, source_target_pairs={{0,5},{1,4},{2,7},{3,6},{4,1},{5,0},{6,3},{7,2},{8,13},{9,12},{10,... | collective-permute-start | bytes 393224 | tf_op jit(solution)/shard_map/ppermute | solution.py:325
  53.5 2.0 %collective-permute-start.14 = (bf16[256,256]{1,0:T(8,128)(2,1)}, bf16[256,256]{1,0:T(8,128)(2,1)S(1)}, u32[]{:S(2)}, u32[]{:S(2)}) collective-permute-start(bf16[256,256]{1,0:T(8,128)(2,1)} %get-tuple-element.58), channel_id=1, source_target_pairs={{0,7},{1,6},{2,5},{3,4},{4,3},{5,2},{6,1},{7,0},{8,15},{9,14},{10,... | collective-permute-start | bytes 393224 | tf_op jit(solution)/shard_map/ppermute | solution.py:325
  56.5 16.9 %shard_map.85 = (f32[2048,256]{1,0:T(8,128)}, f32[2048,256]{1,0:T(8,128)}) custom-call(s32[3]{0:T(128)} %pad_add_fusion.scal_ref, bf16[16,128,256]{2,1,0:T(8,128)(2,1)} %copy-done, bf16[256,256]{1,0:T(8,128)(2,1)} %copy-done.26, bf16[256,256]{1,0:T(8,128)(2,1)} %copy-done.28, bf16[4096,256]{1,0:T(8,128)(2,1)} %refs_2_.1, bf16[4096,256]{1,0:T(8,128)(2,1)} %refs_3_.1), custom_call_target="tpu_custom_call" | custom-call | flops 7247757312 | bytes 8650752 | tf_op jit(solution)/shard_map/pallas_call | solution.py:195
  74.2 1.2 collective-permute-start.2
  76.4 2.2 %collective-permute-start.4 = (bf16[256,256]{1,0:T(8,128)(2,1)S(1)}, bf16[256,256]{1,0:T(8,128)(2,1)S(1)}, u32[]{:S(2)}, u32[]{:S(2)}) collective-permute-start(bf16[256,256]{1,0:T(8,128)(2,1)S(1)} %copy-done.18), channel_id=1, source_target_pairs={{0,14},{1,15},{2,12},{3,13},{4,10},{5,11},{6,8},{7,9},{8,6},{9,7},... | collective-permute-start | bytes 393224 | tf_op jit(solution)/shard_map/ppermute | solution.py:325
  79.2 11.4 %shard_map.86 = (f32[2048,256]{1,0:T(8,128)}, f32[2048,256]{1,0:T(8,128)}) custom-call(s32[3]{0:T(128)} %pad_add_fusion.scal_ref, bf16[16,128,256]{2,1,0:T(8,128)(2,1)} %copy-done, f32[2048,256]{1,0:T(8,128)} %get-tuple-element.49.refs_0_, f32[2048,256]{1,0:T(8,128)} %get-tuple-element.50.refs_1_, bf16[256,256]{1,0:T(8,128)(2,1)} %get-tuple-element.51.refs_2_, ...), custom_call_target="tpu_custom_call" | custom-call | flops 3221225472 | bytes 7340032 | tf_op jit(solution)/shard_map/pallas_call | solution.py:195
  90.9 4.7 %collective-permute-done.2.refs_2_ = bf16[256,256]{1,0:T(8,128)(2,1)S(1)} collective-permute-done((bf16[256,256]{1,0:T(8,128)(2,1)S(1)}, bf16[256,256]{1,0:T(8,128)(2,1)S(1)}, u32[]{:S(2)}, u32[]{:S(2)}) %collective-permute-start.2) | collective-permute-done | bytes 131104 | tf_op jit(solution)/shard_map/ppermute | solution.py:325
  95.7 3.7 %collective-permute-done.3.refs_3_ = bf16[256,256]{1,0:T(8,128)(2,1)S(1)} collective-permute-done((bf16[256,256]{1,0:T(8,128)(2,1)S(1)}, bf16[256,256]{1,0:T(8,128)(2,1)S(1)}, u32[]{:S(2)}, u32[]{:S(2)}) %collective-permute-start.3) | collective-permute-done | bytes 131104 | tf_op jit(solution)/shard_map/ppermute | solution.py:325
  100.1 4.3 %collective-permute-done.5.refs_5_ = bf16[256,256]{1,0:T(8,128)(2,1)S(1)} collective-permute-done((bf16[256,256]{1,0:T(8,128)(2,1)S(1)}, bf16[256,256]{1,0:T(8,128)(2,1)S(1)}, u32[]{:S(2)}, u32[]{:S(2)}) %collective-permute-start.5) | collective-permute-done | bytes 131104 | tf_op jit(solution)/shard_map/ppermute | solution.py:325
  105.1 9.8 %shard_map.87 = (bf16[128,256]{1,0:T(8,128)(2,1)}, bf16[128,256]{1,0:T(8,128)(2,1)}, bf16[128,256]{1,0:T(8,128)(2,1)}, bf16[128,256]{1,0:T(8,128)(2,1)}, bf16[12...) custom-call(s32[3]{0:T(128)} %pad_add_fusion.scal_ref, ...), custom_call_target="tpu_custom_call" | custom-call | flops 2415919104 | bytes 7077888 | tf_op jit(solution)/shard_map/pallas_call | solution.py:277
  115.0 1.3 collective-permute-start.16
  117.1 1.5 collective-permute-start.19
  119.5 2.0 %collective-permute-start.21 = (bf16[128,256]{1,0:T(8,128)(2,1)}, bf16[128,256]{1,0:T(8,128)(2,1)S(1)}, u32[]{:S(2)}, u32[]{:S(2)}) collective-permute-start(bf16[128,256]{1,0:T(8,128)(2,1)} %get-tuple-element.68), channel_id=1, source_target_pairs={{0,7},{1,6},{2,5},{3,4},{4,3},{5,2},{6,1},{7,0},{8,15},{9,14},{10,... | collective-permute-start | bytes 196616 | tf_op jit(solution)/shard_map/ppermute | solution.py:325
  121.5 1.4 collective-permute-start.22
  125.2 2.5 %collective-permute-start.25 = (bf16[128,256]{1,0:T(8,128)(2,1)}, bf16[128,256]{1,0:T(8,128)(2,1)S(1)}, u32[]{:S(2)}, u32[]{:S(2)}) collective-permute-start(bf16[128,256]{1,0:T(8,128)(2,1)} %get-tuple-element.72), channel_id=1, source_target_pairs={{0,11},{1,10},{2,9},{3,8},{4,15},{5,14},{6,13},{7,12},{8,3},{9,2},... | collective-permute-start | bytes 196616 | tf_op jit(solution)/shard_map/ppermute | solution.py:325
  128.0 1.4 collective-permute-start.27
  129.4 3.7 %collective-permute-done.23.refs_9_ = bf16[128,256]{1,0:T(8,128)(2,1)S(1)} collective-permute-done((bf16[128,256]{1,0:T(8,128)(2,1)}, bf16[128,256]{1,0:T(8,128)(2,1)S(1)}, u32[]{:S(2)}, u32[]{:S(2)}) %collective-permute-start.23) | collective-permute-done | bytes 65568 | tf_op jit(solution)/shard_map/ppermute | solution.py:325
  133.1 2.5 %collective-permute-start.28 = (bf16[128,256]{1,0:T(8,128)(2,1)}, bf16[128,256]{1,0:T(8,128)(2,1)S(1)}, u32[]{:S(2)}, u32[]{:S(2)}) collective-permute-start(bf16[128,256]{1,0:T(8,128)(2,1)} %get-tuple-element.75), channel_id=1, source_target_pairs={{0,14},{1,15},{2,12},{3,13},{4,10},{5,11},{6,8},{7,9},{8,6},{9,7},... | collective-permute-start | bytes 196616 | tf_op jit(solution)/shard_map/ppermute | solution.py:325
  135.9 1.6 %collective-permute-start.29 = (bf16[128,256]{1,0:T(8,128)(2,1)}, bf16[128,256]{1,0:T(8,128)(2,1)S(1)}, u32[]{:S(2)}, u32[]{:S(2)}) collective-permute-start(bf16[128,256]{1,0:T(8,128)(2,1)} %get-tuple-element.76), channel_id=1, source_target_pairs={{0,15},{1,14},{2,13},{3,12},{4,11},{5,10},{6,9},{7,8},{8,7},{9,6},... | collective-permute-start | bytes 196616 | tf_op jit(solution)/shard_map/ppermute | solution.py:325
  137.5 3.0 %collective-permute-done.26.refs_12_ = bf16[128,256]{1,0:T(8,128)(2,1)S(1)} collective-permute-done((bf16[128,256]{1,0:T(8,128)(2,1)}, bf16[128,256]{1,0:T(8,128)(2,1)S(1)}, u32[]{:S(2)}, u32[]{:S(2)}) %collective-permute-start.26) | collective-permute-done | bytes 65568 | tf_op jit(solution)/shard_map/ppermute | solution.py:325
  141.2 4.8 %collective-permute-done.28.refs_14_ = bf16[128,256]{1,0:T(8,128)(2,1)S(1)} collective-permute-done((bf16[128,256]{1,0:T(8,128)(2,1)}, bf16[128,256]{1,0:T(8,128)(2,1)S(1)}, u32[]{:S(2)}, u32[]{:S(2)}) %collective-permute-start.28) | collective-permute-done | bytes 65568 | tf_op jit(solution)/shard_map/ppermute | solution.py:325
  146.0 1.4 collective-permute-done.29.refs_15_
  148.1 2.3 %shard_map.88 = bf16[128,4096]{1,0:T(8,128)(2,1)} custom-call(s32[1]{0:T(128)} %bitcast.scal_ref, bf16[128,256]{1,0:T(8,128)(2,1)} %get-tuple-element.61.refs_0_, bf16[128,256]{1,0:T(8,128)(2,1)} %copy-done.1, bf16[128,256]{1,0:T(8,128)(2,1)} %copy-done.2, bf16[128,256]{1,0:T(8,128)(2,1)} %copy-done.3, bf16[128,256]{1,0:T(8,128)(2,1)} %copy-done.4, ...), custom_call_target="tpu_custom_call" | custom-call | tf_op jit(solution)/shard_map/pallas_call | solution.py:307
  (110 shorter events, 13.2 us)
Async XLA Ops:
  2.4 53.1 %all-to-all-start = ((bf16[16,128,256]{2,1,0:T(8,128)(2,1)}), bf16[16,128,256]{2,1,0:T(8,128)(2,1)S(1)}, u32[]{:S(2)}, u32[]{:S(2)}) async-start(bf16[16,128,256]{2,1,0:T(8,128)(2,1)} %shard_map.83), calls=%async_computation | async-start | bytes 2097152 | tf_op jit(solution)/shard_map/all_to_all | solution.py:335
  10.7 32.3 %collective-permute-start.6 = (bf16[256,256]{1,0:T(8,128)(2,1)}, bf16[256,256]{1,0:T(8,128)(2,1)S(1)}, u32[]{:S(2)}, u32[]{:S(2)}) collective-permute-start(bf16[256,256]{1,0:T(8,128)(2,1)} %get-tuple-element.47), channel_id=1, source_target_pairs={{0,8},{1,9},{2,10},{3,11},{4,12},{5,13},{6,14},{7,15},{8,0},{9,1},... | collective-permute-start | bytes 393224 | tf_op jit(solution)/shard_map/ppermute | solution.py:325
  12.8 32.9 %collective-permute-start.7 = (bf16[256,256]{1,0:T(8,128)(2,1)}, bf16[256,256]{1,0:T(8,128)(2,1)S(1)}, u32[]{:S(2)}, u32[]{:S(2)}) collective-permute-start(bf16[256,256]{1,0:T(8,128)(2,1)} %get-tuple-element.48), channel_id=1, source_target_pairs={{0,9},{1,8},{2,11},{3,10},{4,13},{5,12},{6,15},{7,14},{8,1},{9,0},... | collective-permute-start | bytes 393224 | tf_op jit(solution)/shard_map/ppermute | solution.py:325
  16.6 33.0 %collective-permute-start = (bf16[256,256]{1,0:T(8,128)(2,1)}, bf16[256,256]{1,0:T(8,128)(2,1)S(1)}, u32[]{:S(2)}, u32[]{:S(2)}) collective-permute-start(bf16[256,256]{1,0:T(8,128)(2,1)} %get-tuple-element.41), channel_id=1, source_target_pairs={{0,10},{1,11},{2,8},{3,9},{4,14},{5,15},{6,12},{7,13},{8,2},{9,3},... | collective-permute-start | bytes 393224 | tf_op jit(solution)/shard_map/ppermute | solution.py:325
  19.7 33.7 %collective-permute-start.8 = (bf16[256,256]{1,0:T(8,128)(2,1)}, bf16[256,256]{1,0:T(8,128)(2,1)S(1)}, u32[]{:S(2)}, u32[]{:S(2)}) collective-permute-start(bf16[256,256]{1,0:T(8,128)(2,1)} %get-tuple-element.52), channel_id=1, source_target_pairs={{0,1},{1,0},{2,3},{3,2},{4,5},{5,4},{6,7},{7,6},{8,9},{9,8},{10,11... | collective-permute-start | bytes 393224 | tf_op jit(solution)/shard_map/ppermute | solution.py:325
  19.8 33.6 %collective-permute-start.9 = (bf16[256,256]{1,0:T(8,128)(2,1)}, bf16[256,256]{1,0:T(8,128)(2,1)S(1)}, u32[]{:S(2)}, u32[]{:S(2)}) collective-permute-start(bf16[256,256]{1,0:T(8,128)(2,1)} %get-tuple-element.53), channel_id=1, source_target_pairs={{0,2},{1,3},{2,0},{3,1},{4,6},{5,7},{6,4},{7,5},{8,10},{9,11},{10,... | collective-permute-start | bytes 393224 | tf_op jit(solution)/shard_map/ppermute | solution.py:325
  42.9 30.4 %collective-permute-start.10 = (bf16[256,256]{1,0:T(8,128)(2,1)}, bf16[256,256]{1,0:T(8,128)(2,1)S(1)}, u32[]{:S(2)}, u32[]{:S(2)}) collective-permute-start(bf16[256,256]{1,0:T(8,128)(2,1)} %get-tuple-element.54), channel_id=1, source_target_pairs={{0,3},{1,2},{2,1},{3,0},{4,7},{5,6},{6,5},{7,4},{8,11},{9,10},{10,... | collective-permute-start | bytes 393224 | tf_op jit(solution)/shard_map/ppermute | solution.py:325
  45.8 28.4 %collective-permute-start.11 = (bf16[256,256]{1,0:T(8,128)(2,1)}, bf16[256,256]{1,0:T(8,128)(2,1)S(1)}, u32[]{:S(2)}, u32[]{:S(2)}) collective-permute-start(bf16[256,256]{1,0:T(8,128)(2,1)} %get-tuple-element.55), channel_id=1, source_target_pairs={{0,4},{1,5},{2,6},{3,7},{4,0},{5,1},{6,2},{7,3},{8,12},{9,13},{10,... | collective-permute-start | bytes 393224 | tf_op jit(solution)/shard_map/ppermute | solution.py:325
  49.6 25.8 %collective-permute-start.12 = (bf16[256,256]{1,0:T(8,128)(2,1)}, bf16[256,256]{1,0:T(8,128)(2,1)S(1)}, u32[]{:S(2)}, u32[]{:S(2)}) collective-permute-start(bf16[256,256]{1,0:T(8,128)(2,1)} %get-tuple-element.56), channel_id=1, source_target_pairs={{0,5},{1,4},{2,7},{3,6},{4,1},{5,0},{6,3},{7,2},{8,13},{9,12},{10,... | collective-permute-start | bytes 393224 | tf_op jit(solution)/shard_map/ppermute | solution.py:325
  53.4 23.0 %collective-permute-start.13 = (bf16[256,256]{1,0:T(8,128)(2,1)}, bf16[256,256]{1,0:T(8,128)(2,1)S(1)}, u32[]{:S(2)}, u32[]{:S(2)}) collective-permute-start(bf16[256,256]{1,0:T(8,128)(2,1)} %get-tuple-element.57), channel_id=1, source_target_pairs={{0,6},{1,7},{2,4},{3,5},{4,2},{5,3},{6,0},{7,1},{8,14},{9,15},{10,... | collective-permute-start | bytes 393224 | tf_op jit(solution)/shard_map/ppermute | solution.py:325
  53.5 25.1 %collective-permute-start.14 = (bf16[256,256]{1,0:T(8,128)(2,1)}, bf16[256,256]{1,0:T(8,128)(2,1)S(1)}, u32[]{:S(2)}, u32[]{:S(2)}) collective-permute-start(bf16[256,256]{1,0:T(8,128)(2,1)} %get-tuple-element.58), channel_id=1, source_target_pairs={{0,7},{1,6},{2,5},{3,4},{4,3},{5,2},{6,1},{7,0},{8,15},{9,14},{10,... | collective-permute-start | bytes 393224 | tf_op jit(solution)/shard_map/ppermute | solution.py:325
  73.4 17.5 %collective-permute-start.1 = (bf16[256,256]{1,0:T(8,128)(2,1)S(1)}, bf16[256,256]{1,0:T(8,128)(2,1)S(1)}, u32[]{:S(2)}, u32[]{:S(2)}) collective-permute-start(bf16[256,256]{1,0:T(8,128)(2,1)S(1)} %copy-done.21), channel_id=1, source_target_pairs={{0,11},{1,10},{2,9},{3,8},{4,15},{5,14},{6,13},{7,12},{8,3},{9,2},... | collective-permute-start | bytes 393224 | tf_op jit(solution)/shard_map/ppermute | solution.py:325
  74.2 21.5 %collective-permute-start.2 = (bf16[256,256]{1,0:T(8,128)(2,1)S(1)}, bf16[256,256]{1,0:T(8,128)(2,1)S(1)}, u32[]{:S(2)}, u32[]{:S(2)}) collective-permute-start(bf16[256,256]{1,0:T(8,128)(2,1)S(1)} %copy-done.20), channel_id=1, source_target_pairs={{0,12},{1,13},{2,14},{3,15},{4,8},{5,9},{6,10},{7,11},{8,4},{9,5},... | collective-permute-start | bytes 393224 | tf_op jit(solution)/shard_map/ppermute | solution.py:325
  75.5 24.0 %collective-permute-start.3 = (bf16[256,256]{1,0:T(8,128)(2,1)S(1)}, bf16[256,256]{1,0:T(8,128)(2,1)S(1)}, u32[]{:S(2)}, u32[]{:S(2)}) collective-permute-start(bf16[256,256]{1,0:T(8,128)(2,1)S(1)} %copy-done.19), channel_id=1, source_target_pairs={{0,13},{1,12},{2,15},{3,14},{4,9},{5,8},{6,11},{7,10},{8,5},{9,4},... | collective-permute-start | bytes 393224 | tf_op jit(solution)/shard_map/ppermute | solution.py:325
  76.4 23.7 %collective-permute-start.4 = (bf16[256,256]{1,0:T(8,128)(2,1)S(1)}, bf16[256,256]{1,0:T(8,128)(2,1)S(1)}, u32[]{:S(2)}, u32[]{:S(2)}) collective-permute-start(bf16[256,256]{1,0:T(8,128)(2,1)S(1)} %copy-done.18), channel_id=1, source_target_pairs={{0,14},{1,15},{2,12},{3,13},{4,10},{5,11},{6,8},{7,9},{8,6},{9,7},... | collective-permute-start | bytes 393224 | tf_op jit(solution)/shard_map/ppermute | solution.py:325
  78.6 25.8 %collective-permute-start.5 = (bf16[256,256]{1,0:T(8,128)(2,1)S(1)}, bf16[256,256]{1,0:T(8,128)(2,1)S(1)}, u32[]{:S(2)}, u32[]{:S(2)}) collective-permute-start(bf16[256,256]{1,0:T(8,128)(2,1)S(1)} %copy-done.17), channel_id=1, source_target_pairs={{0,15},{1,14},{2,13},{3,12},{4,11},{5,10},{6,9},{7,8},{8,7},{9,6},... | collective-permute-start | bytes 393224 | tf_op jit(solution)/shard_map/ppermute | solution.py:325
  114.9 3.7 %collective-permute-start.15 = (bf16[128,256]{1,0:T(8,128)(2,1)}, bf16[128,256]{1,0:T(8,128)(2,1)S(1)}, u32[]{:S(2)}, u32[]{:S(2)}) collective-permute-start(bf16[128,256]{1,0:T(8,128)(2,1)} %get-tuple-element.62), channel_id=1, source_target_pairs={{0,1},{1,0},{2,3},{3,2},{4,5},{5,4},{6,7},{7,6},{8,9},{9,8},{10,11... | collective-permute-start | bytes 196616 | tf_op jit(solution)/shard_map/ppermute | solution.py:325
  115.0 4.6 %collective-permute-start.16 = (bf16[128,256]{1,0:T(8,128)(2,1)}, bf16[128,256]{1,0:T(8,128)(2,1)S(1)}, u32[]{:S(2)}, u32[]{:S(2)}) collective-permute-start(bf16[128,256]{1,0:T(8,128)(2,1)} %get-tuple-element.63), channel_id=1, source_target_pairs={{0,2},{1,3},{2,0},{3,1},{4,6},{5,7},{6,4},{7,5},{8,10},{9,11},{10,... | collective-permute-start | bytes 196616 | tf_op jit(solution)/shard_map/ppermute | solution.py:325
  116.2 5.3 %collective-permute-start.17 = (bf16[128,256]{1,0:T(8,128)(2,1)}, bf16[128,256]{1,0:T(8,128)(2,1)S(1)}, u32[]{:S(2)}, u32[]{:S(2)}) collective-permute-start(bf16[128,256]{1,0:T(8,128)(2,1)} %get-tuple-element.64), channel_id=1, source_target_pairs={{0,3},{1,2},{2,1},{3,0},{4,7},{5,6},{6,5},{7,4},{8,11},{9,10},{10,... | collective-permute-start | bytes 196616 | tf_op jit(solution)/shard_map/ppermute | solution.py:325
  117.1 5.8 %collective-permute-start.18 = (bf16[128,256]{1,0:T(8,128)(2,1)}, bf16[128,256]{1,0:T(8,128)(2,1)S(1)}, u32[]{:S(2)}, u32[]{:S(2)}) collective-permute-start(bf16[128,256]{1,0:T(8,128)(2,1)} %get-tuple-element.65), channel_id=1, source_target_pairs={{0,4},{1,5},{2,6},{3,7},{4,0},{5,1},{6,2},{7,3},{8,12},{9,13},{10,... | collective-permute-start | bytes 196616 | tf_op jit(solution)/shard_map/ppermute | solution.py:325
  117.1 7.0 %collective-permute-start.19 = (bf16[128,256]{1,0:T(8,128)(2,1)}, bf16[128,256]{1,0:T(8,128)(2,1)S(1)}, u32[]{:S(2)}, u32[]{:S(2)}) collective-permute-start(bf16[128,256]{1,0:T(8,128)(2,1)} %get-tuple-element.66), channel_id=1, source_target_pairs={{0,5},{1,4},{2,7},{3,6},{4,1},{5,0},{6,3},{7,2},{8,13},{9,12},{10,... | collective-permute-start | bytes 196616 | tf_op jit(solution)/shard_map/ppermute | solution.py:325
  118.6 28.9 %copy-start.1 = (bf16[128,256]{1,0:T(8,128)(2,1)}, bf16[128,256]{1,0:T(8,128)(2,1)S(1)}, u32[]{:S(2)}) copy-start(bf16[128,256]{1,0:T(8,128)(2,1)S(1)} %collective-permute-done.15.refs_1_) | copy-start | bytes 196612
  118.6 6.7 %collective-permute-start.20 = (bf16[128,256]{1,0:T(8,128)(2,1)}, bf16[128,256]{1,0:T(8,128)(2,1)S(1)}, u32[]{:S(2)}, u32[]{:S(2)}) collective-permute-start(bf16[128,256]{1,0:T(8,128)(2,1)} %get-tuple-element.67), channel_id=1, source_target_pairs={{0,6},{1,7},{2,4},{3,5},{4,2},{5,3},{6,0},{7,1},{8,14},{9,15},{10,... | collective-permute-start | bytes 196616 | tf_op jit(solution)/shard_map/ppermute | solution.py:325
  119.5 8.2 %collective-permute-start.21 = (bf16[128,256]{1,0:T(8,128)(2,1)}, bf16[128,256]{1,0:T(8,128)(2,1)S(1)}, u32[]{:S(2)}, u32[]{:S(2)}) collective-permute-start(bf16[128,256]{1,0:T(8,128)(2,1)} %get-tuple-element.68), channel_id=1, source_target_pairs={{0,7},{1,6},{2,5},{3,4},{4,3},{5,2},{6,1},{7,0},{8,15},{9,14},{10,... | collective-permute-start | bytes 196616 | tf_op jit(solution)/shard_map/ppermute | solution.py:325
  121.5 6.5 %collective-permute-start.22 = (bf16[128,256]{1,0:T(8,128)(2,1)}, bf16[128,256]{1,0:T(8,128)(2,1)S(1)}, u32[]{:S(2)}, u32[]{:S(2)}) collective-permute-start(bf16[128,256]{1,0:T(8,128)(2,1)} %get-tuple-element.69), channel_id=1, source_target_pairs={{0,8},{1,9},{2,10},{3,11},{4,12},{5,13},{6,14},{7,15},{8,0},{9,1},... | collective-permute-start | bytes 196616 | tf_op jit(solution)/shard_map/ppermute | solution.py:325
  122.9 10.2 %collective-permute-start.23 = (bf16[128,256]{1,0:T(8,128)(2,1)}, bf16[128,256]{1,0:T(8,128)(2,1)S(1)}, u32[]{:S(2)}, u32[]{:S(2)}) collective-permute-start(bf16[128,256]{1,0:T(8,128)(2,1)} %get-tuple-element.70), channel_id=1, source_target_pairs={{0,9},{1,8},{2,11},{3,10},{4,13},{5,12},{6,15},{7,14},{8,1},{9,0},... | collective-permute-start | bytes 196616 | tf_op jit(solution)/shard_map/ppermute | solution.py:325
  124.0 11.9 %collective-permute-start.24 = (bf16[128,256]{1,0:T(8,128)(2,1)}, bf16[128,256]{1,0:T(8,128)(2,1)S(1)}, u32[]{:S(2)}, u32[]{:S(2)}) collective-permute-start(bf16[128,256]{1,0:T(8,128)(2,1)} %get-tuple-element.71), channel_id=1, source_target_pairs={{0,10},{1,11},{2,8},{3,9},{4,14},{5,15},{6,12},{7,13},{8,2},{9,3},... | collective-permute-start | bytes 196616 | tf_op jit(solution)/shard_map/ppermute | solution.py:325
  125.2 12.3 %collective-permute-start.25 = (bf16[128,256]{1,0:T(8,128)(2,1)}, bf16[128,256]{1,0:T(8,128)(2,1)S(1)}, u32[]{:S(2)}, u32[]{:S(2)}) collective-permute-start(bf16[128,256]{1,0:T(8,128)(2,1)} %get-tuple-element.72), channel_id=1, source_target_pairs={{0,11},{1,10},{2,9},{3,8},{4,15},{5,14},{6,13},{7,12},{8,3},{9,2},... | collective-permute-start | bytes 196616 | tf_op jit(solution)/shard_map/ppermute | solution.py:325
  127.7 12.8 %collective-permute-start.26 = (bf16[128,256]{1,0:T(8,128)(2,1)}, bf16[128,256]{1,0:T(8,128)(2,1)S(1)}, u32[]{:S(2)}, u32[]{:S(2)}) collective-permute-start(bf16[128,256]{1,0:T(8,128)(2,1)} %get-tuple-element.73), channel_id=1, source_target_pairs={{0,12},{1,13},{2,14},{3,15},{4,8},{5,9},{6,10},{7,11},{8,4},{9,5},... | collective-permute-start | bytes 196616 | tf_op jit(solution)/shard_map/ppermute | solution.py:325
  128.0 13.2 %collective-permute-start.27 = (bf16[128,256]{1,0:T(8,128)(2,1)}, bf16[128,256]{1,0:T(8,128)(2,1)S(1)}, u32[]{:S(2)}, u32[]{:S(2)}) collective-permute-start(bf16[128,256]{1,0:T(8,128)(2,1)} %get-tuple-element.74), channel_id=1, source_target_pairs={{0,13},{1,12},{2,15},{3,14},{4,9},{5,8},{6,11},{7,10},{8,5},{9,4},... | collective-permute-start | bytes 196616 | tf_op jit(solution)/shard_map/ppermute | solution.py:325
  133.1 12.9 %collective-permute-start.28 = (bf16[128,256]{1,0:T(8,128)(2,1)}, bf16[128,256]{1,0:T(8,128)(2,1)S(1)}, u32[]{:S(2)}, u32[]{:S(2)}) collective-permute-start(bf16[128,256]{1,0:T(8,128)(2,1)} %get-tuple-element.75), channel_id=1, source_target_pairs={{0,14},{1,15},{2,12},{3,13},{4,10},{5,11},{6,8},{7,9},{8,6},{9,7},... | collective-permute-start | bytes 196616 | tf_op jit(solution)/shard_map/ppermute | solution.py:325
  135.9 11.5 %collective-permute-start.29 = (bf16[128,256]{1,0:T(8,128)(2,1)}, bf16[128,256]{1,0:T(8,128)(2,1)S(1)}, u32[]{:S(2)}, u32[]{:S(2)}) collective-permute-start(bf16[128,256]{1,0:T(8,128)(2,1)} %get-tuple-element.76), channel_id=1, source_target_pairs={{0,15},{1,14},{2,13},{3,12},{4,11},{5,10},{6,9},{7,8},{8,7},{9,6},... | collective-permute-start | bytes 196616 | tf_op jit(solution)/shard_map/ppermute | solution.py:325
  (35 other events, 461.6 us)

commit v4 on v3

--- a/solution.py
+++ b/solution.py
@@ -13,6 +13,8 @@
 TO_LOG2 = HD ** (-0.5) * math.log2(math.e)
 NT = (((1,), (1,)), ((), ()))
 
+LIMIT = 512
+GROUP = 4
 IN_HBM = pl.BlockSpec(memory_space=pltpu.HBM)
 WHOLE = pl.BlockSpec(memory_space=pltpu.VMEM)
 SCALARS = pl.BlockSpec(memory_space=pltpu.SMEM)
@@ -70,7 +72,8 @@
 
 
 def softmax_add(queries, tops, accs, take_keys, take_values, total, limit):
-    chunk = math.gcd(limit, total)
+    unit = math.gcd(256, total)
+    chunk = max(c for c in range(unit, max(limit, unit) + 1, unit) if total % c == 0)
     ones = jnp.ones((chunk, HD), jnp.bfloat16)
     every = range(len(queries))
     for at in range(0, total, chunk):
@@ -167,7 +170,7 @@
                 lambda i, at, chunk, cols=cols: keys[at : at + chunk, cols],
                 lambda i, at, chunk, cols=cols: values[at : at + chunk, cols],
                 total,
-                1024 if has_state else 512,
+                LIMIT,
             )
             acc_ref[here, cols] = acc[:, :HD]
             stat_ref[here, cols] = jnp.where(lane < HD // 2, top, acc[:, HD:])
@@ -212,7 +215,7 @@
     kv_refs = refs[:n_kv]
     q_hbm, acc_hbm, stat_hbm, gate_hbm = refs[n_kv : n_kv + 4]
     out_refs = refs[n_kv + 4 : n_kv + 4 + n]
-    q_ref, acc_ref, stat_ref, gate_ref, keys, values, sems = refs[n_kv + 4 + n :]
+    q_ref, acc_ref, stat_ref, gate_ref, keys, values, pieces, sems = refs[n_kv + 4 + n :]
     rows, width = out_refs[0].shape
     me = scal_ref[0]
     at = pl.multiple_of(me * width, HD)
@@ -244,14 +247,15 @@
 
     for copy in kv_copies:
         copy.wait()
-    gate = None
-    for first in range(0, n, 2):
-        for copy in copies[3 * first : 3 * first + 6]:
+    gate, out_copies = None, []
+    group = min(GROUP, n)
+    for first in range(0, n, group):
+        for copy in copies[3 * first : 3 * (first + group)]:
             copy.wait()
         if gate is None:
             gate_copy.wait()
             gate = gate_ref[pl.ds(scal_ref[2], 1), :]
-        here = slice(first * rows, (first + 2) * rows)
+        here = slice(first * rows, (first + group) * rows)
         for cols in head_cols:
             top, row_sum = split_stat(stat_ref[here, cols])
             _, (acc,) = softmax_add(
@@ -261,12 +265,18 @@
                 lambda i, at, chunk, cols=cols: keys[at : at + chunk, cols],
                 lambda i, at, chunk, cols=cols: values[at : at + chunk, cols],
                 n_kv * rows,
-                1024,
+                LIMIT,
             )
             attn = (acc[:, :HD] / acc[:, HD:]).astype(jnp.bfloat16)
             gated = (attn.astype(jnp.float32) * gate[:, cols]).astype(jnp.bfloat16)
-            out_refs[first][:, cols] = gated[:rows]
-            out_refs[first + 1][:, cols] = gated[rows:]
+            for place in range(group):
+                pieces[first + place, :, cols] = gated[place * rows : (place + 1) * rows]
+        for slot in range(first, first + group):
+            sem = sems.at[3 * n + 1 + len(kv_copies) + slot]
+            out_copies.append(pltpu.make_async_copy(pieces.at[slot], out_refs[slot], sem))
+            out_copies[-1].start()
+    for copy in out_copies:
+        copy.wait()
 
 
 def attend_last(scal, queries, state, kv, gate_table):
@@ -278,7 +288,7 @@
         functools.partial(last_body, len(kv), n),
         out_shape=[piece] * n,
         in_specs=[SCALARS] + [IN_HBM] * (len(kv) + 4),
-        out_specs=[WHOLE] * n,
+        out_specs=[IN_HBM] * n,
         scratch_shapes=[
             pltpu.VMEM((n * rows, width), jnp.bfloat16),
             kept,
@@ -286,7 +296,8 @@
             pltpu.VMEM((gate_table.shape[0], width), jnp.float32),
             full,
             full,
-            pltpu.SemaphoreType.DMA((3 * n + 1 + 2 * len(kv),)),
+            pltpu.VMEM((n, rows, width), jnp.bfloat16),
+            pltpu.SemaphoreType.DMA((4 * n + 1 + 2 * len(kv),)),
         ],
         cost_estimate=cost(n * rows, len(kv) * rows, width),
     )(scal, *kv, queries, *state, gate_table)
@@ -313,6 +324,11 @@
     )(scal, *parts)
 
 
+def split_far(n):
+    far, few = range(n // 2, n), max(1, n // 8)
+    return far[:few], far[few:]
+
+
 def shards(
     fresh_query, fresh_key, fresh_value, stale_key, stale_value, patch_start, timestep, gate_table
 ):
@@ -328,8 +344,16 @@
         return [b if s == 0 else send(s, b) for s, b in zip(slots, blocks)]
 
     scal = jnp.stack([me, patch_start[0], timestep[0]])
-    head, tail = far[: n // 8], far[n // 8 :]
-    head_blocks = pack(me[None], fresh_key, fresh_value, head, width)
+    head, tail = split_far(n)
+    head_blocks = [
+        jnp.concatenate(
+            [
+                lax.dynamic_slice_in_dim(x, (me ^ slot) * width, width, 1)
+                for x in (fresh_key, fresh_value)
+            ]
+        )
+        for slot in head
+    ]
     head_kv = send_all(head, head_blocks)
     spread_q = spread(fresh_query, n, width)
     queries = lax.all_to_all(spread_q, "seq", 0, 0, tiled=True)

time: 151 us -> 151 us (level)
  Pallas kernels: 47.5 us -> 44.7 us
    pallas_call x2 -> x1, Pallas kernels: 4.69 us -> 2.99 us  [pack(): pl.pallas_call(functools.partial(pack_body, tuple(slots)), out_shape=[blo...]
  transfers between devices with their start and end apart: 31 -> 31, of which waited for: 13 -> 13; matrix products, arithmetic and copies ran while one was open for 0% -> 1% of each run, Pallas kernels for 22% -> 21%
where the time goes in v4:
time: 151 us; the launch traced here: 150 us
  waiting for transfers between devices  50 us (33%)
  starting transfers between devices  49.4 us (33%)
  Pallas kernels  44.7 us (30%)
  local copies, waits for them, and re-layouts  3.46 us (2%)
  between operations  1.8 us (1%)
    ppermute x30, waiting for transfers between devices, send(): return lax.ppermute(block, 'seq', [(i, i ^ slot) for i in range(n)])  50 us
    ppermute x30, starting transfers between devices, send(): return lax.ppermute(block, 'seq', [(i, i ^ slot) for i in range(n)])  42.8 us
    pallas_call x2, Pallas kernels, attend_stage(): pl.pallas_call(functools.partial(stage_body, len(kv), bool(stale), bool(s...  27.8 us
    pallas_call x1, Pallas kernels, attend_last(): pl.pallas_call(functools.partial(last_body, len(kv), n), out_shape=[piece...  9.24 us
    all_to_all x1, starting transfers between devices, shards(): queries = lax.all_to_all(spread_q, 'seq', 0, 0, tiled=True)  6.59 us
  transfers between devices with their start and end apart: 31, of which 13 were waited for; matrix products, arithmetic and copies ran while one was open for 1% of the time, Pallas kernels for 21%

profile of v4, /device:TPU:11, one launch (start us, length us, event | category | flops | bytes accessed | tf_op | source)
XLA Modules:
  0.0 150.0 jit_solution(7769688967777353343)
XLA Ops:
  0.0 2.4 %shard_map.83 = bf16[16,128,256]{2,1,0:T(8,128)(2,1)} custom-call(bf16[128,4096]{1,0:T(8,128)(2,1)} %x_ref.1), custom_call_target="tpu_custom_call" | custom-call | tf_op jit(solution)/shard_map/pallas_call | solution.py:41
  2.4 6.6 %all-to-all-start = ((bf16[16,128,256]{2,1,0:T(8,128)(2,1)}), bf16[16,128,256]{2,1,0:T(8,128)(2,1)S(1)}, u32[]{:S(2)}, u32[]{:S(2)}) async-start(bf16[16,128,256]{2,1,0:T(8,128)(2,1)} %shard_map.83), calls=%async_computation | async-start | bytes 2097152 | tf_op jit(solution)/shard_map/all_to_all | solution.py:359
  9.9 2.2 %collective-permute-start.6 = (bf16[256,256]{1,0:T(8,128)(2,1)S(1)}, bf16[256,256]{1,0:T(8,128)(2,1)S(1)}, u32[]{:S(2)}, u32[]{:S(2)}) collective-permute-start(bf16[256,256]{1,0:T(8,128)(2,1)S(1)} %pad_maximum_fusion), channel_id=1, source_target_pairs={{0,8},{1,9},{2,10},{3,11},{4,12},{5,13},{6,14},{7,15},{8,0},{9,1},... | collective-permute-start | bytes 393224 | tf_op jit(solution)/shard_map/ppermute | solution.py:341
  13.0 3.0 %shard_map.82 = (bf16[256,256]{1,0:T(8,128)(2,1)}, bf16[256,256]{1,0:T(8,128)(2,1)}, bf16[256,256]{1,0:T(8,128)(2,1)}, bf16[256,256]{1,0:T(8,128)(2,1)}, bf16[25...) custom-call(s32[1]{0:T(128)} %bitcast.scal_ref, ...), custom_call_target="tpu_custom_call" | custom-call | tf_op jit(solution)/shard_map/pallas_call | solution.py:65
  16.0 3.1 %collective-permute-start = (bf16[256,256]{1,0:T(8,128)(2,1)}, bf16[256,256]{1,0:T(8,128)(2,1)S(1)}, u32[]{:S(2)}, u32[]{:S(2)}) collective-permute-start(bf16[256,256]{1,0:T(8,128)(2,1)} %get-tuple-element.39), channel_id=1, source_target_pairs={{0,10},{1,11},{2,8},{3,9},{4,14},{5,15},{6,12},{7,13},{8,2},{9,3},... | collective-permute-start | bytes 393224 | tf_op jit(solution)/shard_map/ppermute | solution.py:341
  21.4 21.5 %collective-permute-done.6.refs_0_ = bf16[256,256]{1,0:T(8,128)(2,1)S(1)} collective-permute-done((bf16[256,256]{1,0:T(8,128)(2,1)S(1)}, bf16[256,256]{1,0:T(8,128)(2,1)S(1)}, u32[]{:S(2)}, u32[]{:S(2)}) %collective-permute-start.6) | collective-permute-done | bytes 131104 | tf_op jit(solution)/shard_map/ppermute | solution.py:341
  42.8 2.6 %collective-permute-start.10 = (bf16[256,256]{1,0:T(8,128)(2,1)}, bf16[256,256]{1,0:T(8,128)(2,1)S(1)}, u32[]{:S(2)}, u32[]{:S(2)}) collective-permute-start(bf16[256,256]{1,0:T(8,128)(2,1)} %get-tuple-element.50), channel_id=1, source_target_pairs={{0,3},{1,2},{2,1},{3,0},{4,7},{5,6},{6,5},{7,4},{8,11},{9,10},{10,... | collective-permute-start | bytes 393224 | tf_op jit(solution)/shard_map/ppermute | solution.py:341
  45.7 4.0 %collective-permute-start.11 = (bf16[256,256]{1,0:T(8,128)(2,1)}, bf16[256,256]{1,0:T(8,128)(2,1)S(1)}, u32[]{:S(2)}, u32[]{:S(2)}) collective-permute-start(bf16[256,256]{1,0:T(8,128)(2,1)} %get-tuple-element.51), channel_id=1, source_target_pairs={{0,4},{1,5},{2,6},{3,7},{4,0},{5,1},{6,2},{7,3},{8,12},{9,13},{10,... | collective-permute-start | bytes 393224 | tf_op jit(solution)/shard_map/ppermute | solution.py:341
  49.6 3.8 %collective-permute-start.12 = (bf16[256,256]{1,0:T(8,128)(2,1)}, bf16[256,256]{1,0:T(8,128)(2,1)S(1)}, u32[]{:S(2)}, u32[]{:S(2)}) collective-permute-start(bf16[256,256]{1,0:T(8,128)(2,1)} %get-tuple-element.52), channel_id=1, source_target_pairs={{0,5},{1,4},{2,7},{3,6},{4,1},{5,0},{6,3},{7,2},{8,13},{9,12},{10,... | collective-permute-start | bytes 393224 | tf_op jit(solution)/shard_map/ppermute | solution.py:341
  53.5 2.0 %collective-permute-start.14 = (bf16[256,256]{1,0:T(8,128)(2,1)}, bf16[256,256]{1,0:T(8,128)(2,1)S(1)}, u32[]{:S(2)}, u32[]{:S(2)}) collective-permute-start(bf16[256,256]{1,0:T(8,128)(2,1)} %get-tuple-element.54), channel_id=1, source_target_pairs={{0,7},{1,6},{2,5},{3,4},{4,3},{5,2},{6,1},{7,0},{8,15},{9,14},{10,... | collective-permute-start | bytes 393224 | tf_op jit(solution)/shard_map/ppermute | solution.py:341
  56.5 16.9 %shard_map.84 = (f32[2048,256]{1,0:T(8,128)}, f32[2048,256]{1,0:T(8,128)}) custom-call(s32[3]{0:T(128)} %pad_add_fusion.scal_ref, bf16[16,128,256]{2,1,0:T(8,128)(2,1)} %copy-done, bf16[256,256]{1,0:T(8,128)(2,1)} %copy-done.25, bf16[256,256]{1,0:T(8,128)(2,1)} %copy-done.28, bf16[4096,256]{1,0:T(8,128)(2,1)} %refs_2_.1, bf16[4096,256]{1,0:T(8,128)(2,1)} %refs_3_.1), custom_call_target="tpu_custom_call" | custom-call | flops 7247757312 | bytes 8650752 | tf_op jit(solution)/shard_map/pallas_call | solution.py:198
  74.2 1.2 collective-permute-start.2
  76.4 2.2 %collective-permute-start.4 = (bf16[256,256]{1,0:T(8,128)(2,1)S(1)}, bf16[256,256]{1,0:T(8,128)(2,1)S(1)}, u32[]{:S(2)}, u32[]{:S(2)}) collective-permute-start(bf16[256,256]{1,0:T(8,128)(2,1)S(1)} %copy-done.18), channel_id=1, source_target_pairs={{0,14},{1,15},{2,12},{3,13},{4,10},{5,11},{6,8},{7,9},{8,6},{9,7},... | collective-permute-start | bytes 393224 | tf_op jit(solution)/shard_map/ppermute | solution.py:341
  79.2 10.9 %shard_map.85 = (f32[2048,256]{1,0:T(8,128)}, f32[2048,256]{1,0:T(8,128)}) custom-call(s32[3]{0:T(128)} %pad_add_fusion.scal_ref, bf16[16,128,256]{2,1,0:T(8,128)(2,1)} %copy-done, f32[2048,256]{1,0:T(8,128)} %get-tuple-element.45.refs_0_, f32[2048,256]{1,0:T(8,128)} %get-tuple-element.46.refs_1_, bf16[256,256]{1,0:T(8,128)(2,1)} %get-tuple-element.47.refs_2_, ...), custom_call_target="tpu_custom_call" | custom-call | flops 3221225472 | bytes 7340032 | tf_op jit(solution)/shard_map/pallas_call | solution.py:198
  90.9 4.7 %collective-permute-done.2.refs_2_ = bf16[256,256]{1,0:T(8,128)(2,1)S(1)} collective-permute-done((bf16[256,256]{1,0:T(8,128)(2,1)S(1)}, bf16[256,256]{1,0:T(8,128)(2,1)S(1)}, u32[]{:S(2)}, u32[]{:S(2)}) %collective-permute-start.2) | collective-permute-done | bytes 131104 | tf_op jit(solution)/shard_map/ppermute | solution.py:341
  95.7 3.7 %collective-permute-done.3.refs_3_ = bf16[256,256]{1,0:T(8,128)(2,1)S(1)} collective-permute-done((bf16[256,256]{1,0:T(8,128)(2,1)S(1)}, bf16[256,256]{1,0:T(8,128)(2,1)S(1)}, u32[]{:S(2)}, u32[]{:S(2)}) %collective-permute-start.3) | collective-permute-done | bytes 131104 | tf_op jit(solution)/shard_map/ppermute | solution.py:341
  100.1 4.3 %collective-permute-done.5.refs_5_ = bf16[256,256]{1,0:T(8,128)(2,1)S(1)} collective-permute-done((bf16[256,256]{1,0:T(8,128)(2,1)S(1)}, bf16[256,256]{1,0:T(8,128)(2,1)S(1)}, u32[]{:S(2)}, u32[]{:S(2)}) %collective-permute-start.5) | collective-permute-done | bytes 131104 | tf_op jit(solution)/shard_map/ppermute | solution.py:341
  105.1 9.2 %shard_map.86 = (bf16[128,256]{1,0:T(8,128)(2,1)}, bf16[128,256]{1,0:T(8,128)(2,1)}, bf16[128,256]{1,0:T(8,128)(2,1)}, bf16[128,256]{1,0:T(8,128)(2,1)}, bf16[12...) custom-call(s32[3]{0:T(128)} %pad_add_fusion.scal_ref, ...), custom_call_target="tpu_custom_call" | custom-call | flops 2415919104 | bytes 7077888 | tf_op jit(solution)/shard_map/pallas_call | solution.py:287
  114.4 1.2 collective-permute-start.16
  116.5 1.5 collective-permute-start.19
  119.0 2.0 %collective-permute-start.21 = (bf16[128,256]{1,0:T(8,128)(2,1)}, bf16[128,256]{1,0:T(8,128)(2,1)S(1)}, u32[]{:S(2)}, u32[]{:S(2)}) collective-permute-start(bf16[128,256]{1,0:T(8,128)(2,1)} %get-tuple-element.64), channel_id=1, source_target_pairs={{0,7},{1,6},{2,5},{3,4},{4,3},{5,2},{6,1},{7,0},{8,15},{9,14},{10,... | collective-permute-start | bytes 196616 | tf_op jit(solution)/shard_map/ppermute | solution.py:341
  120.9 1.4 collective-permute-start.22
  123.5 1.2 collective-permute-start.24
  124.7 2.5 %collective-permute-start.25 = (bf16[128,256]{1,0:T(8,128)(2,1)}, bf16[128,256]{1,0:T(8,128)(2,1)S(1)}, u32[]{:S(2)}, u32[]{:S(2)}) collective-permute-start(bf16[128,256]{1,0:T(8,128)(2,1)} %get-tuple-element.68), channel_id=1, source_target_pairs={{0,11},{1,10},{2,9},{3,8},{4,15},{5,14},{6,13},{7,12},{8,3},{9,2},... | collective-permute-start | bytes 196616 | tf_op jit(solution)/shard_map/ppermute | solution.py:341
  127.4 1.4 collective-permute-start.27
  128.8 3.7 %collective-permute-done.23.refs_9_ = bf16[128,256]{1,0:T(8,128)(2,1)S(1)} collective-permute-done((bf16[128,256]{1,0:T(8,128)(2,1)}, bf16[128,256]{1,0:T(8,128)(2,1)S(1)}, u32[]{:S(2)}, u32[]{:S(2)}) %collective-permute-start.23) | collective-permute-done | bytes 65568 | tf_op jit(solution)/shard_map/ppermute | solution.py:341
  132.5 2.5 %collective-permute-start.28 = (bf16[128,256]{1,0:T(8,128)(2,1)}, bf16[128,256]{1,0:T(8,128)(2,1)S(1)}, u32[]{:S(2)}, u32[]{:S(2)}) collective-permute-start(bf16[128,256]{1,0:T(8,128)(2,1)} %get-tuple-element.71), channel_id=1, source_target_pairs={{0,14},{1,15},{2,12},{3,13},{4,10},{5,11},{6,8},{7,9},{8,6},{9,7},... | collective-permute-start | bytes 196616 | tf_op jit(solution)/shard_map/ppermute | solution.py:341
  135.3 1.6 %collective-permute-start.29 = (bf16[128,256]{1,0:T(8,128)(2,1)}, bf16[128,256]{1,0:T(8,128)(2,1)S(1)}, u32[]{:S(2)}, u32[]{:S(2)}) collective-permute-start(bf16[128,256]{1,0:T(8,128)(2,1)} %get-tuple-element.72), channel_id=1, source_target_pairs={{0,15},{1,14},{2,13},{3,12},{4,11},{5,10},{6,9},{7,8},{8,7},{9,6},... | collective-permute-start | bytes 196616 | tf_op jit(solution)/shard_map/ppermute | solution.py:341
  136.9 3.0 %collective-permute-done.26.refs_12_ = bf16[128,256]{1,0:T(8,128)(2,1)S(1)} collective-permute-done((bf16[128,256]{1,0:T(8,128)(2,1)}, bf16[128,256]{1,0:T(8,128)(2,1)S(1)}, u32[]{:S(2)}, u32[]{:S(2)}) %collective-permute-start.26) | collective-permute-done | bytes 65568 | tf_op jit(solution)/shard_map/ppermute | solution.py:341
  140.6 4.9 %collective-permute-done.28.refs_14_ = bf16[128,256]{1,0:T(8,128)(2,1)S(1)} collective-permute-done((bf16[128,256]{1,0:T(8,128)(2,1)}, bf16[128,256]{1,0:T(8,128)(2,1)S(1)}, u32[]{:S(2)}, u32[]{:S(2)}) %collective-permute-start.28) | collective-permute-done | bytes 65568 | tf_op jit(solution)/shard_map/ppermute | solution.py:341
  145.5 1.4 collective-permute-done.29.refs_15_
  147.5 2.3 %shard_map.87 = bf16[128,4096]{1,0:T(8,128)(2,1)} custom-call(s32[1]{0:T(128)} %bitcast.scal_ref, bf16[128,256]{1,0:T(8,128)(2,1)} %get-tuple-element.57.refs_0_, bf16[128,256]{1,0:T(8,128)(2,1)} %copy-done.1, bf16[128,256]{1,0:T(8,128)(2,1)} %copy-done.2, bf16[128,256]{1,0:T(8,128)(2,1)} %copy-done.3, bf16[128,256]{1,0:T(8,128)(2,1)} %copy-done.4, ...), custom_call_target="tpu_custom_call" | custom-call | tf_op jit(solution)/shard_map/pallas_call | solution.py:318
  (112 shorter events, 13.6 us)
Async XLA Ops:
  2.4 53.1 %all-to-all-start = ((bf16[16,128,256]{2,1,0:T(8,128)(2,1)}), bf16[16,128,256]{2,1,0:T(8,128)(2,1)S(1)}, u32[]{:S(2)}, u32[]{:S(2)}) async-start(bf16[16,128,256]{2,1,0:T(8,128)(2,1)} %shard_map.83), calls=%async_computation | async-start | bytes 2097152 | tf_op jit(solution)/shard_map/all_to_all | solution.py:359
  9.9 32.9 %collective-permute-start.6 = (bf16[256,256]{1,0:T(8,128)(2,1)S(1)}, bf16[256,256]{1,0:T(8,128)(2,1)S(1)}, u32[]{:S(2)}, u32[]{:S(2)}) collective-permute-start(bf16[256,256]{1,0:T(8,128)(2,1)S(1)} %pad_maximum_fusion), channel_id=1, source_target_pairs={{0,8},{1,9},{2,10},{3,11},{4,12},{5,13},{6,14},{7,15},{8,0},{9,1},... | collective-permute-start | bytes 393224 | tf_op jit(solution)/shard_map/ppermute | solution.py:341
  12.1 33.6 %collective-permute-start.7 = (bf16[256,256]{1,0:T(8,128)(2,1)S(1)}, bf16[256,256]{1,0:T(8,128)(2,1)S(1)}, u32[]{:S(2)}, u32[]{:S(2)}) collective-permute-start(bf16[256,256]{1,0:T(8,128)(2,1)S(1)} %pad_maximum_fusion.1), channel_id=1, source_target_pairs={{0,9},{1,8},{2,11},{3,10},{4,13},{5,12},{6,15},{7,14},{8,1},{9,0},... | collective-permute-start | bytes 393224 | tf_op jit(solution)/shard_map/ppermute | solution.py:341
  16.0 33.6 %collective-permute-start = (bf16[256,256]{1,0:T(8,128)(2,1)}, bf16[256,256]{1,0:T(8,128)(2,1)S(1)}, u32[]{:S(2)}, u32[]{:S(2)}) collective-permute-start(bf16[256,256]{1,0:T(8,128)(2,1)} %get-tuple-element.39), channel_id=1, source_target_pairs={{0,10},{1,11},{2,8},{3,9},{4,14},{5,15},{6,12},{7,13},{8,2},{9,3},... | collective-permute-start | bytes 393224 | tf_op jit(solution)/shard_map/ppermute | solution.py:341
  19.1 34.4 %collective-permute-start.8 = (bf16[256,256]{1,0:T(8,128)(2,1)}, bf16[256,256]{1,0:T(8,128)(2,1)S(1)}, u32[]{:S(2)}, u32[]{:S(2)}) collective-permute-start(bf16[256,256]{1,0:T(8,128)(2,1)} %get-tuple-element.48), channel_id=1, source_target_pairs={{0,1},{1,0},{2,3},{3,2},{4,5},{5,4},{6,7},{7,6},{8,9},{9,8},{10,11... | collective-permute-start | bytes 393224 | tf_op jit(solution)/shard_map/ppermute | solution.py:341
  19.2 34.3 %collective-permute-start.9 = (bf16[256,256]{1,0:T(8,128)(2,1)}, bf16[256,256]{1,0:T(8,128)(2,1)S(1)}, u32[]{:S(2)}, u32[]{:S(2)}) collective-permute-start(bf16[256,256]{1,0:T(8,128)(2,1)} %get-tuple-element.49), channel_id=1, source_target_pairs={{0,2},{1,3},{2,0},{3,1},{4,6},{5,7},{6,4},{7,5},{8,10},{9,11},{10,... | collective-permute-start | bytes 393224 | tf_op jit(solution)/shard_map/ppermute | solution.py:341
  42.8 30.6 %collective-permute-start.10 = (bf16[256,256]{1,0:T(8,128)(2,1)}, bf16[256,256]{1,0:T(8,128)(2,1)S(1)}, u32[]{:S(2)}, u32[]{:S(2)}) collective-permute-start(bf16[256,256]{1,0:T(8,128)(2,1)} %get-tuple-element.50), channel_id=1, source_target_pairs={{0,3},{1,2},{2,1},{3,0},{4,7},{5,6},{6,5},{7,4},{8,11},{9,10},{10,... | collective-permute-start | bytes 393224 | tf_op jit(solution)/shard_map/ppermute | solution.py:341
  45.7 28.5 %collective-permute-start.11 = (bf16[256,256]{1,0:T(8,128)(2,1)}, bf16[256,256]{1,0:T(8,128)(2,1)S(1)}, u32[]{:S(2)}, u32[]{:S(2)}) collective-permute-start(bf16[256,256]{1,0:T(8,128)(2,1)} %get-tuple-element.51), channel_id=1, source_target_pairs={{0,4},{1,5},{2,6},{3,7},{4,0},{5,1},{6,2},{7,3},{8,12},{9,13},{10,... | collective-permute-start | bytes 393224 | tf_op jit(solution)/shard_map/ppermute | solution.py:341
  49.6 25.8 %collective-permute-start.12 = (bf16[256,256]{1,0:T(8,128)(2,1)}, bf16[256,256]{1,0:T(8,128)(2,1)S(1)}, u32[]{:S(2)}, u32[]{:S(2)}) collective-permute-start(bf16[256,256]{1,0:T(8,128)(2,1)} %get-tuple-element.52), channel_id=1, source_target_pairs={{0,5},{1,4},{2,7},{3,6},{4,1},{5,0},{6,3},{7,2},{8,13},{9,12},{10,... | collective-permute-start | bytes 393224 | tf_op jit(solution)/shard_map/ppermute | solution.py:341
  53.4 23.0 %collective-permute-start.13 = (bf16[256,256]{1,0:T(8,128)(2,1)}, bf16[256,256]{1,0:T(8,128)(2,1)S(1)}, u32[]{:S(2)}, u32[]{:S(2)}) collective-permute-start(bf16[256,256]{1,0:T(8,128)(2,1)} %get-tuple-element.53), channel_id=1, source_target_pairs={{0,6},{1,7},{2,4},{3,5},{4,2},{5,3},{6,0},{7,1},{8,14},{9,15},{10,... | collective-permute-start | bytes 393224 | tf_op jit(solution)/shard_map/ppermute | solution.py:341
  53.5 25.1 %collective-permute-start.14 = (bf16[256,256]{1,0:T(8,128)(2,1)}, bf16[256,256]{1,0:T(8,128)(2,1)S(1)}, u32[]{:S(2)}, u32[]{:S(2)}) collective-permute-start(bf16[256,256]{1,0:T(8,128)(2,1)} %get-tuple-element.54), channel_id=1, source_target_pairs={{0,7},{1,6},{2,5},{3,4},{4,3},{5,2},{6,1},{7,0},{8,15},{9,14},{10,... | collective-permute-start | bytes 393224 | tf_op jit(solution)/shard_map/ppermute | solution.py:341
  73.4 17.5 %collective-permute-start.1 = (bf16[256,256]{1,0:T(8,128)(2,1)S(1)}, bf16[256,256]{1,0:T(8,128)(2,1)S(1)}, u32[]{:S(2)}, u32[]{:S(2)}) collective-permute-start(bf16[256,256]{1,0:T(8,128)(2,1)S(1)} %copy-done.21), channel_id=1, source_target_pairs={{0,11},{1,10},{2,9},{3,8},{4,15},{5,14},{6,13},{7,12},{8,3},{9,2},... | collective-permute-start | bytes 393224 | tf_op jit(solution)/shard_map/ppermute | solution.py:341
  74.2 21.5 %collective-permute-start.2 = (bf16[256,256]{1,0:T(8,128)(2,1)S(1)}, bf16[256,256]{1,0:T(8,128)(2,1)S(1)}, u32[]{:S(2)}, u32[]{:S(2)}) collective-permute-start(bf16[256,256]{1,0:T(8,128)(2,1)S(1)} %copy-done.20), channel_id=1, source_target_pairs={{0,12},{1,13},{2,14},{3,15},{4,8},{5,9},{6,10},{7,11},{8,4},{9,5},... | collective-permute-start | bytes 393224 | tf_op jit(solution)/shard_map/ppermute | solution.py:341
  75.5 24.0 %collective-permute-start.3 = (bf16[256,256]{1,0:T(8,128)(2,1)S(1)}, bf16[256,256]{1,0:T(8,128)(2,1)S(1)}, u32[]{:S(2)}, u32[]{:S(2)}) collective-permute-start(bf16[256,256]{1,0:T(8,128)(2,1)S(1)} %copy-done.19), channel_id=1, source_target_pairs={{0,13},{1,12},{2,15},{3,14},{4,9},{5,8},{6,11},{7,10},{8,5},{9,4},... | collective-permute-start | bytes 393224 | tf_op jit(solution)/shard_map/ppermute | solution.py:341
  76.4 23.7 %collective-permute-start.4 = (bf16[256,256]{1,0:T(8,128)(2,1)S(1)}, bf16[256,256]{1,0:T(8,128)(2,1)S(1)}, u32[]{:S(2)}, u32[]{:S(2)}) collective-permute-start(bf16[256,256]{1,0:T(8,128)(2,1)S(1)} %copy-done.18), channel_id=1, source_target_pairs={{0,14},{1,15},{2,12},{3,13},{4,10},{5,11},{6,8},{7,9},{8,6},{9,7},... | collective-permute-start | bytes 393224 | tf_op jit(solution)/shard_map/ppermute | solution.py:341
  78.6 25.8 %collective-permute-start.5 = (bf16[256,256]{1,0:T(8,128)(2,1)S(1)}, bf16[256,256]{1,0:T(8,128)(2,1)S(1)}, u32[]{:S(2)}, u32[]{:S(2)}) collective-permute-start(bf16[256,256]{1,0:T(8,128)(2,1)S(1)} %copy-done.17), channel_id=1, source_target_pairs={{0,15},{1,14},{2,13},{3,12},{4,11},{5,10},{6,9},{7,8},{8,7},{9,6},... | collective-permute-start | bytes 393224 | tf_op jit(solution)/shard_map/ppermute | solution.py:341
  114.3 3.7 %collective-permute-start.15 = (bf16[128,256]{1,0:T(8,128)(2,1)}, bf16[128,256]{1,0:T(8,128)(2,1)S(1)}, u32[]{:S(2)}, u32[]{:S(2)}) collective-permute-start(bf16[128,256]{1,0:T(8,128)(2,1)} %get-tuple-element.58), channel_id=1, source_target_pairs={{0,1},{1,0},{2,3},{3,2},{4,5},{5,4},{6,7},{7,6},{8,9},{9,8},{10,11... | collective-permute-start | bytes 196616 | tf_op jit(solution)/shard_map/ppermute | solution.py:341
  114.4 4.6 %collective-permute-start.16 = (bf16[128,256]{1,0:T(8,128)(2,1)}, bf16[128,256]{1,0:T(8,128)(2,1)S(1)}, u32[]{:S(2)}, u32[]{:S(2)}) collective-permute-start(bf16[128,256]{1,0:T(8,128)(2,1)} %get-tuple-element.59), channel_id=1, source_target_pairs={{0,2},{1,3},{2,0},{3,1},{4,6},{5,7},{6,4},{7,5},{8,10},{9,11},{10,... | collective-permute-start | bytes 196616 | tf_op jit(solution)/shard_map/ppermute | solution.py:341
  115.6 5.3 %collective-permute-start.17 = (bf16[128,256]{1,0:T(8,128)(2,1)}, bf16[128,256]{1,0:T(8,128)(2,1)S(1)}, u32[]{:S(2)}, u32[]{:S(2)}) collective-permute-start(bf16[128,256]{1,0:T(8,128)(2,1)} %get-tuple-element.60), channel_id=1, source_target_pairs={{0,3},{1,2},{2,1},{3,0},{4,7},{5,6},{6,5},{7,4},{8,11},{9,10},{10,... | collective-permute-start | bytes 196616 | tf_op jit(solution)/shard_map/ppermute | solution.py:341
  116.5 5.8 %collective-permute-start.18 = (bf16[128,256]{1,0:T(8,128)(2,1)}, bf16[128,256]{1,0:T(8,128)(2,1)S(1)}, u32[]{:S(2)}, u32[]{:S(2)}) collective-permute-start(bf16[128,256]{1,0:T(8,128)(2,1)} %get-tuple-element.61), channel_id=1, source_target_pairs={{0,4},{1,5},{2,6},{3,7},{4,0},{5,1},{6,2},{7,3},{8,12},{9,13},{10,... | collective-permute-start | bytes 196616 | tf_op jit(solution)/shard_map/ppermute | solution.py:341
  116.5 7.0 %collective-permute-start.19 = (bf16[128,256]{1,0:T(8,128)(2,1)}, bf16[128,256]{1,0:T(8,128)(2,1)S(1)}, u32[]{:S(2)}, u32[]{:S(2)}) collective-permute-start(bf16[128,256]{1,0:T(8,128)(2,1)} %get-tuple-element.62), channel_id=1, source_target_pairs={{0,5},{1,4},{2,7},{3,6},{4,1},{5,0},{6,3},{7,2},{8,13},{9,12},{10,... | collective-permute-start | bytes 196616 | tf_op jit(solution)/shard_map/ppermute | solution.py:341
  118.0 28.9 %copy-start.1 = (bf16[128,256]{1,0:T(8,128)(2,1)}, bf16[128,256]{1,0:T(8,128)(2,1)S(1)}, u32[]{:S(2)}) copy-start(bf16[128,256]{1,0:T(8,128)(2,1)S(1)} %collective-permute-done.15.refs_1_) | copy-start | bytes 196612
  118.0 6.7 %collective-permute-start.20 = (bf16[128,256]{1,0:T(8,128)(2,1)}, bf16[128,256]{1,0:T(8,128)(2,1)S(1)}, u32[]{:S(2)}, u32[]{:S(2)}) collective-permute-start(bf16[128,256]{1,0:T(8,128)(2,1)} %get-tuple-element.63), channel_id=1, source_target_pairs={{0,6},{1,7},{2,4},{3,5},{4,2},{5,3},{6,0},{7,1},{8,14},{9,15},{10,... | collective-permute-start | bytes 196616 | tf_op jit(solution)/shard_map/ppermute | solution.py:341
  119.0 8.2 %collective-permute-start.21 = (bf16[128,256]{1,0:T(8,128)(2,1)}, bf16[128,256]{1,0:T(8,128)(2,1)S(1)}, u32[]{:S(2)}, u32[]{:S(2)}) collective-permute-start(bf16[128,256]{1,0:T(8,128)(2,1)} %get-tuple-element.64), channel_id=1, source_target_pairs={{0,7},{1,6},{2,5},{3,4},{4,3},{5,2},{6,1},{7,0},{8,15},{9,14},{10,... | collective-permute-start | bytes 196616 | tf_op jit(solution)/shard_map/ppermute | solution.py:341
  120.9 6.5 %collective-permute-start.22 = (bf16[128,256]{1,0:T(8,128)(2,1)}, bf16[128,256]{1,0:T(8,128)(2,1)S(1)}, u32[]{:S(2)}, u32[]{:S(2)}) collective-permute-start(bf16[128,256]{1,0:T(8,128)(2,1)} %get-tuple-element.65), channel_id=1, source_target_pairs={{0,8},{1,9},{2,10},{3,11},{4,12},{5,13},{6,14},{7,15},{8,0},{9,1},... | collective-permute-start | bytes 196616 | tf_op jit(solution)/shard_map/ppermute | solution.py:341
  122.3 10.2 %collective-permute-start.23 = (bf16[128,256]{1,0:T(8,128)(2,1)}, bf16[128,256]{1,0:T(8,128)(2,1)S(1)}, u32[]{:S(2)}, u32[]{:S(2)}) collective-permute-start(bf16[128,256]{1,0:T(8,128)(2,1)} %get-tuple-element.66), channel_id=1, source_target_pairs={{0,9},{1,8},{2,11},{3,10},{4,13},{5,12},{6,15},{7,14},{8,1},{9,0},... | collective-permute-start | bytes 196616 | tf_op jit(solution)/shard_map/ppermute | solution.py:341
  123.5 11.9 %collective-permute-start.24 = (bf16[128,256]{1,0:T(8,128)(2,1)}, bf16[128,256]{1,0:T(8,128)(2,1)S(1)}, u32[]{:S(2)}, u32[]{:S(2)}) collective-permute-start(bf16[128,256]{1,0:T(8,128)(2,1)} %get-tuple-element.67), channel_id=1, source_target_pairs={{0,10},{1,11},{2,8},{3,9},{4,14},{5,15},{6,12},{7,13},{8,2},{9,3},... | collective-permute-start | bytes 196616 | tf_op jit(solution)/shard_map/ppermute | solution.py:341
  124.7 12.3 %collective-permute-start.25 = (bf16[128,256]{1,0:T(8,128)(2,1)}, bf16[128,256]{1,0:T(8,128)(2,1)S(1)}, u32[]{:S(2)}, u32[]{:S(2)}) collective-permute-start(bf16[128,256]{1,0:T(8,128)(2,1)} %get-tuple-element.68), channel_id=1, source_target_pairs={{0,11},{1,10},{2,9},{3,8},{4,15},{5,14},{6,13},{7,12},{8,3},{9,2},... | collective-permute-start | bytes 196616 | tf_op jit(solution)/shard_map/ppermute | solution.py:341
  127.1 12.8 %collective-permute-start.26 = (bf16[128,256]{1,0:T(8,128)(2,1)}, bf16[128,256]{1,0:T(8,128)(2,1)S(1)}, u32[]{:S(2)}, u32[]{:S(2)}) collective-permute-start(bf16[128,256]{1,0:T(8,128)(2,1)} %get-tuple-element.69), channel_id=1, source_target_pairs={{0,12},{1,13},{2,14},{3,15},{4,8},{5,9},{6,10},{7,11},{8,4},{9,5},... | collective-permute-start | bytes 196616 | tf_op jit(solution)/shard_map/ppermute | solution.py:341
  127.4 13.2 %collective-permute-start.27 = (bf16[128,256]{1,0:T(8,128)(2,1)}, bf16[128,256]{1,0:T(8,128)(2,1)S(1)}, u32[]{:S(2)}, u32[]{:S(2)}) collective-permute-start(bf16[128,256]{1,0:T(8,128)(2,1)} %get-tuple-element.70), channel_id=1, source_target_pairs={{0,13},{1,12},{2,15},{3,14},{4,9},{5,8},{6,11},{7,10},{8,5},{9,4},... | collective-permute-start | bytes 196616 | tf_op jit(solution)/shard_map/ppermute | solution.py:341
  132.5 12.9 %collective-permute-start.28 = (bf16[128,256]{1,0:T(8,128)(2,1)}, bf16[128,256]{1,0:T(8,128)(2,1)S(1)}, u32[]{:S(2)}, u32[]{:S(2)}) collective-permute-start(bf16[128,256]{1,0:T(8,128)(2,1)} %get-tuple-element.71), channel_id=1, source_target_pairs={{0,14},{1,15},{2,12},{3,13},{4,10},{5,11},{6,8},{7,9},{8,6},{9,7},... | collective-permute-start | bytes 196616 | tf_op jit(solution)/shard_map/ppermute | solution.py:341
  135.3 11.5 %collective-permute-start.29 = (bf16[128,256]{1,0:T(8,128)(2,1)}, bf16[128,256]{1,0:T(8,128)(2,1)S(1)}, u32[]{:S(2)}, u32[]{:S(2)}) collective-permute-start(bf16[128,256]{1,0:T(8,128)(2,1)} %get-tuple-element.72), channel_id=1, source_target_pairs={{0,15},{1,14},{2,13},{3,12},{4,11},{5,10},{6,9},{7,8},{8,7},{9,6},... | collective-permute-start | bytes 196616 | tf_op jit(solution)/shard_map/ppermute | solution.py:341
  (35 other events, 461.9 us)
